TPU v7x, 32 devices: a whole 2x2x4 slice. The times are simulated.
32 devices in a mesh: dp: 8 (over z, x), mp: 4 (over y, core).
Axes of the slice: x: 2, y: 2, z: 4, core: 2. Of those that a mesh axis runs over, the one named last changes fastest.
Arguments:
- rows: float32 [16384, 1280], P(('dp', 'mp')), may hold values from -6 to 6
- lengths: int32 [256], P('dp'), may hold values from 1 to 64, as said below
- freq_class: int32 [256], P(('dp', 'mp')), may hold values from 0 to 2
- freq_table: float32 [3, 1280], replicated, may hold values from -3 to 3
- gain_attn: float32 [1280], replicated, may hold values from 0.5 to 1.5
- gain_mlp: float32 [1280], replicated, may hold values from 0.5 to 1.5
- w_qkv: float32 [3, 1280, 1280], P(None, None, 'mp'), may hold values from -0.15625 to 0.15625
- w_out: float32 [1280, 1280], P('mp'), may hold values from -0.5 to 0.5
- w_gate_up: float32 [2, 1280, 5120], P(None, None, 'mp'), may hold values from -0.15625 to 0.15625
- w_down: float32 [5120, 1280], P('mp'), may hold values from -0.15625 to 0.15625
- cotangent: float32 [16384, 1280], P(('dp', 'mp')), may hold values from -6 to 6
Outputs:
- output: float32 [16384, 1280], P(('dp', 'mp'))
- grad_rows: float32 [16384, 1280], P(('dp', 'mp'))
- grad_qkv: float32 [3, 1280, 1280], P(None, None, 'mp')
- grad_out: float32 [1280, 1280], P('mp')
- grad_gate_up: float32 [2, 1280, 5120], P(None, None, 'mp')
- grad_down: float32 [5120, 1280], P('mp')
- grad_gain_attn: float32 [1280], replicated
- grad_gain_mlp: float32 [1280], replicated
- grad_table: float32 [3, 1280], replicated
Inputs may be any that keep to these rules, and one draw needn't show every extreme that they name: `lengths`: the valid patches of a series are the last of its 64 slots; some series has all 64, and some only one.
All inputs are finite; a program needn't handle non-finite values.
Results may differ from a plain program's by a relative error of at most 0.02.
Values may be sent and summed in bfloat16 or wider, within the bound.
A program may use at most 256 MiB of HBM per device.

v0:
```python
import jax
import jax.numpy as jnp
from jax import lax
from jax.sharding import PartitionSpec as P

HS = 80
NFREQ = 3
SEQ = 64


EPSILON = 1e-06
NEGATIVE = -1e30
HIGHEST = lax.Precision.HIGHEST


def rotate(values, cosines, sines):
    half_width = values.shape[-1] // 2
    first_half = values[..., :half_width]
    second_half = values[..., half_width:]
    return jnp.concatenate(
        [first_half * cosines - second_half * sines, second_half * cosines + first_half * sines], -1
    )


def series_tables(series_lengths):
    places = jnp.arange(SEQ, dtype=jnp.int32)
    starts = SEQ - series_lengths
    valid_mask = places[None, :] >= starts[:, None]
    positions = (places[None, :] - starts[:, None]).astype(jnp.float32)
    frequency = 10000.0 ** (-2.0 * jnp.arange(HS // 2, dtype=jnp.float32) / HS)
    angles = positions[:, :, None] * frequency[None, None, :]
    return (valid_mask, jnp.cos(angles)[:, :, None, :], jnp.sin(angles)[:, :, None, :])


def allowed_pairs(valid_mask):
    places = jnp.arange(SEQ, dtype=jnp.int32)
    causal = places[:, None] >= places[None, :]
    itself = places[:, None] == places[None, :]
    return causal[None, None] & (valid_mask[:, None, None, :] | itself[None, None])


def norm_forward(values, gain):
    inverse = lax.rsqrt(jnp.mean(values * values, -1, keepdims=True) + EPSILON)
    return ((values * inverse * gain).astype(jnp.bfloat16), inverse)


def norm_backward(values, inverse, gain, grad_normed):
    normal = values * inverse
    grad_gain = jnp.sum(grad_normed * normal, 0)
    scaled = grad_normed * gain
    grad_values = inverse * (scaled - normal * jnp.mean(scaled * normal, -1, keepdims=True))
    return (grad_values, grad_gain)


def attention_scores(queries, keys, allowed):
    raw_scores = jnp.einsum("sihe,sjhe->shij", queries, keys, preferred_element_type=jnp.float32)
    return jnp.where(allowed, raw_scores * HS ** (-0.5), NEGATIVE)


def body(
    rows,
    lengths,
    freq_class,
    freq_table,
    gain_attn,
    gain_mlp,
    w_qkv,
    w_out,
    w_gate_up,
    w_down,
    cotangent,
):
    local_rows = rows.shape[0]
    mp_index = lax.axis_index("mp")
    series_count = lengths.shape[0]
    group_rows = series_count * SEQ
    heads_width = w_out.shape[0]
    head_count = heads_width // HS
    valid_mask, cosines, sines = series_tables(lengths)
    allowed = allowed_pairs(valid_mask)
    flat_valid = valid_mask.reshape(group_rows).astype(jnp.float32)
    mine_valid = lax.dynamic_slice_in_dim(flat_valid, mp_index * local_rows, local_rows)[:, None]
    classes = jnp.repeat(freq_class, SEQ)
    onehot = (classes[:, None] == jnp.arange(NFREQ, dtype=jnp.int32)[None, :]).astype(jnp.float32)
    start_rows = rows + jnp.dot(onehot, freq_table, precision=HIGHEST)
    normed_mine, inverse_attn = norm_forward(start_rows, gain_attn)
    normed = lax.all_gather(normed_mine, "mp", axis=0, tiled=True)
    qkv_low = w_qkv.astype(jnp.bfloat16)
    projected = jnp.einsum("td,cdf->ctf", normed, qkv_low, preferred_element_type=jnp.float32)
    projected = projected.reshape(3, series_count, SEQ, head_count, HS)
    queries = rotate(projected[0], cosines, sines).astype(jnp.bfloat16)
    keys = rotate(projected[1], cosines, sines).astype(jnp.bfloat16)
    values = projected[2].astype(jnp.bfloat16)
    scores = attention_scores(queries, keys, allowed)
    row_max = jnp.max(scores, -1, keepdims=True)
    exponent = jnp.exp(scores - row_max)
    row_total = jnp.sum(exponent, -1, keepdims=True)
    log_total = row_max + jnp.log(row_total)
    attention = (exponent / row_total).astype(jnp.bfloat16)
    mixed = jnp.einsum("shij,sjhe->sihe", attention, values, preferred_element_type=jnp.float32)
    mixed = mixed.reshape(group_rows, heads_width).astype(jnp.bfloat16)
    out_low = w_out.astype(jnp.bfloat16)
    attn_part = jnp.dot(mixed, out_low, preferred_element_type=jnp.float32)
    after_attn = start_rows + lax.psum_scatter(
        attn_part.astype(jnp.bfloat16), "mp", scatter_dimension=0, tiled=True
    ).astype(jnp.float32)
    normed_mlp_mine, inverse_mlp = norm_forward(after_attn, gain_mlp)
    normed_mlp = lax.all_gather(normed_mlp_mine, "mp", axis=0, tiled=True)
    gate_up_low = w_gate_up.astype(jnp.bfloat16)
    gate_up = jnp.einsum("td,cdf->ctf", normed_mlp, gate_up_low, preferred_element_type=jnp.float32)
    gate_pre = gate_up[0]
    up_pre = gate_up[1]
    sigmoid_gate = jax.nn.sigmoid(gate_pre)
    activated = gate_pre * sigmoid_gate
    hidden = (activated * up_pre).astype(jnp.bfloat16)
    down_low = w_down.astype(jnp.bfloat16)
    mlp_part = jnp.dot(hidden, down_low, preferred_element_type=jnp.float32)
    output = after_attn + lax.psum_scatter(
        mlp_part.astype(jnp.bfloat16), "mp", scatter_dimension=0, tiled=True
    ).astype(jnp.float32)
    grad_output = cotangent * mine_valid
    grad_down_in = lax.all_gather(grad_output.astype(jnp.bfloat16), "mp", axis=0, tiled=True)
    grad_down = jnp.einsum("tf,td->fd", hidden, grad_down_in, preferred_element_type=jnp.float32)
    grad_hidden = jnp.einsum(
        "td,fd->tf", grad_down_in, down_low, preferred_element_type=jnp.float32
    )
    grad_gate = grad_hidden * up_pre * (sigmoid_gate * (1.0 + gate_pre * (1.0 - sigmoid_gate)))
    grad_up = grad_hidden * activated
    grad_pre = jnp.stack([grad_gate, grad_up]).astype(jnp.bfloat16)
    grad_gate_up = jnp.einsum(
        "td,ctf->cdf", normed_mlp, grad_pre, preferred_element_type=jnp.float32
    )
    mlp_back_part = jnp.einsum(
        "ctf,cdf->td", grad_pre, gate_up_low, preferred_element_type=jnp.float32
    )
    grad_normed_mlp = lax.psum_scatter(
        mlp_back_part.astype(jnp.bfloat16), "mp", scatter_dimension=0, tiled=True
    ).astype(jnp.float32)
    grad_rows_mlp, grad_gain_mlp = norm_backward(after_attn, inverse_mlp, gain_mlp, grad_normed_mlp)
    grad_after = grad_output + grad_rows_mlp
    grad_attn_in = lax.all_gather(grad_after.astype(jnp.bfloat16), "mp", axis=0, tiled=True)
    grad_out = jnp.einsum("tf,td->fd", mixed, grad_attn_in, preferred_element_type=jnp.float32)
    grad_mixed = jnp.einsum("td,fd->tf", grad_attn_in, out_low, preferred_element_type=jnp.float32)
    grad_mixed = grad_mixed.astype(jnp.bfloat16).reshape(series_count, SEQ, head_count, HS)
    attention_again = jnp.exp(attention_scores(queries, keys, allowed) - log_total)
    grad_attention = jnp.einsum(
        "sihe,sjhe->shij", grad_mixed, values, preferred_element_type=jnp.float32
    )
    grad_values = jnp.einsum(
        "shij,sihe->sjhe",
        attention_again.astype(jnp.bfloat16),
        grad_mixed,
        preferred_element_type=jnp.float32,
    )
    row_dot = jnp.sum(attention_again * grad_attention, -1, keepdims=True)
    grad_scores = (attention_again * (grad_attention - row_dot)).astype(jnp.bfloat16)
    grad_queries = jnp.einsum(
        "shij,sjhe->sihe", grad_scores, keys, preferred_element_type=jnp.float32
    ) * HS ** (-0.5)
    grad_keys = jnp.einsum(
        "shij,sihe->sjhe", grad_scores, queries, preferred_element_type=jnp.float32
    ) * HS ** (-0.5)
    grad_projected = jnp.stack(
        [rotate(grad_queries, cosines, -sines), rotate(grad_keys, cosines, -sines), grad_values]
    )
    grad_projected = grad_projected.reshape(3, group_rows, heads_width).astype(jnp.bfloat16)
    grad_qkv = jnp.einsum("td,ctf->cdf", normed, grad_projected, preferred_element_type=jnp.float32)
    attn_back_part = jnp.einsum(
        "ctf,cdf->td", grad_projected, qkv_low, preferred_element_type=jnp.float32
    )
    grad_normed = lax.psum_scatter(
        attn_back_part.astype(jnp.bfloat16), "mp", scatter_dimension=0, tiled=True
    ).astype(jnp.float32)
    grad_rows_attn, grad_gain_attn = norm_backward(start_rows, inverse_attn, gain_attn, grad_normed)
    grad_rows = grad_after + grad_rows_attn
    grad_table = jnp.dot(onehot.T, grad_rows, precision=HIGHEST)
    grad_gain_attn, grad_gain_mlp, grad_table, token_total = lax.psum(
        (grad_gain_attn, grad_gain_mlp, grad_table, jnp.sum(mine_valid)), ("dp", "mp")
    )
    grad_qkv, grad_out, grad_gate_up, grad_down = (
        lax.psum(grad_qkv.astype(jnp.bfloat16), "dp").astype(jnp.float32),
        lax.psum(grad_out.astype(jnp.bfloat16), "dp").astype(jnp.float32),
        lax.psum(grad_gate_up.astype(jnp.bfloat16), "dp").astype(jnp.float32),
        lax.psum(grad_down.astype(jnp.bfloat16), "dp").astype(jnp.float32),
    )
    root_scale = lax.rsqrt(token_total)
    return (
        output,
        grad_rows,
        grad_qkv * root_scale,
        grad_out * root_scale,
        grad_gate_up * root_scale,
        grad_down * root_scale,
        grad_gain_attn * root_scale,
        grad_gain_mlp * root_scale,
        grad_table * root_scale,
    )


def solution(mesh):
    return jax.shard_map(
        body,
        mesh=mesh,
        in_specs=(
            P(("dp", "mp"), None),
            P("dp"),
            P(("dp", "mp")),
            P(),
            P(),
            P(),
            P(None, None, "mp"),
            P("mp", None),
            P(None, None, "mp"),
            P("mp", None),
            P(("dp", "mp"), None),
        ),
        out_specs=(
            P(("dp", "mp"), None),
            P(("dp", "mp"), None),
            P(None, None, "mp"),
            P("mp", None),
            P(None, None, "mp"),
            P("mp", None),
            P(),
            P(),
            P(),
        ),
        check_vma=False,
    )
```

profile of v0, /device:TPU:0, one launch (start us, length us, event | category | flops | bytes accessed | tf_op | source)
XLA Modules:
  0.0 1067.7 jit_solution(17084121526547978977)
XLA Ops:
  13.6 5.8 fusion.48
  19.4 36.9 %all-gather.5.cloned.1.call-done = bf16[2048,1280]{1,0:T(8,128)(2,1)} async-done(((bf16[512,1280]{1,0:T(8,128)(2,1)}), bf16[2048,1280]{1,0:T(8,128)(2,1)}) %all-gather.5.cloned.1.call-update) | async-done | bytes 5242896 | tf_op jit(solution)/shard_map/all_gather | solution.py:87
  56.3 8.7 fusion.10
  78.8 5.3 reshape.177
  84.1 5.5 fusion.62
  99.3 5.3 reshape.178
  104.7 5.5 fusion.63
  119.9 7.9 subtract_convert_fusion.3
  143.3 7.1 convolution_convert_fusion.2
  150.6 51.5 %reduce-scatter.5.cloned.1.call-done = bf16[512,1280]{1,0:T(8,128)(2,1)} async-done(((bf16[2048,1280]{1,0:T(8,128)(2,1)}), bf16[512,1280]{1,0:T(8,128)(2,1)}) %reduce-scatter.5.cloned.1.call-update) | async-done | bytes 1310736 | tf_op jit(solution)/shard_map/reduce_scatter | solution.py:104
  208.8 38.5 %all-gather.7.cloned.1.call-done = bf16[2048,1280]{1,0:T(8,128)(2,1)} async-done(((bf16[512,1280]{1,0:T(8,128)(2,1)}), bf16[2048,1280]{1,0:T(8,128)(2,1)}) %all-gather.7.cloned.1.call-update) | async-done | bytes 5242896 | tf_op jit(solution)/shard_map/all_gather | solution.py:108
  247.3 22.5 %convolution_bitcast_fusion = f32[2,2048,1280]{2,1,0:T(8,128)} fusion(bf16[2048,1280]{1,0:T(8,128)(2,1)} %all-gather.7.cloned.1.call-done, f32[2,1280,1280]{2,1,0:T(8,128)} %param.19), kind=kOutput, calls=%fused_computation.1 | convolution fusion | flops 13425049600 | bytes 39321600 | tf_op jit(solution)/shard_map/td,cdf->ctf/dot_general | solution.py:110
  269.8 20.0 %all-gather.9.cloned.1.call-done = bf16[2048,1280]{1,0:T(8,128)(2,1)} async-done(((bf16[512,1280]{1,0:T(8,128)(2,1)}), bf16[2048,1280]{1,0:T(8,128)(2,1)}) %all-gather.9.cloned.1.call-update) | async-done | bytes 5242896 | tf_op jit(solution)/shard_map/all_gather | solution.py:122
  289.8 21.7 %fusion.9 = (bf16[1,2048,1280]{2,1,0:T(8,128)(2,1)}, bf16[1,2048,1280]{2,1,0:T(8,128)(2,1)}, bf16[2048,1280]{1,0:T(8,128)(2,1)}) fusion(f32[2,2048,1280]{2,1,0:T(8,128)} %convolution_bitcast_fusion, bf16[2048,1280]{1,0:T(8,128)(2,1)} %all-gather.9.cloned.1.call-done, f32[1280,1280]{1,0:T(8,128)} %param.20), kind=kOutput, calls=%fused_computation.25 | convolution fusion | flops 6751846400 | bytes 48496640 | tf_op jit(solution)/shard_map/td,fd->tf/dot_general | solution.py:124
  311.5 21.5 %bitcast_convert_fusion.1 = bf16[2048,1280]{1,0:T(8,128)(2,1)} fusion(bf16[1,2048,1280]{2,1,0:T(8,128)(2,1)} %get-tuple-element.46, bf16[1,2048,1280]{2,1,0:T(8,128)(2,1)} %get-tuple-element.45, f32[2,1280,1280]{2,1,0:T(8,128)} %param.19), kind=kOutput, calls=%fused_computation.7 | convolution fusion | flops 13432913920 | bytes 28835840 | tf_op jit(solution)/shard_map/ctf,cdf->td/dot_general | solution.py:133
  333.1 12.4 %convolution_convert_fusion.1 = bf16[2048,1280]{1,0:T(8,128)(2,1)} fusion(bf16[2048,1280]{1,0:T(8,128)(2,1)} %get-tuple-element.47, f32[1280,1280]{1,0:T(8,128)} %param.20), kind=kOutput, calls=%fused_computation.14 | convolution fusion | flops 6715146240 | bytes 17039360 | tf_op jit(solution)/shard_map/dot_general | solution.py:117
  345.5 39.1 %reduce-scatter.9.cloned.1.call-done = bf16[512,1280]{1,0:T(8,128)(2,1)} async-done(((bf16[2048,1280]{1,0:T(8,128)(2,1)}), bf16[512,1280]{1,0:T(8,128)(2,1)}) %reduce-scatter.9.cloned.1.call-update) | async-done | bytes 1310736 | tf_op jit(solution)/shard_map/reduce_scatter | solution.py:136
  386.7 51.7 %reduce-scatter.7.cloned.1.call-done = bf16[512,1280]{1,0:T(8,128)(2,1)} async-done(((bf16[2048,1280]{1,0:T(8,128)(2,1)}), bf16[512,1280]{1,0:T(8,128)(2,1)}) %reduce-scatter.7.cloned.1.call-update) | async-done | bytes 1310736 | tf_op jit(solution)/shard_map/reduce_scatter | solution.py:118
  438.4 6.3 fusion.59
  444.8 40.5 %all-gather.11.cloned.1.call-done = bf16[2048,1280]{1,0:T(8,128)(2,1)} async-done(((bf16[512,1280]{1,0:T(8,128)(2,1)}), bf16[2048,1280]{1,0:T(8,128)(2,1)}) %all-gather.11.cloned.1.call-update) | async-done | bytes 5242896 | tf_op jit(solution)/shard_map/all_gather | solution.py:141
  517.4 5.0 copy.59
  525.4 5.0 copy.60
  537.9 5.0 copy.58
  550.7 9.9 bitcast_convert_fusion
  560.7 12.1 %convolution_convert_fusion.3 = bf16[1280,1280]{1,0:T(8,128)(2,1)} fusion(bf16[2048,1280]{1,0:T(8,128)(2,1)} %get-tuple-element.47, bf16[2048,1280]{1,0:T(8,128)(2,1)} %all-gather.9.cloned.1.call-done), kind=kOutput, calls=%fused_computation.16 | convolution fusion | flops 6712524800 | bytes 13762560 | tf_op jit(solution)/shard_map/tf,td->fd/dot_general | solution.py:123
  572.8 20.4 %fusion.1 = bf16[2,1280,1280]{1,2,0:T(8,128)(2,1)} fusion(bf16[1,2048,1280]{2,1,0:T(8,128)(2,1)} %get-tuple-element.46, bf16[1,2048,1280]{2,1,0:T(8,128)(2,1)} %get-tuple-element.45, bf16[2048,1280]{1,0:T(8,128)(2,1)} %all-gather.7.cloned.1.call-done), kind=kOutput, calls=%fused_computation.13 | convolution fusion | flops 13430292480 | bytes 22282240 | tf_op jit(solution)/shard_map/td,ctf->cdf/dot_general | solution.py:130
  596.0 6.5 fusion.20
  602.6 9.6 reduce-scatter.11.cloned.1.call-done
  617.9 44.3 %all-reduce = (f32[]{:T(128)}, f32[1280]{0:T(1024)S(1)}, f32[1280]{0:T(1024)S(1)}, f32[3,1280]{1,0:T(4,128)S(1)}) all-reduce(f32[]{:T(128)} %get-tuple-element.39, f32[1280]{0:T(1024)S(1)} %get-tuple-element.29, f32[1280]{0:T(1024)S(1)} %get-tuple-element.27, f32[3,1280]{1,0:T(4,128)S(1)} %fusion.49), channel_id=1, replica_groups=mesh['dp'=8,'mp'=4] {'dp','mp'}, use_global_device_ids=true, to_apply=%region_13.14 | all-reduce | flops 6401 | bytes 51208 | tf_op jit(solution)/shard_map/psum | solution.py:177
  664.7 365.7 %all-reduce.4.cloned.1.call-done = (bf16[3,1280,320]{1,2,0:T(8,128)(2,1)}, bf16[320,1280]{1,0:T(8,128)(2,1)}, bf16[2,1280,1280]{1,2,0:T(8,128)(2,1)}, bf16[1280,1280]{1,0:T(8,128)(2,1)}) async-done(((bf16[3,1280,320]{1,2,0:T(8,128)(2,1)}, bf16[320,1280]{1,0:T(8,128)(2,1)}, bf16[2,1280,1280]{1,2,0:T(8,128)(2,1)}, bf16[1280,1280]{1,0:T(8,128)(2,1)}), (bf16[3,1280,320]{1,2,0:T(8,128)(2,1)}, ...) | async-done | bytes 13107216 | tf_op jit(solution)/shard_map/psum | solution.py:181
  1041.0 5.8 convert_multiply_fusion
  1046.8 13.9 %copy.54 = f32[2,1280,1280]{2,1,0:T(8,128)} copy(f32[2,1280,1280]{1,2,0:T(8,128)} %convert_multiply_fusion) | data formatting | bytes 26214400
  (170 shorter events, 135.5 us)
Async XLA Ops:
  7.2 4.1 copy-start.31
  7.2 49.1 %all-gather.5.cloned.1.call-start = ((), (), s32[]{:S(2)}) async-start(), calls=%async_computation.4 | async-start | bytes 6553600 | tf_op jit(solution)/shard_map/all_gather | solution.py:87
  8.1 4.9 copy-start.35
  11.3 190.8 %copy-start.4 = (f32[512,1280]{1,0:T(8,128)}, f32[512,1280]{1,0:T(8,128)S(1)}, u32[]{:S(2)}) copy-start(f32[512,1280]{1,0:T(8,128)S(1)} %get-tuple-element.73) | copy-start | bytes 7864324
  13.0 189.1 %reduce-scatter.5.cloned.1.call-start = ((), (), s32[]{:S(2)}) async-start(), calls=%async_computation.5 | async-start | bytes 6553600 | tf_op jit(solution)/shard_map/reduce_scatter | solution.py:104
  127.9 3.5 copy-start.8
  127.9 3.5 copy-start.10
  127.9 3.5 copy-start.12
  131.4 4.3 copy-start.2
  150.5 54.8 %copy-start.30 = (f32[1280]{0:T(1024)S(1)}, f32[1280]{0:T(1024)}, u32[]{:S(2)}) copy-start(f32[1280]{0:T(1024)} %param.16) | copy-start | bytes 15364
  150.5 96.8 %all-gather.7.cloned.1.call-start = ((), (), s32[]{:S(2)}) async-start(), calls=%async_computation.6 | async-start | bytes 6553600 | tf_op jit(solution)/shard_map/all_gather | solution.py:108
  203.8 3.7 copy-start.18
  206.7 83.1 %all-gather.9.cloned.1.call-start = ((), (), s32[]{:S(2)}) async-start(), calls=%async_computation.8 | async-start | bytes 6553600 | tf_op jit(solution)/shard_map/all_gather | solution.py:122
  208.8 175.8 %reduce-scatter.9.cloned.1.call-start = ((), (), s32[]{:S(2)}) async-start(), calls=%async_computation.9 | async-start | bytes 6553600 | tf_op jit(solution)/shard_map/reduce_scatter | solution.py:136
  333.0 105.4 %reduce-scatter.7.cloned.1.call-start = ((), (), s32[]{:S(2)}) async-start(), calls=%async_computation.7 | async-start | bytes 6553600 | tf_op jit(solution)/shard_map/reduce_scatter | solution.py:118
  345.5 39.2 %copy-start.7 = (f32[512,1280]{1,0:T(8,128)S(1)}, f32[512,1280]{1,0:T(8,128)}, u32[]{:S(2)}) copy-start(f32[512,1280]{1,0:T(8,128)} %copy-done.6) | copy-start | bytes 7864324
  345.5 139.8 %all-gather.11.cloned.1.call-start = ((), (), s32[]{:S(2)}) async-start(), calls=%async_computation.10 | async-start | bytes 6553600 | tf_op jit(solution)/shard_map/all_gather | solution.py:141
  444.7 167.5 %reduce-scatter.11.cloned.1.call-start = ((), (), s32[]{:S(2)}) async-start(), calls=%async_computation.11 | async-start | bytes 6553600 | tf_op jit(solution)/shard_map/reduce_scatter | solution.py:171
  498.1 4.5 copy-start.3
  498.1 4.5 copy-start.21
  560.6 469.8 %all-reduce.4.cloned.1.call-start = ((), (), s32[]{:S(2)}) async-start(), calls=%async_computation.12 | async-start | bytes 26214400 | tf_op jit(solution)/shard_map/psum | solution.py:181
  560.7 32.5 %slice-start.4 = ((s8[5242880]{0:T(1024)(128)(4,1)}), s8[4194304]{0:T(1024)(128)(4,1)S(1)}, s32[]{:S(2)}) async-start(s8[5242880]{0:T(1024)(128)(4,1)} %bitcast.110), calls=%async_computation.17 | async-start | bytes 8388608
  560.7 35.3 %slice-start.2 = ((s8[5242880]{0:T(1024)(128)(4,1)}), s8[4194304]{0:T(1024)(128)(4,1)S(1)}, s32[]{:S(2)}) async-start(s8[5242880]{0:T(1024)(128)(4,1)} %bitcast.108), calls=%async_computation.15 | async-start | bytes 8388608
  572.8 20.4 %copy-start.27 = (bf16[2048,320]{1,0:T(8,128)(2,1)S(1)}, bf16[2048,320]{1,0:T(8,128)(2,1)}, u32[]{:S(2)}) copy-start(bf16[2048,320]{1,0:T(8,128)(2,1)} %convert_element_type.131) | copy-start | bytes 3932164
  572.8 20.4 %slice-start.5 = ((s8[5242880]{0:T(1024)(128)(4,1)}), s8[1048576]{0:T(1024)(128)(4,1)S(1)}, s32[]{:S(2)}) async-start(s8[5242880]{0:T(1024)(128)(4,1)} %bitcast.110), calls=%async_computation.18 | async-start | bytes 2097152
  572.8 23.2 %slice-start.3 = ((s8[5242880]{0:T(1024)(128)(4,1)}), s8[1048576]{0:T(1024)(128)(4,1)S(1)}, s32[]{:S(2)}) async-start(s8[5242880]{0:T(1024)(128)(4,1)} %bitcast.108), calls=%async_computation.16 | async-start | bytes 2097152
  602.6 9.6 copy-start.5
  602.6 9.6 copy-start.32
  602.6 9.6 copy-start.34
  1033.0 7.0 slice-start
  1036.3 4.7 slice-start.1
  1046.8 13.9 %copy-start.1 = (f32[3,1280]{1,0:T(4,128)S(1)}, f32[3,1280]{1,0:T(4,128)}, u32[]{:S(2)}) copy-start(f32[3,1280]{1,0:T(4,128)} %param.14) | copy-start | bytes 46084
  (21 other events, 45.8 us)
Sparse Core Ops, SparseCore 0:
  13.1 43.1 all-gather.4
  150.6 51.3 reduce-scatter.4
  206.8 40.4 all-gather.6
  249.4 40.4 all-gather.8
  333.2 51.3 reduce-scatter.8
  387.0 51.3 reduce-scatter.6
  444.9 40.4 all-gather.10
  560.8 51.3 reduce-scatter.10
  617.6 412.7 all-reduce.3
where the time goes:
time: 1080 us; the launch traced here: 1070 us
  waiting for transfers between devices  654 us (61%)
  matrix products  168 us (16%)
  local copies, waits for them, and re-layouts  122 us (11%)
  other arithmetic  63.7 us (6%)
  blocking collectives  44.3 us (4%)
  between operations  15.5 us (1%)
    psum x1, waiting for transfers between devices, body(): lax.psum(grad_qkv.astype(jnp.bfloat16), 'dp').astype(jnp.float32)  366 us
    reduce_scatter x1, waiting for transfers between devices, body(): lax.psum_scatter(mlp_part.astype(jnp.bfloat16), 'mp', scatter_dimension=0...  51.7 us
    reduce_scatter x1, waiting for transfers between devices, body(): lax.psum_scatter(attn_part.astype(jnp.bfloat16), 'mp', scatter_dimension=...  51.5 us
    unnamed x95, local copies, waits for them, and re-layouts  46.5 us
    psum x1, blocking collectives, body(): lax.psum((grad_gain_attn, grad_gain_mlp, grad_table, jnp.sum(mine_valid))...  44.3 us
    all_gather x1, waiting for transfers between devices, body(): lax.all_gather(grad_after.astype(jnp.bfloat16), 'mp', axis=0, tiled=True)  40.5 us
    reduce_scatter x1, waiting for transfers between devices, body(): lax.psum_scatter(mlp_back_part.astype(jnp.bfloat16), 'mp', scatter_dimens...  39.1 us
    all_gather x1, waiting for transfers between devices, body(): normed_mlp = lax.all_gather(normed_mlp_mine, 'mp', axis=0, tiled=True)  38.5 us
  transfers between devices with their start and end apart: 9, of which 9 were waited for; matrix products, arithmetic and copies ran while one was open for 9% of the time, Pallas kernels for 0%

commit v1 on v0

v1 whole, which is shorter than its diff:
```python
import functools

import jax
import jax.numpy as jnp
import numpy as np
from jax import lax
from jax.experimental import pallas as pl
from jax.experimental.pallas import tpu as pltpu
from jax.sharding import PartitionSpec as P

HS = 80
HALF = HS // 2
LANES = 128
NFREQ = 3
SEQ = 64
PAIR = 128

EPSILON = 1e-06
NEGATIVE = -1e30
HIGHEST = lax.Precision.HIGHEST
LOW = jnp.bfloat16
F32 = jnp.float32
VMEM_LIMIT = 56 * 1024 * 1024
LN2 = float(np.log(2.0))
QSCALE = float(HS**-0.5 / np.log(2.0))


def dot(a, b, ca=1, cb=0):
    return lax.dot_general(a, b, (((ca,), (cb,)), ((), ())), preferred_element_type=F32)


def head_selector(head_count):
    sel = np.zeros((head_count * HS, head_count * LANES), np.float32)
    for h in range(head_count):
        for half in range(2):
            for i in range(HALF):
                sel[h * HS + half * HALF + i, h * LANES + half * (LANES // 2) + i] = 1.0
    return jnp.asarray(sel, LOW)


def slot_tables():
    frequency = 10000.0 ** (-2.0 * np.arange(HALF) / HS)
    angles = np.arange(SEQ)[:, None] * frequency[None, :]
    pad = ((0, 0), (0, LANES // 2 - HALF))
    cosines = np.pad(np.cos(angles), pad)
    sines = np.pad(np.sin(angles), pad)
    return (
        jnp.asarray(np.concatenate([cosines, cosines], 1), F32),
        jnp.asarray(np.concatenate([-sines, sines], 1), F32),
    )


def row_angles(cp, sp, starts, first, count):
    cosines, sines = [], []
    c, s = cp[...], sp[...]
    for i in range(count):
        start = pl.ds(starts[first + i], 1)
        c0, s0 = cp[start, :], sp[start, :]
        cosines.append(c * c0 + s * s0)
        sines.append(s * c0 - c * s0)
    return jnp.concatenate(cosines, 0), jnp.concatenate(sines, 0)


def pair_mask(starts, first):
    j = lax.broadcasted_iota(jnp.int32, (PAIR, PAIR), 0)
    i = lax.broadcasted_iota(jnp.int32, (PAIR, PAIR), 1)
    begin = jnp.where(j < SEQ, starts[first], SEQ + starts[first + 1])
    same = (j < SEQ) == (i < SEQ)
    allowed = (same & (j <= i) & (j >= begin)) | (j == i)
    return jnp.where(allowed, 0.0, NEGATIVE)


def softmax_down(scores):
    exponent = jnp.exp2(scores - jnp.max(scores, 0, keepdims=True))
    return exponent * (1.0 / jnp.sum(exponent, 0, keepdims=True))


def pick(first, xs, a, b):
    @pl.when(first)
    def _():
        xs[...] = a[...]

    @pl.when(jnp.logical_not(first))
    def _():
        xs[...] = b[...]


def put(first, a, b, value):
    @pl.when(first)
    def _():
        a[...] = value

    @pl.when(jnp.logical_not(first))
    def _():
        b[...] = value


def attn_fwd_kernel(nh, starts, x0, x1, wqkv, wout, cp, sp, qkv, mixed, part0, part1, xs):
    step = pl.program_id(0)
    first = step < pl.num_programs(0) // 2
    width = nh * LANES
    rb = xs.shape[0]
    pick(first, xs, x0, x1)
    c, s = row_angles(cp, sp, starts, step * (rb // SEQ), rb // SEQ)
    for part in range(3):
        proj = dot(xs[...], wqkv[part])
        if part == 2:
            qkv[:, 2 * width :] = proj.astype(LOW)
            continue
        scale = QSCALE if part == 0 else 1.0
        cc, ss = c * scale, s * scale
        for h in range(nh):
            p = proj[:, h * LANES : (h + 1) * LANES]
            at = slice(part * width + h * LANES, part * width + (h + 1) * LANES)
            qkv[:, at] = (p * cc + pltpu.roll(p, LANES // 2, 1) * ss).astype(LOW)
    for b in range(rb // PAIR):
        rows = slice(b * PAIR, (b + 1) * PAIR)
        mask = pair_mask(starts, step * (rb // SEQ) + 2 * b)
        get = lambda part, h: qkv[rows, part * width + h * LANES : part * width + (h + 1) * LANES]
        scores = [dot(get(1, h), get(0, h), 1, 1) + mask for h in range(nh)]
        attention = [softmax_down(v).astype(LOW) for v in scores]
        for h in range(nh):
            mixed[rows, h * LANES : (h + 1) * LANES] = dot(attention[h], get(2, h), 0, 0).astype(LOW)
    put(first, part0, part1, dot(mixed[...], wout[...]).astype(LOW))


def attn_bwd_kernel(nh, starts, g0, g1, qkv, wqkv, wout, cp, sp, gproj, part0, part1, gs, gmix):
    step = pl.program_id(0)
    first = step < pl.num_programs(0) // 2
    width = nh * LANES
    rb = gs.shape[0]
    pick(first, gs, g0, g1)
    gmix[...] = dot(gs[...], wout[...], 1, 1).astype(LOW)
    c, s = row_angles(cp, sp, starts, step * (rb // SEQ), rb // SEQ)
    qc, qs = c * HS ** (-0.5), s * HS ** (-0.5)
    kc, ks = c * LN2, s * LN2
    for b in range(rb // PAIR):
        rows = slice(b * PAIR, (b + 1) * PAIR)
        mask = pair_mask(starts, step * (rb // SEQ) + 2 * b)
        at = lambda part, h: slice(part * width + h * LANES, part * width + (h + 1) * LANES)
        heads = range(nh)
        gm = [gmix[rows, at(0, h)] for h in heads]
        scores = [dot(qkv[rows, at(1, h)], qkv[rows, at(0, h)], 1, 1) + mask for h in heads]
        grads = [dot(qkv[rows, at(2, h)], gm[h], 1, 1) for h in heads]
        attention = [softmax_down(v) for v in scores]
        for h in heads:
            gproj[rows, at(2, h)] = dot(attention[h].astype(LOW), gm[h]).astype(LOW)
        low = []
        for h in heads:
            both = attention[h] * grads[h]
            low.append((both - attention[h] * jnp.sum(both, 0, keepdims=True)).astype(LOW))
        for h in heads:
            gk = dot(low[h], qkv[rows, at(0, h)])
            gproj[rows, at(1, h)] = (gk * kc[rows] - pltpu.roll(gk, LANES // 2, 1) * ks[rows]).astype(LOW)
        for h in heads:
            gq = dot(low[h], qkv[rows, at(1, h)], 0, 0)
            gproj[rows, at(0, h)] = (gq * qc[rows] - pltpu.roll(gq, LANES // 2, 1) * qs[rows]).astype(LOW)
    value = dot(gproj[:, :width], wqkv[0], 1, 1)
    value += dot(gproj[:, width : 2 * width], wqkv[1], 1, 1)
    value += dot(gproj[:, 2 * width :], wqkv[2], 1, 1)
    put(first, part0, part1, value.astype(LOW))


def mlp_kernel(x0, x1, y0, y1, wgate, wup, wdown, hidden, gpre, down0, down1, back0, back1, xs, ys):
    first = pl.program_id(0) < pl.num_programs(0) // 2
    pick(first, xs, x0, x1)
    pick(first, ys, y0, y1)
    gate = dot(xs[...], wgate[...])
    sig = jax.nn.sigmoid(gate)
    act = gate * sig
    slope = sig * (1.0 + gate * (1.0 - sig))
    up = dot(xs[...], wup[...])
    hidden[...] = (act * up).astype(LOW)
    gh = dot(ys[...], wdown[...], 1, 1)
    gpre[0] = (gh * up * slope).astype(LOW)
    gpre[1] = (gh * act).astype(LOW)
    put(first, down0, down1, dot(hidden[...], wdown[...]).astype(LOW))
    put(first, back0, back1, (dot(gpre[0], wgate[...], 1, 1) + dot(gpre[1], wup[...], 1, 1)).astype(LOW))


def resident(shape):
    return pl.BlockSpec(shape, lambda i, *_: (0,) * len(shape), pipeline_mode=pl.Buffered(1))


def by_rows(rows, width):
    return pl.BlockSpec((rows, width), lambda i, *_: (i, 0))


def two_parts(rows, width, n):
    return [
        pl.BlockSpec((rows, width), lambda i, *_: (jnp.minimum(i, n - 1), 0)),
        pl.BlockSpec((rows, width), lambda i, *_: (jnp.maximum(i - n, 0), 0)),
    ]


def params():
    return pltpu.CompilerParams(vmem_limit_bytes=VMEM_LIMIT, dimension_semantics=("arbitrary",))


def attn_forward(x, wqkv, wout, starts, tables):
    r, d = x[0].shape
    m = 2 * r
    width = wout.shape[0]
    nh = width // LANES
    rb = min(256, r)
    n = r // rb
    return pl.pallas_call(
        functools.partial(attn_fwd_kernel, nh),
        out_shape=[
            jax.ShapeDtypeStruct((m, 3 * width), LOW),
            jax.ShapeDtypeStruct((m, width), LOW),
            jax.ShapeDtypeStruct((r, d), LOW),
            jax.ShapeDtypeStruct((r, d), LOW),
        ],
        grid_spec=pltpu.PrefetchScalarGridSpec(
            num_scalar_prefetch=1,
            grid=(2 * n,),
            in_specs=[
                *two_parts(rb, d, n),
                resident((3, d, width)),
                resident((width, d)),
                resident((SEQ, LANES)),
                resident((SEQ, LANES)),
            ],
            out_specs=[by_rows(rb, 3 * width), by_rows(rb, width), *two_parts(rb, d, n)],
            scratch_shapes=[pltpu.VMEM((rb, d), LOW)],
        ),
        compiler_params=params(),
        cost_estimate=pl.CostEstimate(
            flops=2 * m * d * 4 * width + 4 * m * PAIR * width,
            bytes_accessed=2 * (2 * m * d + 4 * m * width + 4 * d * width),
            transcendentals=m * PAIR * nh,
        ),
        name="attn_fwd",
    )(starts, *x, wqkv, wout, *tables)


def attn_backward(g, qkv, wqkv, wout, starts, tables):
    r, d = g[0].shape
    m = 2 * r
    width = wout.shape[0]
    nh = width // LANES
    rb = min(256, r)
    n = r // rb
    return pl.pallas_call(
        functools.partial(attn_bwd_kernel, nh),
        out_shape=[
            jax.ShapeDtypeStruct((m, 3 * width), LOW),
            jax.ShapeDtypeStruct((r, d), LOW),
            jax.ShapeDtypeStruct((r, d), LOW),
        ],
        grid_spec=pltpu.PrefetchScalarGridSpec(
            num_scalar_prefetch=1,
            grid=(2 * n,),
            in_specs=[
                *two_parts(rb, d, n),
                by_rows(rb, 3 * width),
                resident((3, d, width)),
                resident((width, d)),
                resident((SEQ, LANES)),
                resident((SEQ, LANES)),
            ],
            out_specs=[by_rows(rb, 3 * width), *two_parts(rb, d, n)],
            scratch_shapes=[pltpu.VMEM((rb, d), LOW), pltpu.VMEM((rb, width), LOW)],
        ),
        compiler_params=params(),
        cost_estimate=pl.CostEstimate(
            flops=2 * m * d * 4 * width + 12 * m * PAIR * width,
            bytes_accessed=2 * (2 * m * d + 6 * m * width + 4 * d * width),
            transcendentals=m * PAIR * nh,
        ),
        name="attn_bwd",
    )(starts, *g, qkv, wqkv, wout, *tables)


def mlp_both(x, gy, wgate, wup, wdown):
    r, d = x[0].shape
    m = 2 * r
    ff = wgate.shape[1]
    rb = min(256, r)
    n = r // rb
    part = jax.ShapeDtypeStruct((r, d), LOW)
    return pl.pallas_call(
        mlp_kernel,
        grid=(2 * n,),
        out_shape=[
            jax.ShapeDtypeStruct((m, ff), LOW),
            jax.ShapeDtypeStruct((2, m, ff), LOW),
            part,
            part,
            part,
            part,
        ],
        in_specs=[
            *two_parts(rb, d, n),
            *two_parts(rb, d, n),
            resident((d, ff)),
            resident((d, ff)),
            resident((ff, d)),
        ],
        out_specs=[
            by_rows(rb, ff),
            pl.BlockSpec((2, rb, ff), lambda i: (0, i, 0)),
            *two_parts(rb, d, n),
            *two_parts(rb, d, n),
        ],
        scratch_shapes=[pltpu.VMEM((rb, d), LOW), pltpu.VMEM((rb, d), LOW)],
        compiler_params=params(),
        cost_estimate=pl.CostEstimate(
            flops=2 * m * d * 6 * ff,
            bytes_accessed=2 * (4 * m * d + 3 * m * ff + 3 * d * ff),
            transcendentals=m * ff,
        ),
        name="mlp_both",
    )(*x, *gy, wgate, wup, wdown)


def weight_grad(a, b, plane=None):
    ra, wide = a[0].shape
    rb, n = b[0].shape[-2:]
    r = min(ra, rb)
    nb = 256 if n % 256 == 0 else 128
    if plane is None:
        b_spec = pl.BlockSpec((rb, nb), lambda i: (0, i))
    else:
        b_spec = pl.BlockSpec((None, rb, nb), lambda i: (plane, 0, i))

    def kernel(*refs):
        xs, ys, out = refs[: len(a)], refs[len(a) : -1], refs[-1]
        total = None
        for at in range(0, len(a) * ra, r):
            x = xs[at // ra][at % ra : at % ra + r]
            y = ys[at // rb][at % rb : at % rb + r]
            part = dot(x, y, 0, 0)
            total = part if total is None else total + part
        out[...] = total.astype(LOW)

    return pl.pallas_call(
        kernel,
        grid=(n // nb,),
        out_shape=jax.ShapeDtypeStruct((wide, n), LOW),
        in_specs=[resident((ra, wide))] * len(a) + [b_spec] * len(b),
        out_specs=pl.BlockSpec((wide, nb), lambda i: (0, i)),
        compiler_params=params(),
        cost_estimate=pl.CostEstimate(
            flops=2 * len(a) * ra * wide * n,
            bytes_accessed=2 * (len(a) * ra * (wide + n) + wide * n),
            transcendentals=0,
        ),
        name="weight_grad",
    )(*a, *b)


def attn_weight_grad(gproj, mixed, normed, ga, selector):
    m, wide = gproj[0].shape
    width = wide // 3
    r, d = normed[0].shape
    real = selector.shape[0]
    chunks = len(normed)
    kb = 256 if d % 256 == 0 else d

    def kernel(*refs):
        gp, mx = refs[: len(gproj)], refs[len(gproj) : 2 * len(gproj)]
        nm, g, sel, out = refs[2 * len(gproj) : -2 - chunks], refs[-2 - chunks : -2], refs[-2], refs[-1]
        for c in range(4):
            total = None
            for i in range(chunks):
                k, at = i * r // m, i * r % m
                x = mx[k][at : at + r] if c == 3 else gp[k][at : at + r, c * width : (c + 1) * width]
                part = dot(x, (g if c == 3 else nm)[i][...], 0, 0)
                total = part if total is None else total + part
            out[c * real : (c + 1) * real] = dot(sel[...], total.astype(LOW)).astype(LOW)

    return pl.pallas_call(
        kernel,
        grid=(d // kb,),
        out_shape=jax.ShapeDtypeStruct((4 * real, d), LOW),
        in_specs=[resident((m, wide))] * len(gproj)
        + [resident((m, width))] * len(mixed)
        + [pl.BlockSpec((r, kb), lambda i: (0, i))] * (2 * chunks)
        + [resident((real, width))],
        out_specs=pl.BlockSpec((4 * real, kb), lambda i: (0, i)),
        compiler_params=params(),
        cost_estimate=pl.CostEstimate(
            flops=2 * chunks * r * d * 4 * width,
            bytes_accessed=2 * chunks * r * (4 * width + 2 * d),
            transcendentals=0,
        ),
        name="attn_weight_grad",
    )(*gproj, *mixed, *normed, *ga, selector)


class Group:
    def __init__(self, mesh):
        self.n = mesh.shape["mp"]
        self.chips = self.n // 2

    def core(self, x):
        return lax.ppermute(x, "mp", [(i, i ^ 1) for i in range(self.n)])

    def from_chip(self, x, k):
        return lax.ppermute(x, "mp", [((i + 2 * k) % self.n, i) for i in range(self.n)])

    def to_chip(self, x, k):
        return lax.ppermute(x, "mp", [(i, (i + 2 * k) % self.n) for i in range(self.n)])

    def gather(self, x):
        mine = [x] + [self.from_chip(x, k) for k in range(1, self.chips)]
        return [(v, self.core(v)) for v in mine]

    def scatter(self, parts):
        total = None
        for k in reversed(range(self.chips)):
            mine = parts[k][0].astype(F32) + self.core(parts[k][1]).astype(F32)
            if k:
                mine = self.to_chip(mine.astype(LOW), k).astype(F32)
            total = mine if total is None else total + mine
        return total


OUTER = 4
CHUNK = 80
MESH = pl.DeviceIdType.MESH


def sum_kernel(inner, group, early, halves, late_pieces, *refs):
    count = len(halves)
    full, refs = refs[:count], refs[count:]
    got, refs = refs[:early], refs[early:]
    small, out, small_out, refs = *refs[:3], refs[3:]
    loc, rc, rb1, rb2, tot, refs = *refs[:5], refs[5:]
    load, late_send, late_recv, s1, r1, s2, r2, s3, r3, s4, r4, keep, refs = *refs[:12], refs[12:]
    sm0, sm1, sm2, small_send, small_recv = refs
    dp = lax.axis_index("dp")
    mp = lax.axis_index("mp")
    place, side = dp // inner, lax.rem(dp, inner)
    outside = jnp.logical_or(place == 0, place == OUTER - 1)
    inside = jnp.logical_not(outside)
    beside = jnp.where(place < OUTER // 2, 1 - place, 5 - place)
    across = (OUTER - 1) - place
    peers = [lax.rem(side + j, inner) for j in range(1, inner)]
    at = lambda p, i: (p * inner + i, mp)

    rounds = []
    me = (mp, side, place)
    others = [
        [(dp, lax.rem(mp + j, group)) for j in range(1, group)],
        [at(place, peer) for peer in peers],
        [at(lax.rem(place + j, OUTER), side) for j in range(1, OUTER)],
    ]
    used = 0
    for mine, buf, devices in zip(me, (sm0, sm1, sm2), others):
        copies = []
        for device in devices:
            copies.append(
                pltpu.make_async_remote_copy(
                    src_ref=buf.at[mine], dst_ref=buf.at[mine], send_sem=small_send.at[used],
                    recv_sem=small_recv.at[used], device_id=device, device_id_type=MESH,
                )
            )
            used += 1
        rounds.append((mine, buf, copies))

    def small_round(i):
        if i:
            for copy in rounds[i - 1][2]:
                copy.wait()
            buf = rounds[i - 1][1]
            value = buf[0]
            for j in range(1, buf.shape[0]):
                value += buf[j]
        else:
            value = small[...]
        if i < len(rounds):
            mine, buf, copies = rounds[i]
            buf[mine] = value
            for copy in copies:
                copy.start()
        else:
            small_out[...] = value

    barrier = pltpu.get_barrier_semaphore()
    for devices in others:
        for device in devices:
            pl.semaphore_signal(barrier, inc=1, device_id=device, device_id_type=MESH)
    pl.semaphore_wait(barrier, sum(len(devices) for devices in others))

    offsets = [sum(halves[:p]) for p in range(count)]
    chunks = sum(halves) // CHUNK

    late = count - 1
    late_copies = []
    for j, peer in enumerate(peers):
        for c in range(late_pieces):
            rows = halves[late] // late_pieces
            late_copies.append(
                pltpu.make_async_remote_copy(
                    src_ref=full[late].at[pl.ds(peer * halves[late] + c * rows, rows)],
                    dst_ref=rc.at[j, pl.ds(offsets[late] + c * rows, rows)],
                    send_sem=late_send.at[j * late_pieces + c],
                    recv_sem=late_recv.at[j * late_pieces + c],
                    device_id=at(place, peer),
                    device_id_type=MESH,
                )
            )
    for copy in late_copies:
        copy.start()

    loads = []
    for p in range(count):
        one = [(full[p].at[pl.ds(side * halves[p], halves[p])], loc.at[pl.ds(offsets[p], halves[p])])]
        if p < early:
            for j in range(inner - 1):
                one.append((got[p].at[j], rc.at[j, pl.ds(offsets[p], halves[p])]))
        loads.append(
            [pltpu.make_async_copy(a, b, load.at[p * inner + i]) for i, (a, b) in enumerate(one)]
        )
    for one in loads:
        for copy in one:
            copy.start()
    small_round(0)

    def to_beside(src, dst, send, recv, t):
        rows = pl.ds(t * CHUNK, CHUNK)
        return pltpu.make_async_remote_copy(
            src_ref=src.at[rows], dst_ref=dst.at[rows], send_sem=send.at[t], recv_sem=recv.at[t],
            device_id=at(beside, side), device_id_type=MESH,
        )

    def to_across(t):
        rows = pl.ds(t * CHUNK, CHUNK)
        return pltpu.make_async_remote_copy(
            src_ref=loc.at[rows], dst_ref=rb2.at[rows], send_sem=s2.at[t], recv_sem=r2.at[t],
            device_id=at(across, side), device_id_type=MESH,
        )

    def to_peer(j, t):
        rows = pl.ds(t * CHUNK, CHUNK)
        return pltpu.make_async_remote_copy(
            src_ref=tot.at[rows], dst_ref=out.at[side, rows], send_sem=s4.at[j, t], recv_sem=r4.at[j, t],
            device_id=at(place, peers[j]), device_id_type=MESH,
        )

    def to_self(t):
        rows = pl.ds(t * CHUNK, CHUNK)
        return pltpu.make_async_copy(tot.at[rows], out.at[side, rows], keep.at[t])

    def hand_out(t):
        for j in range(inner - 1):
            to_peer(j, t).start()
        to_self(t).start()

    def step(t, carry):
        rows = pl.ds(pl.multiple_of(t * CHUNK, CHUNK), CHUNK)

        for i in range(1, len(rounds) + 1):

            @pl.when(t == 2 * i)
            def _(i=i):
                small_round(i)

        @pl.when(t < chunks)
        def _():
            for p in range(count):

                @pl.when(t == offsets[p] // CHUNK)
                def _(p=p):
                    for copy in loads[p]:
                        copy.wait()

            for c in range(late_pieces):

                @pl.when(t == (offsets[late] + c * (halves[late] // late_pieces)) // CHUNK)
                def _(c=c):
                    for j in range(inner - 1):
                        late_copies[j * late_pieces + c].wait_recv()

            total = loc[rows].astype(F32)
            for j in range(inner - 1):
                total += rc[j, rows].astype(F32)
            loc[rows] = total.astype(LOW)

            @pl.when(outside)
            def _():
                to_beside(loc, rb1, s1, r1, t).start()

            @pl.when(inside)
            def _():
                to_beside(loc, rb1, s1, r1, t).wait_recv()
                loc[rows] = (loc[rows].astype(F32) + rb1[rows].astype(F32)).astype(LOW)
                to_across(t).start()

        u = t - 1

        @pl.when(jnp.logical_and(inside, jnp.logical_and(u >= 0, u < chunks)))
        def _():
            ready = pl.ds(pl.multiple_of(u * CHUNK, CHUNK), CHUNK)
            to_across(u).wait_recv()
            tot[ready] = (loc[ready].astype(F32) + rb2[ready].astype(F32)).astype(LOW)
            to_beside(tot, tot, s3, r3, u).start()
            hand_out(u)

        w = t - LAG

        @pl.when(jnp.logical_and(outside, w >= 0))
        def _():
            to_beside(tot, tot, s3, r3, w).wait_recv()
            hand_out(w)

        return carry

    lax.fori_loop(0, chunks + LAG, step, 0)

    def finish(t, carry):
        @pl.when(outside)
        def _():
            to_beside(loc, rb1, s1, r1, t).wait_send()

        @pl.when(inside)
        def _():
            to_across(t).wait_send()
            to_beside(tot, tot, s3, r3, t).wait_send()

        for j in range(inner - 1):
            to_peer(j, t).wait()
        to_self(t).wait()
        return carry

    lax.fori_loop(0, chunks, finish, 0)
    for copy in late_copies:
        copy.wait_send()


LAG = 6


class Reducer:
    def __init__(self, mesh):
        self.inner = mesh.shape["dp"] // OUTER
        self.group = mesh.shape["mp"]

    def exchange(self, x):
        side = lax.rem(lax.axis_index("dp"), self.inner)
        rows = x.shape[0] // self.inner
        got = []
        for j in range(1, self.inner):
            pairs = []
            for o in range(OUTER):
                for i in range(self.inner):
                    pairs.append((o * self.inner + i, o * self.inner + (i + j) % self.inner))
            share = lax.dynamic_slice_in_dim(x, lax.rem(side + j, self.inner) * rows, rows)
            got.append(lax.ppermute(share, "dp", pairs))
        return jnp.stack(got)

    def reduce(self, pieces, got, small):
        inner = self.inner
        width = pieces[0].shape[1]
        halves = tuple(p.shape[0] // inner for p in pieces)
        share = sum(halves)
        chunks = share // CHUNK
        any_spec = pl.BlockSpec(memory_space=pl.ANY)
        late_pieces = halves[-1] // CHUNK // 2
        buffer = pltpu.VMEM((share, width), LOW)
        sems = lambda *shape: pltpu.SemaphoreType.DMA(shape)
        return pl.pallas_call(
            functools.partial(sum_kernel, inner, self.group, len(got), halves, late_pieces),
            out_shape=[
                jax.ShapeDtypeStruct((inner, share, width), LOW),
                jax.ShapeDtypeStruct(small.shape, F32),
            ],
            in_specs=[any_spec] * (len(pieces) + len(got)) + [pl.BlockSpec(memory_space=pltpu.VMEM)],
            out_specs=[any_spec, pl.BlockSpec(memory_space=pltpu.VMEM)],
            scratch_shapes=[
                buffer,
                pltpu.VMEM((inner - 1, share, width), LOW),
                buffer,
                buffer,
                buffer,
                sems(len(pieces) * inner),
                sems((inner - 1) * late_pieces),
                sems((inner - 1) * late_pieces),
                *[sems(chunks) for _ in range(6)],
                sems(inner - 1, chunks),
                sems(inner - 1, chunks),
                sems(chunks),
                pltpu.VMEM((self.group, *small.shape), F32),
                pltpu.VMEM((inner, *small.shape), F32),
                pltpu.VMEM((OUTER, *small.shape), F32),
                sems(self.group + inner + OUTER - 3),
                sems(self.group + inner + OUTER - 3),
            ],
            compiler_params=pltpu.CompilerParams(
                collective_id=0, has_side_effects=True, vmem_limit_bytes=VMEM_LIMIT
            ),
            cost_estimate=pl.CostEstimate(flops=0, bytes_accessed=600_000_000, transcendentals=0),
            name="sum_over_dp",
        )(*pieces, *got, small)


def norm_forward(values, gain):
    inverse = lax.rsqrt(jnp.mean(values * values, -1, keepdims=True) + EPSILON)
    return ((values * inverse * gain).astype(LOW), inverse)


def norm_backward(values, inverse, gain, grad_normed):
    normal = values * inverse
    grad_gain = jnp.sum(grad_normed * normal, 0)
    scaled = grad_normed * gain
    grad_values = inverse * (scaled - normal * jnp.mean(scaled * normal, -1, keepdims=True))
    return (grad_values, grad_gain)


def body(
    mesh,
    rows,
    lengths,
    freq_class,
    freq_table,
    gain_attn,
    gain_mlp,
    w_qkv,
    w_out,
    w_gate_up,
    w_down,
    cotangent,
):
    group = Group(mesh)
    reducer = Reducer(mesh)
    local_rows, d = rows.shape
    own_series = local_rows // SEQ
    mp_index = lax.axis_index("mp")
    heads_width = w_out.shape[0]
    head_count = heads_width // HS
    ff = w_down.shape[0]
    chips = range(group.chips)

    places = jnp.arange(group.n, dtype=jnp.int32)
    owners = ((mp_index // 2 + places // 2) % group.chips) * 2 + (mp_index % 2 + places) % 2
    starts = (SEQ - lengths.reshape(group.n, own_series))[owners]
    group_starts = [starts[2 * k : 2 * k + 2].reshape(-1) for k in chips]
    tables = slot_tables()
    slots = jnp.arange(SEQ, dtype=jnp.int32)
    mine_valid = (slots[None, :] >= starts[0][:, None]).astype(F32)

    by_series = lambda v: v.reshape(own_series, SEQ, d)
    picked = freq_table[NFREQ - 1][None]
    for f in range(NFREQ - 1):
        picked = jnp.where((freq_class == f)[:, None], freq_table[f][None], picked)
    start_rows = (by_series(rows) + picked[:, None]).reshape(local_rows, d)
    normed_mine, inverse_attn = norm_forward(start_rows, gain_attn)
    normed = group.gather(normed_mine)
    grad_output = (by_series(cotangent) * mine_valid[:, :, None]).reshape(local_rows, d)
    grad_down_in = group.gather(grad_output.astype(LOW))

    selector = head_selector(head_count)
    qkv_low = jnp.einsum("cdf,fg->cdg", w_qkv.astype(LOW), selector, preferred_element_type=F32).astype(LOW)
    out_low = dot(selector, w_out.astype(LOW), 0, 0).astype(LOW)
    gate_low = w_gate_up[0].astype(LOW)
    up_low = w_gate_up[1].astype(LOW)
    down_low = w_down.astype(LOW)

    fwd = [attn_forward(normed[k], qkv_low, out_low, group_starts[k], tables) for k in chips]
    after_attn = start_rows + group.scatter([f[2:] for f in fwd])
    normed_mlp_mine, inverse_mlp = norm_forward(after_attn, gain_mlp)
    normed_mlp = group.gather(normed_mlp_mine)

    mlp = [mlp_both(normed_mlp[k], grad_down_in[k], gate_low, up_low, down_low) for k in chips]
    grad_normed_mlp = group.scatter([m[4:] for m in mlp])
    output = after_attn + group.scatter([m[2:4] for m in mlp])
    flat = lambda pairs: [v for pair in pairs for v in pair]
    grad_down = weight_grad([m[0] for m in mlp], flat(grad_down_in))
    ups = [weight_grad(flat(normed_mlp), [m[1] for m in mlp], c) for c in range(2)]
    pieces = [grad_down] + (ups if ff >= d else [jnp.concatenate(ups, 1)])
    got = [reducer.exchange(p) for p in pieces]

    grad_rows_mlp, grad_gain_mlp = norm_backward(after_attn, inverse_mlp, gain_mlp, grad_normed_mlp)
    grad_after = grad_output + grad_rows_mlp
    grad_attn_in = group.gather(grad_after.astype(LOW))

    bwd = [
        attn_backward(grad_attn_in[k], fwd[k][0], qkv_low, out_low, group_starts[k], tables) for k in chips
    ]
    grad_normed = group.scatter([b[1:] for b in bwd])
    pieces.append(
        attn_weight_grad(
            [b[0] for b in bwd], [f[1] for f in fwd], flat(normed), flat(grad_attn_in), selector
        )
    )

    grad_rows_attn, grad_gain_attn = norm_backward(start_rows, inverse_attn, gain_attn, grad_normed)
    grad_rows = grad_after + grad_rows_attn
    series_sums = jnp.sum(by_series(grad_rows), 1)
    grad_table = [jnp.sum(jnp.where((freq_class == f)[:, None], series_sums, 0.0), 0) for f in range(NFREQ)]

    tokens = jnp.full((d,), jnp.sum(mine_valid))
    zero = jnp.zeros((d,), F32)
    small = jnp.stack([grad_gain_attn, grad_gain_mlp, *grad_table, tokens, zero, zero])
    sums, small = reducer.reduce(pieces, got, small)
    root_scale = lax.rsqrt(small[2 + NFREQ, 0])
    small = small * root_scale
    finals, offset = [], 0
    for piece in pieces:
        share = piece.shape[0] // reducer.inner
        finals.append(sums[:, offset : offset + share].reshape(piece.shape))
        offset += share
    down_out = finals[0].astype(F32) * root_scale
    if len(finals) == 3:
        gate_up_out = jnp.stack([finals[1][:, :ff], finals[1][:, ff:]]).astype(F32) * root_scale
    else:
        gate_up_out = jnp.stack(finals[1:3]).astype(F32) * root_scale
    identity = jnp.eye(heads_width, dtype=LOW)
    last = finals[-1]
    qkv_out = jnp.stack(
        [dot(last[c * heads_width : (c + 1) * heads_width], identity, 0, 0) * root_scale for c in range(3)]
    )
    out_out = last[3 * heads_width :].astype(F32) * root_scale
    return (
        output,
        grad_rows,
        qkv_out,
        out_out,
        gate_up_out,
        down_out,
        small[0],
        small[1],
        small[2 : 2 + NFREQ],
    )


def solution(mesh):
    return jax.shard_map(
        functools.partial(body, mesh),
        mesh=mesh,
        in_specs=(
            P(("dp", "mp"), None),
            P("dp"),
            P(("dp", "mp")),
            P(),
            P(),
            P(),
            P(None, None, "mp"),
            P("mp", None),
            P(None, None, "mp"),
            P("mp", None),
            P(("dp", "mp"), None),
        ),
        out_specs=(
            P(("dp", "mp"), None),
            P(("dp", "mp"), None),
            P(None, None, "mp"),
            P("mp", None),
            P(None, None, "mp"),
            P("mp", None),
            P(),
            P(),
            P(),
        ),
        check_vma=False,
    )
```

time: 1080 us -> 685 us (0.63)
  waiting for transfers between devices: 654 us -> 175 us
  Pallas kernels: 0 us -> 394 us
  matrix products: 168 us -> 11.8 us
  local copies, waits for them, and re-layouts: 122 us -> 23.9 us
  blocking collectives: 44.3 us -> 0 us
  starting transfers between devices: 0.37 us -> 19 us
  between operations: 15.5 us -> 2.18 us
    pallas_call x0 -> x11, Pallas kernels: none -> 394 us  [the longest x1 194 us: reduce(): pl.pallas_call(functools.partial(sum_kernel, inner, self.group, len(got),...]
    psum x1 -> x0, waiting for transfers between devices: 366 us -> none  [body(): lax.psum(grad_qkv.astype(jnp.bfloat16), 'dp').astype(jnp.float32)]
    ppermute x0 -> x27, waiting for transfers between devices: none -> 175 us  [the longest x4 93.3 us: from_chip(): lax.ppermute(x, 'mp', [((i + 2 * k) % self.n, i) for i in range(self.n)])]
    dot_general x20 -> x5, matrix products: 168 us -> 11.8 us  [the longest x1 6.56 us: body(): jnp.einsum('cdf,fg->cdg', w_qkv.astype(LOW), selector, preferred_element_...]
    reduce_scatter x4 -> x0, waiting for transfers between devices: 152 us -> none  [the longest x1 51.7 us: body(): lax.psum_scatter(mlp_part.astype(jnp.bfloat16), 'mp', scatter_dimension=0...]
    all_gather x4 -> x0, waiting for transfers between devices: 136 us -> none  [the longest x1 40.5 us: body(): lax.all_gather(grad_after.astype(jnp.bfloat16), 'mp', axis=0, tiled=True)]
    psum x1 -> x0, blocking collectives: 44.3 us -> none  [body(): lax.psum((grad_gain_attn, grad_gain_mlp, grad_table, jnp.sum(mine_valid))...]
    unnamed x95 -> x50, local copies, waits for them, and re-layouts: 46.5 us -> 4.7 us
  transfers between devices with their start and end apart: 9 -> 27, of which waited for: 9 -> 8; matrix products, arithmetic and copies ran while one was open for 9% -> 8% of each run, Pallas kernels for 0% -> 29%
where the time goes in v1:
time: 685 us; the launch traced here: 681 us
  Pallas kernels  394 us (58%)
  waiting for transfers between devices  175 us (26%)
  other arithmetic  55.1 us (8%)
  local copies, waits for them, and re-layouts  23.9 us (3%)
  starting transfers between devices  19 us (3%)
  matrix products  11.8 us (2%)
    pallas_call x1, Pallas kernels, reduce(): pl.pallas_call(functools.partial(sum_kernel, inner, self.group, len(got),...  194 us
    ppermute x4, waiting for transfers between devices, from_chip(): lax.ppermute(x, 'mp', [((i + 2 * k) % self.n, i) for i in range(self.n)])  93.3 us
    ppermute x4, waiting for transfers between devices, to_chip(): lax.ppermute(x, 'mp', [(i, (i + 2 * k) % self.n) for i in range(self.n)])  81.4 us
    pallas_call x2, Pallas kernels, mlp_both(): pl.pallas_call(mlp_kernel, grid=(2 * n,), out_shape=[jax.ShapeDtypeStruct...  66.2 us
    pallas_call x3, Pallas kernels, weight_grad(): pl.pallas_call(kernel, grid=(n // nb,), out_shape=jax.ShapeDtypeStruct((w...  35.4 us
    pallas_call x2, Pallas kernels, attn_backward(): pl.pallas_call(functools.partial(attn_bwd_kernel, nh), out_shape=[jax.Sha...  34.8 us
    pallas_call x1, Pallas kernels, attn_weight_grad(): pl.pallas_call(kernel, grid=(d // kb,), out_shape=jax.ShapeDtypeStruct((4...  32.4 us
    pallas_call x2, Pallas kernels, attn_forward(): pl.pallas_call(functools.partial(attn_fwd_kernel, nh), out_shape=[jax.Sha...  31.2 us
  transfers between devices with their start and end apart: 27, of which 8 were waited for; matrix products, arithmetic and copies ran while one was open for 8% of the time, Pallas kernels for 29%

profile of v1, /device:TPU:0, one launch (start us, length us, event | category | flops | bytes accessed | tf_op | source)
XLA Modules:
  0.0 681.5 jit_solution(10177129830157137606)
XLA Ops:
  6.0 3.0 collective-permute-start
  8.9 29.1 %collective-permute-done.x0.refs_6_ = bf16[512,1280]{1,0:T(8,128)(2,1)} collective-permute-done((bf16[512,1280]{1,0:T(8,128)(2,1)}, bf16[512,1280]{1,0:T(8,128)(2,1)}, u32[]{:S(2)}, u32[]{:S(2)}) %collective-permute-start) | collective-permute-done | bytes 1310752 | tf_op jit(solution)/shard_map/ppermute | solution.py:402
  39.3 3.4 convolution_convert_fusion.1.wout
  42.7 6.6 fusion.wqkv
  49.3 15.8 %attn_fwd.2 = (bf16[1024,1536]{1,0:T(8,128)(2,1)}, bf16[1024,512]{1,0:T(8,128)(2,1)}, bf16[512,1280]{1,0:T(8,128)(2,1)}, bf16[512,1280]{1,0:T(8,128)(2,1)}) custom-call(s32[16]{0:T(128)} %reshape.281.starts, bf16[512,1280]{1,0:T(8,128)(2,1)} %collective-permute-done.x0.refs_6_, bf16[512,1280]{1,0:T(8,128)(2,1)} %collective-permute-done.1.x1.refs_7_, ...), custom_call_target="tpu_custom_call" | custom-call | flops 5637144576 | bytes 14680064 | tf_op jit(solution)/shard_map/attn_fwd/pallas_call | solution.py:207
  66.1 15.4 %attn_fwd.3 = (bf16[1024,1536]{1,0:T(8,128)(2,1)}, bf16[1024,512]{1,0:T(8,128)(2,1)}, bf16[512,1280]{1,0:T(8,128)(2,1)}, bf16[512,1280]{1,0:T(8,128)(2,1)}) custom-call(s32[16]{0:T(128)} %reshape.282.starts, bf16[512,1280]{1,0:T(8,128)(2,1)} %multiply_convert_fusion.1.x0.refs_4_, bf16[512,1280]{1,0:T(8,128)(2,1)} %collective-permute-done.4.x1.refs_5_, ...), custom_call_target="tpu_custom_call" | custom-call | flops 5637144576 | bytes 14680064 | tf_op jit(solution)/shard_map/attn_fwd/pallas_call | solution.py:207
  81.6 2.7 add_convert_fusion.3
  86.2 3.1 multiply_convert_fusion.2.y0.refs_2_
  89.5 26.6 %collective-permute-done.3 = bf16[512,1280]{1,0:T(8,128)(2,1)} collective-permute-done((bf16[512,1280]{1,0:T(8,128)(2,1)}, bf16[512,1280]{1,0:T(8,128)(2,1)}, u32[]{:S(2)}, u32[]{:S(2)}) %collective-permute-start.3) | collective-permute-done | bytes 1310752 | tf_op jit(solution)/shard_map/ppermute | solution.py:405
  123.3 8.1 %convert.5 = bf16[2,1280,1280]{2,1,0:T(8,128)(2,1)} convert(f32[2,1280,1280]{2,1,0:T(8,128)} %param.22) | non-fusion elementwise | flops 3276800 | bytes 19660800 | tf_op jit(solution)/shard_map/convert.2
  131.4 5.1 convert_element_type.145.wdown
  136.5 7.7 %collective-permute-done.8.y0.refs_4_ = bf16[512,1280]{1,0:T(8,128)(2,1)} collective-permute-done((bf16[512,1280]{1,0:T(8,128)(2,1)}, bf16[512,1280]{1,0:T(8,128)(2,1)}, u32[]{:S(2)}, u32[]{:S(2)}) %collective-permute-start.8) | collective-permute-done | bytes 1310752 | tf_op jit(solution)/shard_map/ppermute | solution.py:402
  144.2 27.7 %collective-permute-done.6.x0.refs_2_ = bf16[512,1280]{1,0:T(8,128)(2,1)} collective-permute-done((bf16[512,1280]{1,0:T(8,128)(2,1)}, bf16[512,1280]{1,0:T(8,128)(2,1)}, u32[]{:S(2)}, u32[]{:S(2)}) %collective-permute-start.6) | collective-permute-done | bytes 1310752 | tf_op jit(solution)/shard_map/ppermute | solution.py:402
  171.9 3.1 slice_bitcast_fusion
  177.1 33.2 %mlp_both.2 = (bf16[1024,1280]{1,0:T(8,128)(2,1)}, bf16[2,1024,1280]{2,1,0:T(8,128)(2,1)}, bf16[512,1280]{1,0:T(8,128)(2,1)}, bf16[512,1280]{1,0:T(8,128)(2,1)},...) custom-call(bf16[512,1280]{1,0:T(8,128)(2,1)} %collective-permute-done.6.x0.refs_2_, bf16[512,1280]{1,0:T(8,128)(2,1)} %copy-done.21, ...), custom_call_target="tpu_custom_call" | custom-call | flops 20132659200 | bytes 28180480 | tf_op jit(solution)/shard_map/mlp_both/pallas_call | solution.py:283
  210.8 33.0 %mlp_both.3 = (bf16[1024,1280]{1,0:T(8,128)(2,1)}, bf16[2,1024,1280]{2,1,0:T(8,128)(2,1)}, bf16[512,1280]{1,0:T(8,128)(2,1)}, bf16[512,1280]{1,0:T(8,128)(2,1)},...) custom-call(bf16[512,1280]{1,0:T(8,128)(2,1)} %multiply_convert_fusion.x0.refs_0_, ...), custom_call_target="tpu_custom_call" | custom-call | flops 20132659200 | bytes 28180480 | tf_op jit(solution)/shard_map/mlp_both/pallas_call | solution.py:283
  247.7 28.4 %collective-permute-done.16 = bf16[512,1280]{1,0:T(8,128)(2,1)S(1)} collective-permute-done((bf16[512,1280]{1,0:T(8,128)(2,1)S(1)}, bf16[512,1280]{1,0:T(8,128)(2,1)S(1)}, u32[]{:S(2)}, u32[]{:S(2)}) %collective-permute-start.16) | collective-permute-done | bytes 1310752 | tf_op jit(solution)/shard_map/ppermute | solution.py:405
  277.2 26.4 %collective-permute-done.11 = bf16[512,1280]{1,0:T(8,128)(2,1)S(1)} collective-permute-done((bf16[512,1280]{1,0:T(8,128)(2,1)S(1)}, bf16[512,1280]{1,0:T(8,128)(2,1)S(1)}, u32[]{:S(2)}, u32[]{:S(2)}) %collective-permute-start.11) | collective-permute-done | bytes 1310752 | tf_op jit(solution)/shard_map/ppermute | solution.py:405
  303.6 4.1 fusion.18
  309.4 28.8 %collective-permute-done.18.g0.refs_10_ = bf16[512,1280]{1,0:T(8,128)(2,1)} collective-permute-done((bf16[512,1280]{1,0:T(8,128)(2,1)}, bf16[512,1280]{1,0:T(8,128)(2,1)}, u32[]{:S(2)}, u32[]{:S(2)}) %collective-permute-start.18) | collective-permute-done | bytes 1310752 | tf_op jit(solution)/shard_map/ppermute | solution.py:402
  338.3 11.8 %weight_grad.5.refs_2_ = bf16[1280,1280]{1,0:T(8,128)(2,1)} custom-call(bf16[512,1280]{1,0:T(8,128)(2,1)} %multiply_convert_fusion.x0.refs_0_, bf16[512,1280]{1,0:T(8,128)(2,1)} %collective-permute-done.12.x1.refs_1_, bf16[512,1280]{1,0:T(8,128)(2,1)} %collective-permute-done.6.x0.refs_2_, bf16[512,1280]{1,0:T(8,128)(2,1)} %copy-done.21, ...), custom_call_target="tpu_custom_call" | custom-call | flops 6710886400 | bytes 13762560 | tf_op jit(solution)/shard_map/weight_grad/pallas_call | solution.py:338
  350.0 2.7 constant_dynamic-slice_fusion
  354.5 11.7 %weight_grad.4.refs_1_ = bf16[1280,1280]{1,0:T(8,128)(2,1)} custom-call(bf16[512,1280]{1,0:T(8,128)(2,1)} %multiply_convert_fusion.x0.refs_0_, bf16[512,1280]{1,0:T(8,128)(2,1)} %collective-permute-done.12.x1.refs_1_, bf16[512,1280]{1,0:T(8,128)(2,1)} %collective-permute-done.6.x0.refs_2_, bf16[512,1280]{1,0:T(8,128)(2,1)} %copy-done.21, ...), custom_call_target="tpu_custom_call" | custom-call | flops 6710886400 | bytes 13762560 | tf_op jit(solution)/shard_map/weight_grad/pallas_call | solution.py:338
  367.5 17.3 %attn_bwd.2 = (bf16[1024,1536]{1,0:T(8,128)(2,1)}, bf16[512,1280]{1,0:T(8,128)(2,1)}, bf16[512,1280]{1,0:T(8,128)(2,1)}) custom-call(s32[16]{0:T(128)} %reshape.281.starts, bf16[512,1280]{1,0:T(8,128)(2,1)} %collective-permute-done.18.g0.refs_10_, bf16[512,1280]{1,0:T(8,128)(2,1)} %copy-done.22, bf16[1024,1536]{1,0:T(8,128)(2,1)} %get-tuple-element.49.qkv, ...), custom_call_target="tpu_custom_call" | custom-call | flops 6174015488 | bytes 16777216 | tf_op jit(solution)/shard_map/attn_bwd/pallas_call | solution.py:245
  386.8 11.8 %weight_grad.3.refs_0_ = bf16[1280,1280]{1,0:T(8,128)(2,1)} custom-call(bf16[1024,1280]{1,0:T(8,128)(2,1)} %get-tuple-element.55.refs_0_, bf16[1024,1280]{1,0:T(8,128)(2,1)} %get-tuple-element.56.refs_1_, bf16[512,1280]{1,0:T(8,128)(2,1)} %multiply_convert_fusion.2.y0.refs_2_, bf16[512,1280]{1,0:T(8,128)(2,1)} %collective-permute-done.13.y1.refs_3_, ...), custom_call_target="tpu_custom_call" | custom-call | flops 6710886400 | bytes 13762560 | tf_op jit(solution)/shard_map/weight_grad/pallas_call | solution.py:338
  398.7 17.5 %attn_bwd.3 = (bf16[1024,1536]{1,0:T(8,128)(2,1)}, bf16[512,1280]{1,0:T(8,128)(2,1)}, bf16[512,1280]{1,0:T(8,128)(2,1)}) custom-call(s32[16]{0:T(128)} %reshape.282.starts, bf16[512,1280]{1,0:T(8,128)(2,1)} %get-tuple-element.79.g0.refs_8_, bf16[512,1280]{1,0:T(8,128)(2,1)} %collective-permute-done.22.g1.refs_9_, bf16[1024,1536]{1,0:T(8,128)(2,1)} %get-tuple-element.52.qkv, ...), custom_call_target="tpu_custom_call" | custom-call | flops 6174015488 | bytes 16777216 | tf_op jit(solution)/shard_map/attn_bwd/pallas_call | solution.py:245
  422.8 32.4 %attn_weight_grad.1.refs_3_ = bf16[1280,1280]{1,0:T(8,128)(2,1)} custom-call(bf16[1024,1536]{1,0:T(8,128)(2,1)} %get-tuple-element.59.refs_0_, bf16[1024,1536]{1,0:T(8,128)(2,1)} %get-tuple-element.60.refs_1_, bf16[1024,512]{1,0:T(8,128)(2,1)} %get-tuple-element.61.refs_2_, bf16[1024,512]{1,0:T(8,128)(2,1)} %get-tuple-element.62.refs_3_, ...), custom_call_target="tpu_custom_call" | custom-call | flops 10737418240 | bytes 18874368 | tf_op jit(solution)/shard_map/attn_weight_grad/pallas_call | solution.py:374
  456.9 2.8 bitcast_reduce_fusion
  461.5 194.4 %sum_over_dp.1 = (bf16[2,2560,1280]{2,1,0:T(8,128)(2,1)}, f32[8,1280]{1,0:T(8,128)}) custom-call(bf16[1280,1280]{1,0:T(8,128)(2,1)} %weight_grad.3.refs_0_, bf16[1280,1280]{1,0:T(8,128)(2,1)} %weight_grad.4.refs_1_, bf16[1280,1280]{1,0:T(8,128)(2,1)} %weight_grad.5.refs_2_, bf16[1280,1280]{1,0:T(8,128)(2,1)} %attn_weight_grad.1.refs_3_, ...), custom_call_target="tpu_custom_call" | custom-call | bytes 600000000 | tf_op jit(solution)/shard_map/sum_over_dp/pallas_call | solution.py:665
  659.8 5.2 convert_multiply_fusion.1
  665.1 4.2 fusion.19
  672.5 6.0 convert_multiply_fusion
  (144 shorter events, 50.2 us)
Async XLA Ops:
  4.5 33.5 %copy-start.24 = (s32[32]{0:T(128)S(1)}, s32[32]{0:T(128)}, u32[]{:S(2)}) copy-start(s32[32]{0:T(128)} %param.15) | copy-start | bytes 388
  4.5 34.8 %copy-start.17 = (bf16[320,512]{1,0:T(8,128)(2,1)S(1)}, bf16[320,512]{1,0:T(8,128)(2,1)}, u32[]{:S(2)}) copy-start(bf16[320,512]{1,0:T(8,128)(2,1)} %constant.95.clone.refs_12_) | copy-start | bytes 983044
  6.0 36.7 %copy-start.16 = (bf16[320,512,1]{1,0,2:T(8,128)(2,1)S(1)}, bf16[320,512,1]{1,0,2:T(8,128)(2,1)}, u32[]{:S(2)}) copy-start(bf16[320,512,1]{1,0,2:T(8,128)(2,1)} %constant.97) | copy-start | bytes 983044
  6.0 32.1 %collective-permute-start = (bf16[512,1280]{1,0:T(8,128)(2,1)}, bf16[512,1280]{1,0:T(8,128)(2,1)}, u32[]{:S(2)}, u32[]{:S(2)}) collective-permute-start(bf16[512,1280]{1,0:T(8,128)(2,1)} %multiply_convert_fusion.1.x0.refs_4_), channel_id=1, source_target_pairs={{2,0},{3,1},{0,2},{1,3},{6,4},{7,5},{4,6},{5,7},{10,8},{11,9},{8,1... | collective-permute-start | bytes 3932168 | tf_op jit(solution)/shard_map/ppermute | solution.py:402
  8.9 57.2 %collective-permute-start.4 = (bf16[512,1280]{1,0:T(8,128)(2,1)}, bf16[512,1280]{1,0:T(8,128)(2,1)}, u32[]{:S(2)}, u32[]{:S(2)}) collective-permute-start(bf16[512,1280]{1,0:T(8,128)(2,1)} %multiply_convert_fusion.1.x0.refs_4_), channel_id=1, source_target_pairs={{0,1},{1,0},{2,3},{3,2},{4,5},{5,4},{6,7},{7,6},{8,9},{9,8},{10,11... | collective-permute-start | bytes 3932168 | tf_op jit(solution)/shard_map/ppermute | solution.py:399
  38.0 11.2 %collective-permute-start.1 = (bf16[512,1280]{1,0:T(8,128)(2,1)}, bf16[512,1280]{1,0:T(8,128)(2,1)}, u32[]{:S(2)}, u32[]{:S(2)}) collective-permute-start(bf16[512,1280]{1,0:T(8,128)(2,1)} %collective-permute-done.x0.refs_6_), channel_id=1, source_target_pairs={{0,1},{1,0},{2,3},{3,2},{4,5},{5,4},{6,7},{7,6},{8,9},{9,8},{10,11... | collective-permute-start | bytes 3932168 | tf_op jit(solution)/shard_map/ppermute | solution.py:399
  65.0 16.5 %collective-permute-start.2 = (bf16[512,1280]{1,0:T(8,128)(2,1)}, bf16[512,1280]{1,0:T(8,128)(2,1)}, u32[]{:S(2)}, u32[]{:S(2)}) collective-permute-start(bf16[512,1280]{1,0:T(8,128)(2,1)} %get-tuple-element.38), channel_id=1, source_target_pairs={{0,1},{1,0},{2,3},{3,2},{4,5},{5,4},{6,7},{7,6},{8,9},{9,8},{10,11... | collective-permute-start | bytes 3932168 | tf_op jit(solution)/shard_map/ppermute | solution.py:399
  81.5 8.0 %collective-permute-start.5 = (bf16[512,1280]{1,0:T(8,128)(2,1)}, bf16[512,1280]{1,0:T(8,128)(2,1)}, u32[]{:S(2)}, u32[]{:S(2)}) collective-permute-start(bf16[512,1280]{1,0:T(8,128)(2,1)} %get-tuple-element.40), channel_id=1, source_target_pairs={{0,1},{1,0},{2,3},{3,2},{4,5},{5,4},{6,7},{7,6},{8,9},{9,8},{10,11... | collective-permute-start | bytes 3932168 | tf_op jit(solution)/shard_map/ppermute | solution.py:399
  84.3 31.9 %collective-permute-start.3 = (bf16[512,1280]{1,0:T(8,128)(2,1)}, bf16[512,1280]{1,0:T(8,128)(2,1)}, u32[]{:S(2)}, u32[]{:S(2)}) collective-permute-start(bf16[512,1280]{1,0:T(8,128)(2,1)} %add_convert_fusion.3), channel_id=1, source_target_pairs={{0,2},{1,3},{2,0},{3,1},{4,6},{5,7},{6,4},{7,5},{8,10},{9,11},{10,... | collective-permute-start | bytes 3932168 | tf_op jit(solution)/shard_map/ppermute | solution.py:405
  89.2 55.0 %collective-permute-start.8 = (bf16[512,1280]{1,0:T(8,128)(2,1)}, bf16[512,1280]{1,0:T(8,128)(2,1)}, u32[]{:S(2)}, u32[]{:S(2)}) collective-permute-start(bf16[512,1280]{1,0:T(8,128)(2,1)} %multiply_convert_fusion.2.y0.refs_2_), channel_id=1, source_target_pairs={{2,0},{3,1},{0,2},{1,3},{6,4},{7,5},{4,6},{5,7},{10,8},{11,9},{8,1... | collective-permute-start | bytes 3932168 | tf_op jit(solution)/shard_map/ppermute | solution.py:402
  121.5 50.4 %collective-permute-start.6 = (bf16[512,1280]{1,0:T(8,128)(2,1)}, bf16[512,1280]{1,0:T(8,128)(2,1)}, u32[]{:S(2)}, u32[]{:S(2)}) collective-permute-start(bf16[512,1280]{1,0:T(8,128)(2,1)} %multiply_convert_fusion.x0.refs_0_), channel_id=1, source_target_pairs={{2,0},{3,1},{0,2},{1,3},{6,4},{7,5},{4,6},{5,7},{10,8},{11,9},{8,1... | collective-permute-start | bytes 3932168 | tf_op jit(solution)/shard_map/ppermute | solution.py:402
  123.3 87.5 %collective-permute-start.13 = (bf16[512,1280]{1,0:T(8,128)(2,1)}, bf16[512,1280]{1,0:T(8,128)(2,1)}, u32[]{:S(2)}, u32[]{:S(2)}) collective-permute-start(bf16[512,1280]{1,0:T(8,128)(2,1)} %multiply_convert_fusion.2.y0.refs_2_), channel_id=1, source_target_pairs={{0,1},{1,0},{2,3},{3,2},{4,5},{5,4},{6,7},{7,6},{8,9},{9,8},{10,11... | collective-permute-start | bytes 3932168 | tf_op jit(solution)/shard_map/ppermute | solution.py:399
  131.4 40.5 %copy-start.3 = (bf16[2,1280,1280]{2,1,0:T(8,128)(2,1)S(1)}, bf16[2,1280,1280]{2,1,0:T(8,128)(2,1)}, u32[]{:S(2)}) copy-start(bf16[2,1280,1280]{2,1,0:T(8,128)(2,1)} %convert.5) | copy-start | bytes 19660804
  144.2 31.3 %collective-permute-start.9 = (bf16[512,1280]{1,0:T(8,128)(2,1)}, bf16[512,1280]{1,0:T(8,128)(2,1)S(1)}, u32[]{:S(2)}, u32[]{:S(2)}) collective-permute-start(bf16[512,1280]{1,0:T(8,128)(2,1)} %collective-permute-done.8.y0.refs_4_), channel_id=1, source_target_pairs={{0,1},{1,0},{2,3},{3,2},{4,5},{5,4},{6,7},{7,6},{8,9},{9,8},{10,11... | collective-permute-start | bytes 3932168 | tf_op jit(solution)/shard_map/ppermute | solution.py:399
  171.9 3.7 collective-permute-start.7
  175.1 35.8 %collective-permute-start.12 = (bf16[512,1280]{1,0:T(8,128)(2,1)}, bf16[512,1280]{1,0:T(8,128)(2,1)}, u32[]{:S(2)}, u32[]{:S(2)}) collective-permute-start(bf16[512,1280]{1,0:T(8,128)(2,1)} %multiply_convert_fusion.x0.refs_0_), channel_id=1, source_target_pairs={{0,1},{1,0},{2,3},{3,2},{4,5},{5,4},{6,7},{7,6},{8,9},{9,8},{10,11... | collective-permute-start | bytes 3932168 | tf_op jit(solution)/shard_map/ppermute | solution.py:399
  210.2 36.1 %collective-permute-start.10 = (bf16[512,1280]{1,0:T(8,128)(2,1)}, bf16[512,1280]{1,0:T(8,128)(2,1)S(1)}, u32[]{:S(2)}, u32[]{:S(2)}) collective-permute-start(bf16[512,1280]{1,0:T(8,128)(2,1)} %get-tuple-element.42), channel_id=1, source_target_pairs={{0,1},{1,0},{2,3},{3,2},{4,5},{5,4},{6,7},{7,6},{8,9},{9,8},{10,11... | collective-permute-start | bytes 3932168 | tf_op jit(solution)/shard_map/ppermute | solution.py:399
  210.3 33.8 %copy-start.12 = (bf16[512,1280]{1,0:T(8,128)(2,1)S(1)}, bf16[512,1280]{1,0:T(8,128)(2,1)}, u32[]{:S(2)}) copy-start(bf16[512,1280]{1,0:T(8,128)(2,1)} %get-tuple-element.45) | copy-start | bytes 3932164
  210.3 33.8 %collective-permute-start.15 = (bf16[512,1280]{1,0:T(8,128)(2,1)}, bf16[512,1280]{1,0:T(8,128)(2,1)S(1)}, u32[]{:S(2)}, u32[]{:S(2)}) collective-permute-start(bf16[512,1280]{1,0:T(8,128)(2,1)} %get-tuple-element.46), channel_id=1, source_target_pairs={{0,1},{1,0},{2,3},{3,2},{4,5},{5,4},{6,7},{7,6},{8,9},{9,8},{10,11... | collective-permute-start | bytes 3932168 | tf_op jit(solution)/shard_map/ppermute | solution.py:399
  243.9 3.9 collective-permute-start.17
  244.4 31.7 %collective-permute-start.16 = (bf16[512,1280]{1,0:T(8,128)(2,1)S(1)}, bf16[512,1280]{1,0:T(8,128)(2,1)S(1)}, u32[]{:S(2)}, u32[]{:S(2)}) collective-permute-start(bf16[512,1280]{1,0:T(8,128)(2,1)S(1)} %add_convert_fusion.1), channel_id=1, source_target_pairs={{0,2},{1,3},{2,0},{3,1},{4,6},{5,7},{6,4},{7,5},{8,10},{9,11},{10,... | collective-permute-start | bytes 3932168 | tf_op jit(solution)/shard_map/ppermute | solution.py:405
  246.2 31.0 %collective-permute-start.14 = (bf16[512,1280]{1,0:T(8,128)(2,1)S(1)}, bf16[512,1280]{1,0:T(8,128)(2,1)S(1)}, u32[]{:S(2)}, u32[]{:S(2)}) collective-permute-start(bf16[512,1280]{1,0:T(8,128)(2,1)S(1)} %copy-done.23), channel_id=1, source_target_pairs={{0,1},{1,0},{2,3},{3,2},{4,5},{5,4},{6,7},{7,6},{8,9},{9,8},{10,11... | collective-permute-start | bytes 3932168 | tf_op jit(solution)/shard_map/ppermute | solution.py:399
  246.7 56.9 %collective-permute-start.11 = (bf16[512,1280]{1,0:T(8,128)(2,1)S(1)}, bf16[512,1280]{1,0:T(8,128)(2,1)S(1)}, u32[]{:S(2)}, u32[]{:S(2)}) collective-permute-start(bf16[512,1280]{1,0:T(8,128)(2,1)S(1)} %add_convert_fusion.2), channel_id=1, source_target_pairs={{0,2},{1,3},{2,0},{3,1},{4,6},{5,7},{6,4},{7,5},{8,10},{9,11},{10,... | collective-permute-start | bytes 3932168 | tf_op jit(solution)/shard_map/ppermute | solution.py:405
  307.7 30.5 %collective-permute-start.18 = (bf16[512,1280]{1,0:T(8,128)(2,1)}, bf16[512,1280]{1,0:T(8,128)(2,1)}, u32[]{:S(2)}, u32[]{:S(2)}) collective-permute-start(bf16[512,1280]{1,0:T(8,128)(2,1)} %get-tuple-element.79.g0.refs_8_), channel_id=1, source_target_pairs={{2,0},{3,1},{0,2},{1,3},{6,4},{7,5},{4,6},{5,7},{10,8},{11,9},{8,1... | collective-permute-start | bytes 3932168 | tf_op jit(solution)/shard_map/ppermute | solution.py:402
  338.2 28.2 %collective-permute-start.19 = (bf16[512,1280]{1,0:T(8,128)(2,1)}, bf16[512,1280]{1,0:T(8,128)(2,1)S(1)}, u32[]{:S(2)}, u32[]{:S(2)}) collective-permute-start(bf16[512,1280]{1,0:T(8,128)(2,1)} %collective-permute-done.18.g0.refs_10_), channel_id=1, source_target_pairs={{0,1},{1,0},{2,3},{3,2},{4,5},{5,4},{6,7},{7,6},{8,9},{9,8},{10,11... | collective-permute-start | bytes 3932168 | tf_op jit(solution)/shard_map/ppermute | solution.py:399
  352.8 108.5 %collective-permute-start.26 = (bf16[640,1280]{1,0:T(8,128)(2,1)}, bf16[640,1280]{1,0:T(8,128)(2,1)}, u32[]{:S(2)}, u32[]{:S(2)}) collective-permute-start(bf16[640,1280]{1,0:T(8,128)(2,1)} %constant_dynamic-slice_fusion), channel_id=1, source_target_pairs={{0,4},{4,0},{8,12},{12,8},{16,20},{20,16},{24,28},{28,24},{1,5},{5... | collective-permute-start | bytes 4915208 | tf_op jit(solution)/shard_map/ppermute | solution.py:652
  366.2 32.4 %collective-permute-start.22 = (bf16[512,1280]{1,0:T(8,128)(2,1)}, bf16[512,1280]{1,0:T(8,128)(2,1)}, u32[]{:S(2)}, u32[]{:S(2)}) collective-permute-start(bf16[512,1280]{1,0:T(8,128)(2,1)} %get-tuple-element.79.g0.refs_8_), channel_id=1, source_target_pairs={{0,1},{1,0},{2,3},{3,2},{4,5},{5,4},{6,7},{7,6},{8,9},{9,8},{10,11... | collective-permute-start | bytes 3932168 | tf_op jit(solution)/shard_map/ppermute | solution.py:399
  384.9 31.4 %collective-permute-start.20 = (bf16[512,1280]{1,0:T(8,128)(2,1)}, bf16[512,1280]{1,0:T(8,128)(2,1)S(1)}, u32[]{:S(2)}, u32[]{:S(2)}) collective-permute-start(bf16[512,1280]{1,0:T(8,128)(2,1)} %get-tuple-element.51), channel_id=1, source_target_pairs={{0,1},{1,0},{2,3},{3,2},{4,5},{5,4},{6,7},{7,6},{8,9},{9,8},{10,11... | collective-permute-start | bytes 3932168 | tf_op jit(solution)/shard_map/ppermute | solution.py:399
  386.5 74.7 %collective-permute-start.25 = (bf16[640,1280]{1,0:T(8,128)(2,1)}, bf16[640,1280]{1,0:T(8,128)(2,1)}, u32[]{:S(2)}, u32[]{:S(2)}) collective-permute-start(bf16[640,1280]{1,0:T(8,128)(2,1)} %constant_dynamic-slice_fusion.1), channel_id=1, source_target_pairs={{0,4},{4,0},{8,12},{12,8},{16,20},{20,16},{24,28},{28,24},{1,5},{5... | collective-permute-start | bytes 4915208 | tf_op jit(solution)/shard_map/ppermute | solution.py:652
  416.2 39.0 %collective-permute-start.23 = (bf16[512,1280]{1,0:T(8,128)(2,1)}, bf16[512,1280]{1,0:T(8,128)(2,1)S(1)}, u32[]{:S(2)}, u32[]{:S(2)}) collective-permute-start(bf16[512,1280]{1,0:T(8,128)(2,1)} %get-tuple-element.54), channel_id=1, source_target_pairs={{0,1},{1,0},{2,3},{3,2},{4,5},{5,4},{6,7},{7,6},{8,9},{9,8},{10,11... | collective-permute-start | bytes 3932168 | tf_op jit(solution)/shard_map/ppermute | solution.py:399
  417.6 37.5 %collective-permute-start.21 = (bf16[512,1280]{1,0:T(8,128)(2,1)}, bf16[512,1280]{1,0:T(8,128)(2,1)S(1)}, u32[]{:S(2)}, u32[]{:S(2)}) collective-permute-start(bf16[512,1280]{1,0:T(8,128)(2,1)} %add_convert_fusion), channel_id=1, source_target_pairs={{0,2},{1,3},{2,0},{3,1},{4,6},{5,7},{6,4},{7,5},{8,10},{9,11},{10,... | collective-permute-start | bytes 3932168 | tf_op jit(solution)/shard_map/ppermute | solution.py:405
  420.6 40.9 %collective-permute-start.24 = (bf16[640,1280]{1,0:T(8,128)(2,1)}, bf16[640,1280]{1,0:T(8,128)(2,1)}, u32[]{:S(2)}, u32[]{:S(2)}) collective-permute-start(bf16[640,1280]{1,0:T(8,128)(2,1)} %constant_dynamic-slice_fusion.2), channel_id=1, source_target_pairs={{0,4},{4,0},{8,12},{12,8},{16,20},{20,16},{24,28},{28,24},{1,5},{5... | collective-permute-start | bytes 4915208 | tf_op jit(solution)/shard_map/ppermute | solution.py:652
  (20 other events, 258.3 us)

commit v2 on v1

--- a/solution.py
+++ b/solution.py
@@ -13,6 +13,7 @@
 LANES = 128
 NFREQ = 3
 SEQ = 64
+BLOCK = 256
 PAIR = 128
 
 EPSILON = 1e-06
@@ -20,7 +21,8 @@
 HIGHEST = lax.Precision.HIGHEST
 LOW = jnp.bfloat16
 F32 = jnp.float32
-VMEM_LIMIT = 56 * 1024 * 1024
+VMEM_LIMIT = 60 * 1024 * 1024
+MESH = pl.DeviceIdType.MESH
 LN2 = float(np.log(2.0))
 QSCALE = float(HS**-0.5 / np.log(2.0))
 
@@ -75,107 +77,530 @@
     return exponent * (1.0 / jnp.sum(exponent, 0, keepdims=True))
 
 
-def pick(first, xs, a, b):
-    @pl.when(first)
-    def _():
-        xs[...] = a[...]
-
-    @pl.when(jnp.logical_not(first))
-    def _():
-        xs[...] = b[...]
-
-
-def put(first, a, b, value):
-    @pl.when(first)
-    def _():
-        a[...] = value
-
-    @pl.when(jnp.logical_not(first))
-    def _():
-        b[...] = value
-
-
-def attn_fwd_kernel(nh, starts, x0, x1, wqkv, wout, cp, sp, qkv, mixed, part0, part1, xs):
-    step = pl.program_id(0)
-    first = step < pl.num_programs(0) // 2
+class Links:
+    def __init__(self, chips, blocks, rb):
+        self.chips, self.blocks, self.rb = chips, blocks, rb
+        self.n = 2 * chips
+        self.dp, self.mp = lax.axis_index("dp"), lax.axis_index("mp")
+        self.core = (self.dp, self.mp + 1 - 2 * lax.rem(self.mp, 2))
+
+    def further(self, k):
+        return (self.dp, lax.rem(self.mp + 2 * k, self.n))
+
+    def nearer(self, k):
+        return (self.dp, lax.rem(self.mp + 2 * (self.chips - k), self.n))
+
+    def greet(self):
+        barrier = pltpu.get_barrier_semaphore()
+        for j in range(1, self.n):
+            other = (self.dp, lax.rem(self.mp + j, self.n))
+            pl.semaphore_signal(barrier, inc=1, device_id=other, device_id_type=MESH)
+        pl.semaphore_wait(barrier, self.n - 1)
+
+    def rows(self, b):
+        return pl.ds(b * self.rb, self.rb)
+
+    def each(self, body):
+        def one(q, carry):
+            body(q // self.blocks, lax.rem(q, self.blocks))
+            return carry
+
+        lax.fori_loop(0, self.chips * self.blocks, one, 0)
+
+
+def remote(src, dst, send, recv, device):
+    return pltpu.make_async_remote_copy(
+        src_ref=src, dst_ref=dst, send_sem=send, recv_sem=recv, device_id=device, device_id_type=MESH
+    )
+
+
+class Gather:
+    def __init__(self, links, x, buf, local, core_send, core_recv, chip_send, chip_recv):
+        self.links, self.x, self.buf, self.local = links, x, buf, local
+        self.core_send, self.core_recv = core_send, core_recv
+        self.chip_send, self.chip_recv = chip_send, chip_recv
+
+    def own(self, b):
+        rows = self.links.rows(b)
+        return pltpu.make_async_copy(self.x.at[rows], self.buf.at[0, 0, rows], self.local.at[b])
+
+    def to_chip(self, k, b):
+        rows = self.links.rows(b)
+        return remote(
+            self.x.at[rows], self.buf.at[k, 0, rows], self.chip_send.at[k, b], self.chip_recv.at[k, b],
+            self.links.nearer(k),
+        )
+
+    def to_core(self, k, b):
+        rows = self.links.rows(b)
+        return remote(
+            self.buf.at[k, 0, rows], self.buf.at[k, 1, rows], self.core_send.at[k, b], self.core_recv.at[k, b],
+            self.links.core,
+        )
+
+    def own_to_core(self, b):
+        rows = self.links.rows(b)
+        return remote(
+            self.x.at[rows], self.buf.at[0, 1, rows], self.core_send.at[0, b], self.core_recv.at[0, b],
+            self.links.core,
+        )
+
+    def start_near(self):
+        for b in range(self.links.blocks):
+            self.own(b).start()
+            self.own_to_core(b).start()
+
+    def start_far(self, b):
+        for k in range(1, self.links.chips):
+            self.to_chip(k, b).start()
+
+    def arrive(self, k, b, second):
+        @pl.when(jnp.logical_and(jnp.logical_not(second), k == 0))
+        def _():
+            self.own(b).wait()
+
+        @pl.when(jnp.logical_and(jnp.logical_not(second), k > 0))
+        def _():
+            self.to_chip(k, b).wait_recv()
+            self.to_core(k, b).start()
+
+        @pl.when(second)
+        def _():
+            self.to_core(k, b).wait_recv()
+
+    def finish(self):
+        def sent(k, b):
+            self.to_core(k, b).wait_send()
+
+            @pl.when(k > 0)
+            def _():
+                self.to_chip(k, b).wait_send()
+
+        self.links.each(sent)
+
+    @staticmethod
+    def scratch(chips, blocks):
+        return [pltpu.SemaphoreType.DMA((blocks,))] + [pltpu.SemaphoreType.DMA((chips, blocks))] * 4
+
+
+class Scatter:
+    def __init__(self, links, give, keep, got, far, core_send, core_recv, chip_send, chip_recv):
+        self.links, self.give, self.keep, self.got, self.far = links, give, keep, got, far
+        self.core_send, self.core_recv = core_send, core_recv
+        self.chip_send, self.chip_recv = chip_send, chip_recv
+
+    def to_core(self, k, b):
+        rows = self.links.rows(b)
+        return remote(
+            self.give.at[k, rows], self.got.at[k, rows], self.core_send.at[k, b], self.core_recv.at[k, b],
+            self.links.core,
+        )
+
+    def to_chip(self, k, b):
+        rows = self.links.rows(b)
+        return remote(
+            self.keep.at[k, rows], self.far.at[k, rows], self.chip_send.at[k, b], self.chip_recv.at[k, b],
+            self.links.further(k),
+        )
+
+    def put(self, k, b, second, value):
+        rows = self.links.rows(b)
+
+        @pl.when(jnp.logical_not(second))
+        def _():
+            self.keep[k, rows] = value.astype(LOW)
+
+        @pl.when(second)
+        def _():
+            self.give[k, rows] = value.astype(LOW)
+            self.to_core(k, b).start()
+
+    def pair_done(self, k, b):
+        rows = self.links.rows(b)
+        self.to_core(k, b).wait_recv()
+
+        @pl.when(k > 0)
+        def _():
+            self.keep[k, rows] = (self.keep[k, rows].astype(F32) + self.got[k, rows].astype(F32)).astype(LOW)
+            self.to_chip(k, b).start()
+
+    def total(self, b):
+        rows = self.links.rows(b)
+        value = self.keep[0, rows].astype(F32) + self.got[0, rows].astype(F32)
+        for k in range(1, self.links.chips):
+            self.to_chip(k, b).wait_recv()
+            value += self.far[k, rows].astype(F32)
+        return value
+
+    def finish(self):
+        def sent(k, b):
+            self.to_core(k, b).wait_send()
+
+            @pl.when(k > 0)
+            def _():
+                self.to_chip(k, b).wait_send()
+
+        self.links.each(sent)
+
+    @staticmethod
+    def scratch(chips, blocks, rows, width):
+        return [pltpu.VMEM((chips, rows, width), LOW)] * 4 + [pltpu.SemaphoreType.DMA((chips, blocks))] * 4
+
+
+def run_blocks(links, arrive, compute, scatters):
+    def step(i, carry):
+        q, second = i // 2, lax.rem(i, 2) == 1
+        k, b = q // links.blocks, lax.rem(q, links.blocks)
+        arrive(i, k, b, second)
+        for scatter, value in zip(scatters, compute(i, k, b, second)):
+            scatter.put(k, b, second, value)
+
+        @pl.when(jnp.logical_and(jnp.logical_not(second), q > 0))
+        def _():
+            for scatter in scatters:
+                scatter.pair_done((q - 1) // links.blocks, lax.rem(q - 1, links.blocks))
+
+        return carry
+
+    pairs = links.chips * links.blocks
+    lax.fori_loop(0, 2 * pairs, step, 0)
+    for scatter in scatters:
+        scatter.pair_done(links.chips - 1, links.blocks - 1)
+
+
+class Store:
+    def __init__(self, sems, pairs):
+        self.sems, self.pairs = sems, pairs
+
+    def copies(self, i):
+        return [pltpu.make_async_copy(a, b, self.sems.at[i, j]) for j, (a, b) in enumerate(self.pairs(i))]
+
+    def start(self, i):
+        for copy in self.copies(i):
+            copy.start()
+
+    def wait(self, i):
+        for copy in self.copies(i):
+            copy.wait()
+
+
+def loader(sems, pairs):
+    copies = [pltpu.make_async_copy(a, b, sems.at[i]) for i, (a, b) in enumerate(pairs)]
+    for copy in copies:
+        copy.start()
+    return copies
+
+
+def row_block(links, i, k, b, second):
+    at = (2 * k + second.astype(jnp.int32)) * (links.blocks * links.rb) + b * links.rb
+    return pl.multiple_of(at, links.rb)
+
+
+def attn_fwd_kernel(nh, chips, blocks, rb, x, start, gain, wqkv_any, wout_any, starts, cp, sp, *refs):
+    qkv_out, mixed_out, xg_out, after, normed, refs = *refs[:5], refs[5:]
+    xg, wqkv, wout, qkv, mixed, begin, load, store_sems, refs = *refs[:8], refs[8:]
+    gather_refs, scatter_refs = refs[:5], refs[5:]
+    links = Links(chips, blocks, rb)
+    loads = loader(load, [(wqkv_any, wqkv), (wout_any, wout), (start, begin)])
+    links.greet()
+    gather = Gather(links, x, xg, *gather_refs)
+    scatter = Scatter(links, *scatter_refs)
+    gather.start_near()
+    for b in range(blocks):
+        gather.start_far(b)
+    loads[0].wait()
+    loads[1].wait()
     width = nh * LANES
-    rb = xs.shape[0]
-    pick(first, xs, x0, x1)
-    c, s = row_angles(cp, sp, starts, step * (rb // SEQ), rb // SEQ)
-    for part in range(3):
-        proj = dot(xs[...], wqkv[part])
-        if part == 2:
-            qkv[:, 2 * width :] = proj.astype(LOW)
-            continue
-        scale = QSCALE if part == 0 else 1.0
-        cc, ss = c * scale, s * scale
-        for h in range(nh):
-            p = proj[:, h * LANES : (h + 1) * LANES]
-            at = slice(part * width + h * LANES, part * width + (h + 1) * LANES)
-            qkv[:, at] = (p * cc + pltpu.roll(p, LANES // 2, 1) * ss).astype(LOW)
-    for b in range(rb // PAIR):
-        rows = slice(b * PAIR, (b + 1) * PAIR)
-        mask = pair_mask(starts, step * (rb // SEQ) + 2 * b)
-        get = lambda part, h: qkv[rows, part * width + h * LANES : part * width + (h + 1) * LANES]
-        scores = [dot(get(1, h), get(0, h), 1, 1) + mask for h in range(nh)]
-        attention = [softmax_down(v).astype(LOW) for v in scores]
-        for h in range(nh):
-            mixed[rows, h * LANES : (h + 1) * LANES] = dot(attention[h], get(2, h), 0, 0).astype(LOW)
-    put(first, part0, part1, dot(mixed[...], wout[...]).astype(LOW))
-
-
-def attn_bwd_kernel(nh, starts, g0, g1, qkv, wqkv, wout, cp, sp, gproj, part0, part1, gs, gmix):
-    step = pl.program_id(0)
-    first = step < pl.num_programs(0) // 2
+    series = rb // SEQ
+
+    def places(i):
+        q, second = i // 2, lax.rem(i, 2) == 1
+        k, b = q // blocks, lax.rem(q, blocks)
+        return k, b, lax.rem(i, 2), row_block(links, i, k, b, second)
+
+    def pairs(i):
+        k, b, s, at = places(i)
+        rows = pl.ds(at, rb)
+        return [
+            (qkv.at[rows], qkv_out.at[rows]),
+            (mixed.at[rows], mixed_out.at[rows]),
+            (xg.at[k, s, links.rows(b)], xg_out.at[k, s, links.rows(b)]),
+        ]
+
+    store = Store(store_sems, pairs)
+
+    def compute(i, k, b, second):
+        s = second.astype(jnp.int32)
+        at = row_block(links, i, k, b, second)
+        rows = pl.ds(at, rb)
+        xs = xg[k, s, links.rows(b)]
+        first = at // SEQ
+        c, sn = row_angles(cp, sp, starts, first, series)
+        for part in range(3):
+            proj = dot(xs, wqkv[part])
+            if part == 2:
+                qkv[rows, 2 * width :] = proj.astype(LOW)
+                continue
+            scale = QSCALE if part == 0 else 1.0
+            cc, ss = c * scale, sn * scale
+            for h in range(nh):
+                p = proj[:, h * LANES : (h + 1) * LANES]
+                cols = slice(part * width + h * LANES, part * width + (h + 1) * LANES)
+                qkv[rows, cols] = (p * cc + pltpu.roll(p, LANES // 2, 1) * ss).astype(LOW)
+        for p in range(rb // PAIR):
+            sub = pl.ds(pl.multiple_of(at + p * PAIR, PAIR), PAIR)
+            mask = pair_mask(starts, first + 2 * p)
+            get = lambda part, h: qkv[sub, part * width + h * LANES : part * width + (h + 1) * LANES]
+            scores = [dot(get(1, h), get(0, h), 1, 1) + mask for h in range(nh)]
+            attention = [softmax_down(v).astype(LOW) for v in scores]
+            for h in range(nh):
+                mixed[sub, h * LANES : (h + 1) * LANES] = dot(attention[h], get(2, h), 0, 0).astype(LOW)
+        part = dot(mixed[rows], wout[...])
+        store.start(i)
+        return [part]
+
+    run_blocks(links, lambda i, k, b, second: gather.arrive(k, b, second), compute, [scatter])
+    loads[2].wait()
+
+    def last(b, carry):
+        rows = pl.ds(pl.multiple_of(b * rb, rb), rb)
+        value = begin[rows] + scatter.total(b)
+        after[rows] = value
+        inverse = lax.rsqrt(jnp.mean(value * value, -1, keepdims=True) + EPSILON)
+        normed[rows] = (value * inverse * gain[...]).astype(LOW)
+        return carry
+
+    lax.fori_loop(0, blocks, last, 0)
+    gather.finish()
+    scatter.finish()
+
+    def stored(i, carry):
+        store.wait(i)
+        return carry
+
+    lax.fori_loop(0, 2 * chips * blocks, stored, 0)
+
+
+def norm_backward_block(value, gain, grad_normed, before):
+    inverse = lax.rsqrt(jnp.mean(value * value, -1, keepdims=True) + EPSILON)
+    normal = value * inverse
+    scaled = grad_normed * gain
+    grad = before + inverse * (scaled - normal * jnp.mean(scaled * normal, -1, keepdims=True))
+    return grad, jnp.sum(grad_normed * normal, 0, keepdims=True)
+
+
+def mlp_kernel(chips, blocks, rb, x, gy, after, grad_in, gain, wgate_any, wup_any, wdown_any, *refs):
+    hidden_out, gpre_out, xg_out, yg_out, own_out, far_out, grad_after, low_after, gain_grad, refs = *refs[:9], refs[9:]
+    xg, yg, wgate, wup, wdown, hidden, gpre, begin, before, load, store_sems, down_sems, refs = *refs[:12], refs[12:]
+    xg_refs, yg_refs, back_refs = refs[:5], refs[5:10], refs[10:18]
+    give, keep, got, down_send, down_recv = refs[18:]
+    links = Links(chips, blocks, rb)
+    loads = loader(load, [(wgate_any, wgate), (wup_any, wup), (wdown_any, wdown), (after, begin), (grad_in, before)])
+    links.greet()
+    gather = Gather(links, x, xg, *xg_refs)
+    second_gather = Gather(links, gy, yg, *yg_refs)
+    back = Scatter(links, *back_refs)
+    gather.start_near()
+    second_gather.start_near()
+    for b in range(blocks):
+        gather.start_far(b)
+
+    def down_to_core(k, b):
+        rows = links.rows(b)
+        return remote(
+            give.at[k, rows], got.at[k, rows], down_send.at[k, b], down_recv.at[k, b], links.core
+        )
+
+    def pairs(i):
+        q, second = i // 2, lax.rem(i, 2) == 1
+        k, b, s = q // blocks, lax.rem(q, blocks), lax.rem(i, 2)
+        rows = pl.ds(row_block(links, i, k, b, second), rb)
+        slot = lax.rem(i, 2)
+        return [
+            (hidden.at[slot], hidden_out.at[rows]),
+            (gpre.at[slot, 0], gpre_out.at[0, rows]),
+            (gpre.at[slot, 1], gpre_out.at[1, rows]),
+            (xg.at[k, s, links.rows(b)], xg_out.at[k, s, links.rows(b)]),
+            (yg.at[k, s, links.rows(b)], yg_out.at[k, s, links.rows(b)]),
+        ]
+
+    store = Store(store_sems, pairs)
+    steps = 2 * chips * blocks
+
+    def arrive(i, k, b, second):
+        for j in range(blocks):
+
+            @pl.when(i == min(blocks + j, 2 * blocks - 1))
+            def _(j=j):
+                second_gather.start_far(j)
+
+        gather.arrive(k, b, second)
+
+        @pl.when(i == 0)
+        def _():
+            loads[0].wait()
+            loads[1].wait()
+            loads[2].wait()
+
+    def compute(i, k, b, second):
+        s = second.astype(jnp.int32)
+        slot = lax.rem(i, 2)
+
+        @pl.when(i >= 2)
+        def _():
+            store.wait(i - 2)
+
+        xs = xg[k, s, links.rows(b)]
+        gate = dot(xs, wgate[...])
+        sig = jax.nn.sigmoid(gate)
+        act = gate * sig
+        slope = sig * (1.0 + gate * (1.0 - sig))
+        up = dot(xs, wup[...])
+        hidden[slot] = (act * up).astype(LOW)
+        second_gather.arrive(k, b, second)
+        gh = dot(yg[k, s, links.rows(b)], wdown[...], 1, 1)
+        gpre[slot, 0] = (gh * up * slope).astype(LOW)
+        gpre[slot, 1] = (gh * act).astype(LOW)
+        grad = dot(gpre[slot, 0], wgate[...], 1, 1) + dot(gpre[slot, 1], wup[...], 1, 1)
+        down = dot(hidden[slot], wdown[...]).astype(LOW)
+        rows = links.rows(b)
+
+        @pl.when(jnp.logical_not(second))
+        def _():
+            keep[k, rows] = down
+
+        @pl.when(second)
+        def _():
+            give[k, rows] = down
+            down_to_core(k, b).start()
+
+        store.start(i)
+        return [grad]
+
+    run_blocks(links, arrive, compute, [back])
+
+    def down_sum(k, b):
+        rows = links.rows(b)
+        down_to_core(k, b).wait_recv()
+        keep[k, rows] = (keep[k, rows].astype(F32) + got[k, rows].astype(F32)).astype(LOW)
+
+    links.each(down_sum)
+    outs = [pltpu.make_async_copy(keep.at[0], own_out, down_sems.at[0])]
+    for k in range(1, chips):
+        outs.append(pltpu.make_async_copy(keep.at[k], far_out.at[k - 1], down_sems.at[k]))
+    for copy in outs:
+        copy.start()
+    loads[3].wait()
+    loads[4].wait()
+    gain_grad[...] = jnp.zeros_like(gain_grad)
+
+    def last(b, carry):
+        rows = pl.ds(pl.multiple_of(b * rb, rb), rb)
+        grad, gains = norm_backward_block(begin[rows], gain[...], back.total(b), before[rows])
+        grad_after[rows] = grad
+        low_after[rows] = grad.astype(LOW)
+        gain_grad[0:1] += gains
+        return carry
+
+    lax.fori_loop(0, blocks, last, 0)
+    gather.finish()
+    second_gather.finish()
+    back.finish()
+    links.each(lambda k, b: down_to_core(k, b).wait_send())
+    for copy in outs:
+        copy.wait()
+    store.wait(steps - 2)
+    store.wait(steps - 1)
+
+
+def attn_bwd_kernel(nh, chips, blocks, rb, x, start, grad_in, gain, qkv_any, wqkv_any, wout_any, starts, cp, sp, *refs):
+    gproj_out, xg_out, grad_rows, gain_grad, refs = *refs[:4], refs[4:]
+    xg, wqkv, wout, qkv, gproj, gmix, begin, before, load, store_sems, refs = *refs[:10], refs[10:]
+    gather_refs, scatter_refs = refs[:5], refs[5:]
+    links = Links(chips, blocks, rb)
+    loads = loader(
+        load, [(wout_any, wout), (qkv_any, qkv), (wqkv_any, wqkv), (start, begin), (grad_in, before)]
+    )
+    links.greet()
+    gather = Gather(links, x, xg, *gather_refs)
+    scatter = Scatter(links, *scatter_refs)
+    gather.start_near()
+    for b in range(blocks):
+        gather.start_far(b)
+    for copy in loads[:3]:
+        copy.wait()
     width = nh * LANES
-    rb = gs.shape[0]
-    pick(first, gs, g0, g1)
-    gmix[...] = dot(gs[...], wout[...], 1, 1).astype(LOW)
-    c, s = row_angles(cp, sp, starts, step * (rb // SEQ), rb // SEQ)
-    qc, qs = c * HS ** (-0.5), s * HS ** (-0.5)
-    kc, ks = c * LN2, s * LN2
-    for b in range(rb // PAIR):
-        rows = slice(b * PAIR, (b + 1) * PAIR)
-        mask = pair_mask(starts, step * (rb // SEQ) + 2 * b)
-        at = lambda part, h: slice(part * width + h * LANES, part * width + (h + 1) * LANES)
-        heads = range(nh)
-        gm = [gmix[rows, at(0, h)] for h in heads]
-        scores = [dot(qkv[rows, at(1, h)], qkv[rows, at(0, h)], 1, 1) + mask for h in heads]
-        grads = [dot(qkv[rows, at(2, h)], gm[h], 1, 1) for h in heads]
-        attention = [softmax_down(v) for v in scores]
-        for h in heads:
-            gproj[rows, at(2, h)] = dot(attention[h].astype(LOW), gm[h]).astype(LOW)
-        low = []
-        for h in heads:
-            both = attention[h] * grads[h]
-            low.append((both - attention[h] * jnp.sum(both, 0, keepdims=True)).astype(LOW))
-        for h in heads:
-            gk = dot(low[h], qkv[rows, at(0, h)])
-            gproj[rows, at(1, h)] = (gk * kc[rows] - pltpu.roll(gk, LANES // 2, 1) * ks[rows]).astype(LOW)
-        for h in heads:
-            gq = dot(low[h], qkv[rows, at(1, h)], 0, 0)
-            gproj[rows, at(0, h)] = (gq * qc[rows] - pltpu.roll(gq, LANES // 2, 1) * qs[rows]).astype(LOW)
-    value = dot(gproj[:, :width], wqkv[0], 1, 1)
-    value += dot(gproj[:, width : 2 * width], wqkv[1], 1, 1)
-    value += dot(gproj[:, 2 * width :], wqkv[2], 1, 1)
-    put(first, part0, part1, value.astype(LOW))
-
-
-def mlp_kernel(x0, x1, y0, y1, wgate, wup, wdown, hidden, gpre, down0, down1, back0, back1, xs, ys):
-    first = pl.program_id(0) < pl.num_programs(0) // 2
-    pick(first, xs, x0, x1)
-    pick(first, ys, y0, y1)
-    gate = dot(xs[...], wgate[...])
-    sig = jax.nn.sigmoid(gate)
-    act = gate * sig
-    slope = sig * (1.0 + gate * (1.0 - sig))
-    up = dot(xs[...], wup[...])
-    hidden[...] = (act * up).astype(LOW)
-    gh = dot(ys[...], wdown[...], 1, 1)
-    gpre[0] = (gh * up * slope).astype(LOW)
-    gpre[1] = (gh * act).astype(LOW)
-    put(first, down0, down1, dot(hidden[...], wdown[...]).astype(LOW))
-    put(first, back0, back1, (dot(gpre[0], wgate[...], 1, 1) + dot(gpre[1], wup[...], 1, 1)).astype(LOW))
+    series = rb // SEQ
+
+    def pairs(i):
+        q, second = i // 2, lax.rem(i, 2) == 1
+        k, b, s = q // blocks, lax.rem(q, blocks), lax.rem(i, 2)
+        rows = pl.ds(row_block(links, i, k, b, second), rb)
+        return [
+            (gproj.at[rows], gproj_out.at[rows]),
+            (xg.at[k, s, links.rows(b)], xg_out.at[k, s, links.rows(b)]),
+        ]
+
+    store = Store(store_sems, pairs)
+
+    def compute(i, k, b, second):
+        s = second.astype(jnp.int32)
+        at = row_block(links, i, k, b, second)
+        rows = pl.ds(at, rb)
+        first = at // SEQ
+        gmix[...] = dot(xg[k, s, links.rows(b)], wout[...], 1, 1).astype(LOW)
+        c, sn = row_angles(cp, sp, starts, first, series)
+        qc, qs = c * HS ** (-0.5), sn * HS ** (-0.5)
+        kc, ks = c * LN2, sn * LN2
+        for p in range(rb // PAIR):
+            part = slice(p * PAIR, (p + 1) * PAIR)
+            sub = pl.ds(pl.multiple_of(at + p * PAIR, PAIR), PAIR)
+            mask = pair_mask(starts, first + 2 * p)
+            col = lambda part, h: slice(part * width + h * LANES, part * width + (h + 1) * LANES)
+            heads = range(nh)
+            gm = [gmix[part, col(0, h)] for h in heads]
+            scores = [dot(qkv[sub, col(1, h)], qkv[sub, col(0, h)], 1, 1) + mask for h in heads]
+            grads = [dot(qkv[sub, col(2, h)], gm[h], 1, 1) for h in heads]
+            attention = [softmax_down(v) for v in scores]
+            for h in heads:
+                gproj[sub, col(2, h)] = dot(attention[h].astype(LOW), gm[h]).astype(LOW)
+            low = []
+            for h in heads:
+                both = attention[h] * grads[h]
+                low.append((both - attention[h] * jnp.sum(both, 0, keepdims=True)).astype(LOW))
+            for h in heads:
+                g = dot(low[h], qkv[sub, col(0, h)])
+                gproj[sub, col(1, h)] = (g * kc[part] - pltpu.roll(g, LANES // 2, 1) * ks[part]).astype(LOW)
+            for h in heads:
+                g = dot(low[h], qkv[sub, col(1, h)], 0, 0)
+                gproj[sub, col(0, h)] = (g * qc[part] - pltpu.roll(g, LANES // 2, 1) * qs[part]).astype(LOW)
+        value = dot(gproj[rows, :width], wqkv[0], 1, 1)
+        value += dot(gproj[rows, width : 2 * width], wqkv[1], 1, 1)
+        value += dot(gproj[rows, 2 * width :], wqkv[2], 1, 1)
+        store.start(i)
+        return [value]
+
+    run_blocks(links, lambda i, k, b, second: gather.arrive(k, b, second), compute, [scatter])
+    loads[3].wait()
+    loads[4].wait()
+    gain_grad[...] = jnp.zeros_like(gain_grad)
+
+    def last(b, carry):
+        rows = pl.ds(pl.multiple_of(b * rb, rb), rb)
+        grad, gains = norm_backward_block(begin[rows], gain[...], scatter.total(b), before[rows])
+        grad_rows[rows] = grad
+        gain_grad[0:1] += gains
+        return carry
+
+    lax.fori_loop(0, blocks, last, 0)
+    gather.finish()
+    scatter.finish()
+
+    def stored(i, carry):
+        store.wait(i)
+        return carry
+
+    lax.fori_loop(0, 2 * chips * blocks, stored, 0)
 
 
 def resident(shape):
@@ -186,133 +611,140 @@
     return pl.BlockSpec((rows, width), lambda i, *_: (i, 0))
 
 
-def two_parts(rows, width, n):
-    return [
-        pl.BlockSpec((rows, width), lambda i, *_: (jnp.minimum(i, n - 1), 0)),
-        pl.BlockSpec((rows, width), lambda i, *_: (jnp.maximum(i - n, 0), 0)),
-    ]
-
-
-def params():
-    return pltpu.CompilerParams(vmem_limit_bytes=VMEM_LIMIT, dimension_semantics=("arbitrary",))
-
-
-def attn_forward(x, wqkv, wout, starts, tables):
-    r, d = x[0].shape
-    m = 2 * r
+def params(collective_id=None):
+    return pltpu.CompilerParams(
+        vmem_limit_bytes=VMEM_LIMIT, collective_id=collective_id, has_side_effects=collective_id is not None
+    )
+
+
+ANY = pl.BlockSpec(memory_space=pl.ANY)
+WHOLE = pl.BlockSpec(memory_space=pltpu.VMEM)
+SCALARS = pl.BlockSpec(memory_space=pltpu.SMEM)
+
+
+def sems(*shape):
+    return pltpu.SemaphoreType.DMA(shape)
+
+
+def attn_forward(chips, x, start, gain, wqkv, wout, starts, tables):
+    r, d = x.shape
+    m = 2 * chips * r
     width = wout.shape[0]
     nh = width // LANES
-    rb = min(256, r)
-    n = r // rb
+    rb = min(BLOCK, r)
+    blocks = r // rb
+    steps = 2 * chips * blocks
     return pl.pallas_call(
-        functools.partial(attn_fwd_kernel, nh),
+        functools.partial(attn_fwd_kernel, nh, chips, blocks, rb),
         out_shape=[
             jax.ShapeDtypeStruct((m, 3 * width), LOW),
             jax.ShapeDtypeStruct((m, width), LOW),
-            jax.ShapeDtypeStruct((r, d), LOW),
+            jax.ShapeDtypeStruct((chips, 2, r, d), LOW),
+            jax.ShapeDtypeStruct((r, d), F32),
             jax.ShapeDtypeStruct((r, d), LOW),
         ],
-        grid_spec=pltpu.PrefetchScalarGridSpec(
-            num_scalar_prefetch=1,
-            grid=(2 * n,),
-            in_specs=[
-                *two_parts(rb, d, n),
-                resident((3, d, width)),
-                resident((width, d)),
-                resident((SEQ, LANES)),
-                resident((SEQ, LANES)),
-            ],
-            out_specs=[by_rows(rb, 3 * width), by_rows(rb, width), *two_parts(rb, d, n)],
-            scratch_shapes=[pltpu.VMEM((rb, d), LOW)],
-        ),
-        compiler_params=params(),
-        cost_estimate=pl.CostEstimate(
-            flops=2 * m * d * 4 * width + 4 * m * PAIR * width,
-            bytes_accessed=2 * (2 * m * d + 4 * m * width + 4 * d * width),
-            transcendentals=m * PAIR * nh,
-        ),
+        in_specs=[ANY, ANY, WHOLE, ANY, ANY, SCALARS, WHOLE, WHOLE],
+        out_specs=[ANY, ANY, ANY, WHOLE, WHOLE],
+        scratch_shapes=[
+            pltpu.VMEM((chips, 2, r, d), LOW),
+            pltpu.VMEM((3, d, width), LOW),
+            pltpu.VMEM((width, d), LOW),
+            pltpu.VMEM((m, 3 * width), LOW),
+            pltpu.VMEM((m, width), LOW),
+            pltpu.VMEM((r, d), F32),
+            sems(3),
+            sems(steps, 3),
+            *Gather.scratch(chips, blocks),
+            *Scatter.scratch(chips, blocks, r, d),
+        ],
+        compiler_params=params(1),
         name="attn_fwd",
-    )(starts, *x, wqkv, wout, *tables)
-
-
-def attn_backward(g, qkv, wqkv, wout, starts, tables):
-    r, d = g[0].shape
-    m = 2 * r
-    width = wout.shape[0]
-    nh = width // LANES
-    rb = min(256, r)
-    n = r // rb
+    )(x, start, gain, wqkv, wout, starts, *tables)
+
+
+def mlp_both(chips, x, gy, after, grad_in, gain, wgate, wup, wdown):
+    r, d = x.shape
+    m = 2 * chips * r
+    ff = wgate.shape[1]
+    rb = min(BLOCK, r)
+    blocks = r // rb
+    steps = 2 * chips * blocks
+    group = jax.ShapeDtypeStruct((chips, 2, r, d), LOW)
     return pl.pallas_call(
-        functools.partial(attn_bwd_kernel, nh),
-        out_shape=[
-            jax.ShapeDtypeStruct((m, 3 * width), LOW),
-            jax.ShapeDtypeStruct((r, d), LOW),
-            jax.ShapeDtypeStruct((r, d), LOW),
-        ],
-        grid_spec=pltpu.PrefetchScalarGridSpec(
-            num_scalar_prefetch=1,
-            grid=(2 * n,),
-            in_specs=[
-                *two_parts(rb, d, n),
-                by_rows(rb, 3 * width),
-                resident((3, d, width)),
-                resident((width, d)),
-                resident((SEQ, LANES)),
-                resident((SEQ, LANES)),
-            ],
-            out_specs=[by_rows(rb, 3 * width), *two_parts(rb, d, n)],
-            scratch_shapes=[pltpu.VMEM((rb, d), LOW), pltpu.VMEM((rb, width), LOW)],
-        ),
-        compiler_params=params(),
-        cost_estimate=pl.CostEstimate(
-            flops=2 * m * d * 4 * width + 12 * m * PAIR * width,
-            bytes_accessed=2 * (2 * m * d + 6 * m * width + 4 * d * width),
-            transcendentals=m * PAIR * nh,
-        ),
-        name="attn_bwd",
-    )(starts, *g, qkv, wqkv, wout, *tables)
-
-
-def mlp_both(x, gy, wgate, wup, wdown):
-    r, d = x[0].shape
-    m = 2 * r
-    ff = wgate.shape[1]
-    rb = min(256, r)
-    n = r // rb
-    part = jax.ShapeDtypeStruct((r, d), LOW)
-    return pl.pallas_call(
-        mlp_kernel,
-        grid=(2 * n,),
+        functools.partial(mlp_kernel, chips, blocks, rb),
         out_shape=[
             jax.ShapeDtypeStruct((m, ff), LOW),
             jax.ShapeDtypeStruct((2, m, ff), LOW),
-            part,
-            part,
-            part,
-            part,
+            group,
+            group,
+            jax.ShapeDtypeStruct((r, d), LOW),
+            jax.ShapeDtypeStruct((chips - 1, r, d), LOW),
+            jax.ShapeDtypeStruct((r, d), F32),
+            jax.ShapeDtypeStruct((r, d), LOW),
+            jax.ShapeDtypeStruct((8, d), F32),
         ],
-        in_specs=[
-            *two_parts(rb, d, n),
-            *two_parts(rb, d, n),
-            resident((d, ff)),
-            resident((d, ff)),
-            resident((ff, d)),
+        in_specs=[ANY, ANY, ANY, ANY, WHOLE, ANY, ANY, ANY],
+        out_specs=[ANY] * 6 + [WHOLE] * 3,
+        scratch_shapes=[
+            pltpu.VMEM((chips, 2, r, d), LOW),
+            pltpu.VMEM((chips, 2, r, d), LOW),
+            pltpu.VMEM((d, ff), LOW),
+            pltpu.VMEM((d, ff), LOW),
+            pltpu.VMEM((ff, d), LOW),
+            pltpu.VMEM((2, rb, ff), LOW),
+            pltpu.VMEM((2, 2, rb, ff), LOW),
+            pltpu.VMEM((r, d), F32),
+            pltpu.VMEM((r, d), F32),
+            sems(5),
+            sems(steps, 5),
+            sems(chips),
+            *Gather.scratch(chips, blocks),
+            *Gather.scratch(chips, blocks),
+            *Scatter.scratch(chips, blocks, r, d),
+            *[pltpu.VMEM((chips, r, d), LOW)] * 3,
+            sems(chips, blocks),
+            sems(chips, blocks),
         ],
-        out_specs=[
-            by_rows(rb, ff),
-            pl.BlockSpec((2, rb, ff), lambda i: (0, i, 0)),
-            *two_parts(rb, d, n),
-            *two_parts(rb, d, n),
+        compiler_params=params(2),
+        name="mlp_both",
+    )(x, gy, after, grad_in, gain, wgate, wup, wdown)
+
+
+def attn_backward(chips, x, start, grad_in, gain, qkv, wqkv, wout, starts, tables):
+    r, d = x.shape
+    m = 2 * chips * r
+    width = wout.shape[0]
+    nh = width // LANES
+    rb = min(BLOCK, r)
+    blocks = r // rb
+    steps = 2 * chips * blocks
+    return pl.pallas_call(
+        functools.partial(attn_bwd_kernel, nh, chips, blocks, rb),
+        out_shape=[
+            jax.ShapeDtypeStruct((m, 3 * width), LOW),
+            jax.ShapeDtypeStruct((chips, 2, r, d), LOW),
+            jax.ShapeDtypeStruct((r, d), F32),
+            jax.ShapeDtypeStruct((8, d), F32),
         ],
-        scratch_shapes=[pltpu.VMEM((rb, d), LOW), pltpu.VMEM((rb, d), LOW)],
-        compiler_params=params(),
-        cost_estimate=pl.CostEstimate(
-            flops=2 * m * d * 6 * ff,
-            bytes_accessed=2 * (4 * m * d + 3 * m * ff + 3 * d * ff),
-            transcendentals=m * ff,
-        ),
-        name="mlp_both",
-    )(*x, *gy, wgate, wup, wdown)
+        in_specs=[ANY, ANY, ANY, WHOLE, ANY, ANY, ANY, SCALARS, WHOLE, WHOLE],
+        out_specs=[ANY, ANY, WHOLE, WHOLE],
+        scratch_shapes=[
+            pltpu.VMEM((chips, 2, r, d), LOW),
+            pltpu.VMEM((3, d, width), LOW),
+            pltpu.VMEM((width, d), LOW),
+            pltpu.VMEM((m, 3 * width), LOW),
+            pltpu.VMEM((m, 3 * width), LOW),
+            pltpu.VMEM((rb, width), LOW),
+            pltpu.VMEM((r, d), F32),
+            pltpu.VMEM((r, d), F32),
+            sems(5),
+            sems(steps, 2),
+            *Gather.scratch(chips, blocks),
+            *Scatter.scratch(chips, blocks, r, d),
+        ],
+        compiler_params=params(3),
+        name="attn_bwd",
+    )(x, start, grad_in, gain, qkv, wqkv, wout, starts, *tables)
 
 
 def weight_grad(a, b, plane=None):
@@ -390,37 +822,8 @@
     )(*gproj, *mixed, *normed, *ga, selector)
 
 
-class Group:
-    def __init__(self, mesh):
-        self.n = mesh.shape["mp"]
-        self.chips = self.n // 2
-
-    def core(self, x):
-        return lax.ppermute(x, "mp", [(i, i ^ 1) for i in range(self.n)])
-
-    def from_chip(self, x, k):
-        return lax.ppermute(x, "mp", [((i + 2 * k) % self.n, i) for i in range(self.n)])
-
-    def to_chip(self, x, k):
-        return lax.ppermute(x, "mp", [(i, (i + 2 * k) % self.n) for i in range(self.n)])
-
-    def gather(self, x):
-        mine = [x] + [self.from_chip(x, k) for k in range(1, self.chips)]
-        return [(v, self.core(v)) for v in mine]
-
-    def scatter(self, parts):
-        total = None
-        for k in reversed(range(self.chips)):
-            mine = parts[k][0].astype(F32) + self.core(parts[k][1]).astype(F32)
-            if k:
-                mine = self.to_chip(mine.astype(LOW), k).astype(F32)
-            total = mine if total is None else total + mine
-        return total
-
-
 OUTER = 4
 CHUNK = 80
-MESH = pl.DeviceIdType.MESH
 
 
 def sum_kernel(inner, group, early, halves, late_pieces, *refs):
@@ -661,7 +1064,6 @@
         any_spec = pl.BlockSpec(memory_space=pl.ANY)
         late_pieces = halves[-1] // CHUNK // 2
         buffer = pltpu.VMEM((share, width), LOW)
-        sems = lambda *shape: pltpu.SemaphoreType.DMA(shape)
         return pl.pallas_call(
             functools.partial(sum_kernel, inner, self.group, len(got), halves, late_pieces),
             out_shape=[
@@ -697,19 +1099,6 @@
         )(*pieces, *got, small)
 
 
-def norm_forward(values, gain):
-    inverse = lax.rsqrt(jnp.mean(values * values, -1, keepdims=True) + EPSILON)
-    return ((values * inverse * gain).astype(LOW), inverse)
-
-
-def norm_backward(values, inverse, gain, grad_normed):
-    normal = values * inverse
-    grad_gain = jnp.sum(grad_normed * normal, 0)
-    scaled = grad_normed * gain
-    grad_values = inverse * (scaled - normal * jnp.mean(scaled * normal, -1, keepdims=True))
-    return (grad_values, grad_gain)
-
-
 def body(
     mesh,
     rows,
@@ -724,33 +1113,32 @@
     w_down,
     cotangent,
 ):
-    group = Group(mesh)
     reducer = Reducer(mesh)
+    group_size = mesh.shape["mp"]
+    chips = group_size // 2
     local_rows, d = rows.shape
     own_series = local_rows // SEQ
     mp_index = lax.axis_index("mp")
     heads_width = w_out.shape[0]
     head_count = heads_width // HS
     ff = w_down.shape[0]
-    chips = range(group.chips)
-
-    places = jnp.arange(group.n, dtype=jnp.int32)
-    owners = ((mp_index // 2 + places // 2) % group.chips) * 2 + (mp_index % 2 + places) % 2
-    starts = (SEQ - lengths.reshape(group.n, own_series))[owners]
-    group_starts = [starts[2 * k : 2 * k + 2].reshape(-1) for k in chips]
+
+    places = jnp.arange(group_size, dtype=jnp.int32)
+    owners = ((mp_index // 2 + places // 2) % chips) * 2 + (mp_index % 2 + places) % 2
+    starts = (SEQ - lengths.reshape(group_size, own_series))[owners]
     tables = slot_tables()
     slots = jnp.arange(SEQ, dtype=jnp.int32)
     mine_valid = (slots[None, :] >= starts[0][:, None]).astype(F32)
+    starts = starts.reshape(-1)
 
     by_series = lambda v: v.reshape(own_series, SEQ, d)
     picked = freq_table[NFREQ - 1][None]
     for f in range(NFREQ - 1):
         picked = jnp.where((freq_class == f)[:, None], freq_table[f][None], picked)
     start_rows = (by_series(rows) + picked[:, None]).reshape(local_rows, d)
-    normed_mine, inverse_attn = norm_forward(start_rows, gain_attn)
-    normed = group.gather(normed_mine)
+    inverse = lax.rsqrt(jnp.mean(start_rows * start_rows, -1, keepdims=True) + EPSILON)
+    normed_mine = (start_rows * inverse * gain_attn).astype(LOW)
     grad_output = (by_series(cotangent) * mine_valid[:, :, None]).reshape(local_rows, d)
-    grad_down_in = group.gather(grad_output.astype(LOW))
 
     selector = head_selector(head_count)
     qkv_low = jnp.einsum("cdf,fg->cdg", w_qkv.astype(LOW), selector, preferred_element_type=F32).astype(LOW)
@@ -759,42 +1147,35 @@
     up_low = w_gate_up[1].astype(LOW)
     down_low = w_down.astype(LOW)
 
-    fwd = [attn_forward(normed[k], qkv_low, out_low, group_starts[k], tables) for k in chips]
-    after_attn = start_rows + group.scatter([f[2:] for f in fwd])
-    normed_mlp_mine, inverse_mlp = norm_forward(after_attn, gain_mlp)
-    normed_mlp = group.gather(normed_mlp_mine)
-
-    mlp = [mlp_both(normed_mlp[k], grad_down_in[k], gate_low, up_low, down_low) for k in chips]
-    grad_normed_mlp = group.scatter([m[4:] for m in mlp])
-    output = after_attn + group.scatter([m[2:4] for m in mlp])
-    flat = lambda pairs: [v for pair in pairs for v in pair]
-    grad_down = weight_grad([m[0] for m in mlp], flat(grad_down_in))
-    ups = [weight_grad(flat(normed_mlp), [m[1] for m in mlp], c) for c in range(2)]
+    qkv, mixed, normed, after_attn, normed_mlp_mine = attn_forward(
+        chips, normed_mine, start_rows, gain_mlp[None], qkv_low, out_low, starts, tables
+    )
+    hidden, grad_pre, normed_mlp, grad_down_in, down_own, down_far, grad_after, grad_after_low, gains_mlp = mlp_both(
+        chips, normed_mlp_mine, grad_output.astype(LOW), after_attn, grad_output, gain_mlp[None],
+        gate_low, up_low, down_low,
+    )
+    flat = lambda v: v.reshape(-1, d)
+    grad_down = weight_grad([hidden], [flat(grad_down_in)])
+    ups = [weight_grad([flat(normed_mlp)], [grad_pre], c) for c in range(2)]
     pieces = [grad_down] + (ups if ff >= d else [jnp.concatenate(ups, 1)])
     got = [reducer.exchange(p) for p in pieces]
-
-    grad_rows_mlp, grad_gain_mlp = norm_backward(after_attn, inverse_mlp, gain_mlp, grad_normed_mlp)
-    grad_after = grad_output + grad_rows_mlp
-    grad_attn_in = group.gather(grad_after.astype(LOW))
-
-    bwd = [
-        attn_backward(grad_attn_in[k], fwd[k][0], qkv_low, out_low, group_starts[k], tables) for k in chips
-    ]
-    grad_normed = group.scatter([b[1:] for b in bwd])
+    output = after_attn + down_own.astype(F32)
+    for k in range(1, chips):
+        far = lax.ppermute(down_far[k - 1], "mp", [(i, (i + 2 * k) % group_size) for i in range(group_size)])
+        output += far.astype(F32)
+
+    grad_proj, grad_attn_in, grad_rows, gains_attn = attn_backward(
+        chips, grad_after_low, start_rows, grad_after, gain_attn[None], qkv, qkv_low, out_low, starts, tables
+    )
     pieces.append(
-        attn_weight_grad(
-            [b[0] for b in bwd], [f[1] for f in fwd], flat(normed), flat(grad_attn_in), selector
-        )
+        attn_weight_grad([grad_proj], [mixed], [flat(normed)], [flat(grad_attn_in)], selector)
     )
-
-    grad_rows_attn, grad_gain_attn = norm_backward(start_rows, inverse_attn, gain_attn, grad_normed)
-    grad_rows = grad_after + grad_rows_attn
     series_sums = jnp.sum(by_series(grad_rows), 1)
     grad_table = [jnp.sum(jnp.where((freq_class == f)[:, None], series_sums, 0.0), 0) for f in range(NFREQ)]
 
     tokens = jnp.full((d,), jnp.sum(mine_valid))
     zero = jnp.zeros((d,), F32)
-    small = jnp.stack([grad_gain_attn, grad_gain_mlp, *grad_table, tokens, zero, zero])
+    small = jnp.stack([gains_attn[0], gains_mlp[0], *grad_table, tokens, zero, zero])
     sums, small = reducer.reduce(pieces, got, small)
     root_scale = lax.rsqrt(small[2 + NFREQ, 0])
     small = small * root_scale

time: 685 us -> 601 us (0.88)
  waiting for transfers between devices: 175 us -> 0.01 us
  Pallas kernels: 394 us -> 515 us
  other arithmetic: 55.1 us -> 39.2 us
  starting transfers between devices: 19 us -> 4.91 us
    ppermute x24 -> x1, waiting for transfers between devices: 175 us -> 0.01 us  [body(): lax.ppermute(down_far[k - 1], 'mp', [(i, (i + 2 * k) % group_size) for i...]
    pallas_call x6 -> x3, Pallas kernels: 132 us -> 256 us  [the longest x1 97.2 us: mlp_both(): pl.pallas_call(functools.partial(mlp_kernel, chips, blocks, rb), out_shap...]
    ppermute x24 -> x1, starting transfers between devices: 15.5 us -> 1.51 us  [body(): lax.ppermute(down_far[k - 1], 'mp', [(i, (i + 2 * k) % group_size) for i...]
    convert_element_type x8 -> x2, other arithmetic: 14.6 us -> 3.63 us  [the longest x1 2.29 us: body(): grad_output.astype(LOW)]
  transfers between devices with their start and end apart: 27 -> 4, of which waited for: 8 -> 0; matrix products, arithmetic and copies ran while one was open for 8% -> 2% of each run, Pallas kernels for 29% -> 24%
where the time goes in v2:
time: 601 us; the launch traced here: 600 us
  Pallas kernels  515 us (86%)
  other arithmetic  39.2 us (7%)
  local copies, waits for them, and re-layouts  29.2 us (5%)
  matrix products  10.5 us (2%)
    pallas_call x1, Pallas kernels, reduce(): pl.pallas_call(functools.partial(sum_kernel, inner, self.group, len(got),...  192 us
    pallas_call x1, Pallas kernels, mlp_both(): pl.pallas_call(functools.partial(mlp_kernel, chips, blocks, rb), out_shap...  97.2 us
    pallas_call x1, Pallas kernels, attn_backward(): pl.pallas_call(functools.partial(attn_bwd_kernel, nh, chips, blocks, rb),...  89 us
    pallas_call x1, Pallas kernels, attn_forward(): pl.pallas_call(functools.partial(attn_fwd_kernel, nh, chips, blocks, rb),...  69.3 us
    pallas_call x3, Pallas kernels, weight_grad(): pl.pallas_call(kernel, grid=(n // nb,), out_shape=jax.ShapeDtypeStruct((w...  34.9 us
    pallas_call x1, Pallas kernels, attn_weight_grad(): pl.pallas_call(kernel, grid=(d // kb,), out_shape=jax.ShapeDtypeStruct((4...  32 us
  transfers between devices with their start and end apart: 4, of which 0 were waited for; matrix products, arithmetic and copies ran while one was open for 2% of the time, Pallas kernels for 24%

profile of v2, /device:TPU:0, one launch (start us, length us, event | category | flops | bytes accessed | tf_op | source)
XLA Modules:
  0.0 600.4 jit_solution(14192762399945581838)
XLA Ops:
  3.3 0.9 slice_reduce_fusion.4
  4.2 2.1 multiply_reduce_fusion
  7.2 8.2 %convert.5 = bf16[2,1280,1280]{2,1,0:T(8,128)(2,1)} convert(f32[2,1280,1280]{2,1,0:T(8,128)} %param.22) | non-fusion elementwise | flops 3276800 | bytes 19660800 | tf_op jit(solution)/shard_map/convert.2
  15.4 6.2 %slice_bitcast_fusion = (bf16[1280,1280]{1,0:T(8,128)(2,1)}, bf16[1280,1280]{1,0:T(8,128)(2,1)}) fusion(bf16[2,1280,1280]{2,1,0:T(8,128)(2,1)} %convert.5), kind=kLoop, calls=%fused_computation.6 | loop fusion | bytes 13107200 | tf_op jit(solution)/shard_map/convert_element_type | solution.py:1147
  21.6 2.0 convert_element_type.66.wdown_any
  23.7 6.7 %fusion.wqkv_any = bf16[3,1280,512]{2,1,0:T(8,128)(2,1)} fusion(bf16[320,512,1]{1,0,2:T(8,128)(2,1)S(1)} %copy-done.7, f32[3,1280,320]{1,2,0:T(8,128)} %param.20), kind=kOutput, calls=%fused_computation.5 | convolution fusion | flops 1261486080 | bytes 9175040 | tf_op jit(solution)/shard_map/cdf,fg->cdg/dot_general | solution.py:1144
  30.4 1.9 convolution_convert_fusion.1.wout_any
  32.3 2.3 fusion.17
  34.6 1.3 multiply_convert_fusion.x
  35.9 69.3 %attn_fwd.1 = (bf16[2048,1536]{1,0:T(8,128)(2,1)}, bf16[2048,512]{1,0:T(8,128)(2,1)}, bf16[2,2,512,1280]{3,2,1,0:T(8,128)(2,1)}, f32[512,1280]{1,0:T(8,128)}, bf16[512,1280]{1,0:T(8,128)(2,1)}) custom-call(bf16[512,1280]{1,0:T(8,128)(2,1)} %multiply_convert_fusion.x, f32[512,1280]{1,0:T(8,128)} %copy-done, f32[1,1280]{1,0:T(1,128)} %broadcast_in_dim.92.gain, ...), custom_call_target="tpu_custom_call" | custom-call | tf_op jit(solution)/shard_map/attn_fwd/pallas_call | solution.py:637
  105.3 97.2 %mlp_both.1 = (bf16[2048,1280]{1,0:T(8,128)(2,1)}, bf16[2,2048,1280]{2,1,0:T(8,128)(2,1)}, bf16[2,2,512,1280]{3,2,1,0:T(8,128)(2,1)}, bf16[2,2,512,1280]{3,2,1,0...) custom-call(bf16[512,1280]{1,0:T(8,128)(2,1)} %get-tuple-element.30., ...), custom_call_target="tpu_custom_call" | custom-call | tf_op jit(solution)/shard_map/mlp_both/pallas_call | solution.py:673
  202.5 11.7 %weight_grad.5.refs_2_ = bf16[1280,1280]{1,0:T(8,128)(2,1)} custom-call(bf16[2048,1280]{1,0:T(8,128)(2,1)} %bitcast.47, bf16[2,2048,1280]{2,1,0:T(8,128)(2,1)} %get-tuple-element.40.refs_1_), custom_call_target="tpu_custom_call" | custom-call | flops 6710886400 | bytes 13762560 | tf_op jit(solution)/shard_map/weight_grad/pallas_call | solution.py:770
  214.2 2.7 constant_dynamic-slice_fusion
  216.9 1.4 collective-permute-start.3
  218.3 11.6 %weight_grad.4.refs_1_ = bf16[1280,1280]{1,0:T(8,128)(2,1)} custom-call(bf16[2048,1280]{1,0:T(8,128)(2,1)} %bitcast.48, bf16[2,2048,1280]{2,1,0:T(8,128)(2,1)} %get-tuple-element.40.refs_1_), custom_call_target="tpu_custom_call" | custom-call | flops 6710886400 | bytes 13762560 | tf_op jit(solution)/shard_map/weight_grad/pallas_call | solution.py:770
  229.9 2.7 constant_dynamic-slice_fusion.1
  233.3 11.6 %weight_grad.3.refs_0_ = bf16[1280,1280]{1,0:T(8,128)(2,1)} custom-call(bf16[2048,1280]{1,0:T(8,128)(2,1)} %get-tuple-element.37.refs_0_, bf16[2048,1280]{1,0:T(8,128)(2,1)} %bitcast.46), custom_call_target="tpu_custom_call" | custom-call | flops 6710886400 | bytes 13762560 | tf_op jit(solution)/shard_map/weight_grad/pallas_call | solution.py:770
  244.9 2.7 constant_dynamic-slice_fusion.2
  247.6 1.4 collective-permute-start.1
  249.0 1.5 collective-permute-start
  251.1 89.0 %attn_bwd.1 = (bf16[2048,1536]{1,0:T(8,128)(2,1)}, bf16[2,2,512,1280]{3,2,1,0:T(8,128)(2,1)}, f32[512,1280]{1,0:T(8,128)}, f32[8,1280]{1,0:T(8,128)}) custom-call(bf16[512,1280]{1,0:T(8,128)(2,1)} %get-tuple-element.33.x, f32[512,1280]{1,0:T(8,128)} %copy-done, f32[512,1280]{1,0:T(8,128)} %get-tuple-element.34.grad_in, f32[1,1280]{1,0:T(1,128)} %broadcast_in_dim.93.gain, ...), custom_call_target="tpu_custom_call" | custom-call | tf_op jit(solution)/shard_map/attn_bwd/pallas_call | solution.py:721
  340.1 2.0 bitcast_reduce_fusion
  345.8 32.0 %attn_weight_grad.1.refs_3_ = bf16[1280,1280]{1,0:T(8,128)(2,1)} custom-call(bf16[2048,1536]{1,0:T(8,128)(2,1)} %get-tuple-element.41.refs_0_, bf16[2048,512]{1,0:T(8,128)(2,1)} %get-tuple-element.42.refs_1_, bf16[2048,1280]{1,0:T(8,128)(2,1)} %bitcast.44, bf16[2048,1280]{1,0:T(8,128)(2,1)} %bitcast.45, bf16[320,512]{1,0:T(8,128)(2,1)} %constant.92.clone.refs_4_), custom_call_target="tpu_custom_call" | custom-call | flops 10737418240 | bytes 18874368 | tf_op jit(solution)/shard_map/attn_weight_grad/pallas_call | solution.py:806
  377.8 3.1 convert_add_fusion
  381.0 192.5 %sum_over_dp.1 = (bf16[2,2560,1280]{2,1,0:T(8,128)(2,1)}, f32[8,1280]{1,0:T(8,128)}) custom-call(bf16[1280,1280]{1,0:T(8,128)(2,1)} %weight_grad.3.refs_0_, bf16[1280,1280]{1,0:T(8,128)(2,1)} %weight_grad.4.refs_1_, bf16[1280,1280]{1,0:T(8,128)(2,1)} %weight_grad.5.refs_2_, bf16[1280,1280]{1,0:T(8,128)(2,1)} %attn_weight_grad.1.refs_3_, ...), custom_call_target="tpu_custom_call" | custom-call | bytes 600000000 | tf_op jit(solution)/shard_map/sum_over_dp/pallas_call | solution.py:1067
  573.5 1.2 slice.72
  577.4 5.2 convert_multiply_fusion.1
  582.6 4.2 fusion.18
  586.8 1.3 convert_multiply_fusion.2
  590.0 6.0 convert_multiply_fusion
  596.0 2.6 pad_maximum_fusion
  598.9 1.5 copy.27
  (57 shorter events, 12.7 us)
Async XLA Ops:
  4.2 2.2 copy-start.10
  6.4 28.2 %copy-start = (f32[512,1280]{1,0:T(8,128)}, f32[512,1280]{1,0:T(8,128)S(1)}, u32[]{:S(2)}) copy-start(f32[512,1280]{1,0:T(8,128)S(1)} %get-tuple-element.60.start) | copy-start | bytes 7864324
  15.4 6.2 %copy-start.3 = (f32[1280,1280]{1,0:T(8,128)S(1)}, f32[1280,1280]{1,0:T(8,128)}, u32[]{:S(2)}) copy-start(f32[1280,1280]{1,0:T(8,128)} %param.23) | copy-start | bytes 19660804
  21.6 2.0 copy-start.7
  23.7 6.7 %copy-start.5 = (f32[320,1280]{1,0:T(8,128)S(1)}, f32[320,1280]{1,0:T(8,128)}, u32[]{:S(2)}) copy-start(f32[320,1280]{1,0:T(8,128)} %param.21) | copy-start | bytes 4915204
  23.7 6.7 %copy-start.8 = (bf16[320,512]{1,0:T(8,128)(2,1)S(1)}, bf16[320,512]{1,0:T(8,128)(2,1)}, u32[]{:S(2)}) copy-start(bf16[320,512]{1,0:T(8,128)(2,1)} %constant.92.clone.refs_4_) | copy-start | bytes 983044
  30.4 1.9 copy-start.4
  32.3 2.3 copy-start.9
  216.9 164.0 %collective-permute-start.3 = (bf16[640,1280]{1,0:T(8,128)(2,1)}, bf16[640,1280]{1,0:T(8,128)(2,1)}, u32[]{:S(2)}, u32[]{:S(2)}) collective-permute-start(bf16[640,1280]{1,0:T(8,128)(2,1)} %constant_dynamic-slice_fusion), channel_id=1, source_target_pairs={{0,4},{4,0},{8,12},{12,8},{16,20},{20,16},{24,28},{28,24},{1,5},{5... | collective-permute-start | bytes 4915208 | tf_op jit(solution)/shard_map/ppermute | solution.py:1055
  232.7 148.3 %collective-permute-start.2 = (bf16[640,1280]{1,0:T(8,128)(2,1)}, bf16[640,1280]{1,0:T(8,128)(2,1)}, u32[]{:S(2)}, u32[]{:S(2)}) collective-permute-start(bf16[640,1280]{1,0:T(8,128)(2,1)} %constant_dynamic-slice_fusion.1), channel_id=1, source_target_pairs={{0,4},{4,0},{8,12},{12,8},{16,20},{20,16},{24,28},{28,24},{1,5},{5... | collective-permute-start | bytes 4915208 | tf_op jit(solution)/shard_map/ppermute | solution.py:1055
  247.6 133.4 %collective-permute-start.1 = (bf16[640,1280]{1,0:T(8,128)(2,1)}, bf16[640,1280]{1,0:T(8,128)(2,1)}, u32[]{:S(2)}, u32[]{:S(2)}) collective-permute-start(bf16[640,1280]{1,0:T(8,128)(2,1)} %constant_dynamic-slice_fusion.2), channel_id=1, source_target_pairs={{0,4},{4,0},{8,12},{12,8},{16,20},{20,16},{24,28},{28,24},{1,5},{5... | collective-permute-start | bytes 4915208 | tf_op jit(solution)/shard_map/ppermute | solution.py:1055
  249.0 128.8 %collective-permute-start = (bf16[512,1280]{1,0:T(8,128)(2,1)}, bf16[512,1280]{1,0:T(8,128)(2,1)}, u32[]{:S(2)}, u32[]{:S(2)}) collective-permute-start(bf16[512,1280]{1,0:T(8,128)(2,1)} %bitcast.7), channel_id=1, source_target_pairs={{0,2},{1,3},{2,0},{3,1},{4,6},{5,7},{6,4},{7,5},{8,10},{9,11},{10,... | collective-permute-start | bytes 3932168 | tf_op jit(solution)/shard_map/ppermute | solution.py:1164
  345.8 32.0 %copy-start.2 = (f32[512,1280]{1,0:T(8,128)S(1)}, f32[512,1280]{1,0:T(8,128)}, u32[]{:S(2)}) copy-start(f32[512,1280]{1,0:T(8,128)} %get-tuple-element.29.after) | copy-start | bytes 7864324
  345.8 32.0 %copy-start.6 = (bf16[512,1280]{1,0:T(8,128)(2,1)S(1)}, bf16[512,1280]{1,0:T(8,128)(2,1)}, u32[]{:S(2)}) copy-start(bf16[512,1280]{1,0:T(8,128)(2,1)} %get-tuple-element.31) | copy-start | bytes 3932164
  596.0 2.9 copy-start.1

commit v3 on v2

--- a/solution.py
+++ b/solution.py
@@ -21,7 +21,7 @@
 HIGHEST = lax.Precision.HIGHEST
 LOW = jnp.bfloat16
 F32 = jnp.float32
-VMEM_LIMIT = 60 * 1024 * 1024
+VMEM_LIMIT = 62 * 1024 * 1024 + 512 * 1024
 MESH = pl.DeviceIdType.MESH
 LN2 = float(np.log(2.0))
 QSCALE = float(HS**-0.5 / np.log(2.0))
@@ -100,6 +100,10 @@
     def rows(self, b):
         return pl.ds(b * self.rb, self.rb)
 
+    def block(self, k, s, b):
+        at = (2 * k + s) * (self.blocks * self.rb) + b * self.rb
+        return pl.ds(at if isinstance(at, int) else pl.multiple_of(at, self.rb), self.rb)
+
     def each(self, body):
         def one(q, carry):
             body(q // self.blocks, lax.rem(q, self.blocks))
@@ -120,28 +124,29 @@
         self.core_send, self.core_recv = core_send, core_recv
         self.chip_send, self.chip_recv = chip_send, chip_recv
 
+    def place(self, k, s, b):
+        return self.buf.at[self.links.block(k, s, b)]
+
     def own(self, b):
-        rows = self.links.rows(b)
-        return pltpu.make_async_copy(self.x.at[rows], self.buf.at[0, 0, rows], self.local.at[b])
+        return pltpu.make_async_copy(self.x.at[self.links.rows(b)], self.place(0, 0, b), self.local.at[b])
 
     def to_chip(self, k, b):
         rows = self.links.rows(b)
         return remote(
-            self.x.at[rows], self.buf.at[k, 0, rows], self.chip_send.at[k, b], self.chip_recv.at[k, b],
+            self.x.at[rows], self.place(k, 0, b), self.chip_send.at[k, b], self.chip_recv.at[k, b],
             self.links.nearer(k),
         )
 
     def to_core(self, k, b):
-        rows = self.links.rows(b)
         return remote(
-            self.buf.at[k, 0, rows], self.buf.at[k, 1, rows], self.core_send.at[k, b], self.core_recv.at[k, b],
+            self.place(k, 0, b), self.place(k, 1, b), self.core_send.at[k, b], self.core_recv.at[k, b],
             self.links.core,
         )
 
     def own_to_core(self, b):
         rows = self.links.rows(b)
         return remote(
-            self.x.at[rows], self.buf.at[0, 1, rows], self.core_send.at[0, b], self.core_recv.at[0, b],
+            self.x.at[rows], self.place(0, 1, b), self.core_send.at[0, b], self.core_recv.at[0, b],
             self.links.core,
         )
 
@@ -199,7 +204,7 @@
     def to_chip(self, k, b):
         rows = self.links.rows(b)
         return remote(
-            self.keep.at[k, rows], self.far.at[k, rows], self.chip_send.at[k, b], self.chip_recv.at[k, b],
+            self.keep.at[k, rows], self.far.at[k - 1, rows], self.chip_send.at[k, b], self.chip_recv.at[k, b],
             self.links.further(k),
         )
 
@@ -229,7 +234,7 @@
         value = self.keep[0, rows].astype(F32) + self.got[0, rows].astype(F32)
         for k in range(1, self.links.chips):
             self.to_chip(k, b).wait_recv()
-            value += self.far[k, rows].astype(F32)
+            value += self.far[k - 1, rows].astype(F32)
         return value
 
     def finish(self):
@@ -244,7 +249,8 @@
 
     @staticmethod
     def scratch(chips, blocks, rows, width):
-        return [pltpu.VMEM((chips, rows, width), LOW)] * 4 + [pltpu.SemaphoreType.DMA((chips, blocks))] * 4
+        buffers = [pltpu.VMEM((n, rows, width), LOW) for n in (chips, chips, chips, chips - 1)]
+        return buffers + [pltpu.SemaphoreType.DMA((chips, blocks))] * 4
 
 
 def run_blocks(links, arrive, compute, scatters):
@@ -291,50 +297,106 @@
     return copies
 
 
-def row_block(links, i, k, b, second):
-    at = (2 * k + second.astype(jnp.int32)) * (links.blocks * links.rb) + b * links.rb
-    return pl.multiple_of(at, links.rb)
-
-
-def attn_fwd_kernel(nh, chips, blocks, rb, x, start, gain, wqkv_any, wout_any, starts, cp, sp, *refs):
-    qkv_out, mixed_out, xg_out, after, normed, refs = *refs[:5], refs[5:]
-    xg, wqkv, wout, qkv, mixed, begin, load, store_sems, refs = *refs[:8], refs[8:]
+def step_place(links, i):
+    q, s = i // 2, lax.rem(i, 2)
+    return q // links.blocks, s, lax.rem(q, links.blocks)
+
+
+def valid_rows(starts, first, rows):
+    slot = lax.broadcasted_iota(jnp.int32, (SEQ, 1), 0)
+    return jnp.concatenate(
+        [(slot >= starts[first + i]).astype(F32) for i in range(rows // SEQ)], 0
+    )
+
+
+def with_class_rows(begin, picked):
+    for i in range(begin.shape[0] // SEQ):
+        begin[i * SEQ : (i + 1) * SEQ] += picked[i : i + 1]
+
+
+def norm_low(value, gain):
+    inverse = lax.rsqrt(jnp.mean(value * value, -1, keepdims=True) + EPSILON)
+    return (value * inverse * gain).astype(LOW)
+
+
+def cast_rows(src, dst, wide, low, load, store):
+    tile = wide.shape[1]
+    count = src.shape[0] // tile
+
+    def get(t):
+        return pltpu.make_async_copy(src.at[pl.ds(t * tile, tile)], wide.at[lax.rem(t, 2)], load.at[lax.rem(t, 2)])
+
+    def give(t):
+        return pltpu.make_async_copy(low.at[lax.rem(t, 2)], dst.at[pl.ds(t * tile, tile)], store.at[lax.rem(t, 2)])
+
+    get(0).start()
+
+    def one(t, carry):
+        @pl.when(t + 1 < count)
+        def _():
+            get(t + 1).start()
+
+        get(t).wait()
+
+        @pl.when(t >= 2)
+        def _():
+            give(t - 2).wait()
+
+        low[lax.rem(t, 2)] = wide[lax.rem(t, 2)].astype(LOW)
+        give(t).start()
+        return carry
+
+    lax.fori_loop(0, count, one, 0)
+    for t in range(max(count - 2, 0), count):
+        give(t).wait()
+
+
+def attn_fwd_kernel(
+    nh, chips, blocks, rb, rows_any, cot_any, picked, gain_attn, gain_mlp, wqkv_any, wout_any, gate_any, down_any,
+    selector, starts, cp, sp, *refs
+):
+    qkv_out, mixed_out, xg_out, wqkv_out, wout_out, gate_out, down_out, after, normed, gy, refs = *refs[:10], refs[10:]
+    x, xg, wqkv, wout, wqkv_wide, wout_wide, qkv, mixed, begin, cot, load, store_sems, refs = *refs[:12], refs[12:]
+    gate_wide, gate_low, down_wide, down_low, cast_sems, weight_sems, refs = *refs[:6], refs[6:]
     gather_refs, scatter_refs = refs[:5], refs[5:]
     links = Links(chips, blocks, rb)
-    loads = loader(load, [(wqkv_any, wqkv), (wout_any, wout), (start, begin)])
+    loads = loader(
+        load, [(rows_any, begin), (wqkv_any, wqkv_wide), (wout_any, wout_wide), (cot_any, cot)]
+    )
+    loads[0].wait()
+    with_class_rows(begin, picked)
+    for b in range(blocks):
+        x[b * rb : (b + 1) * rb] = norm_low(begin[b * rb : (b + 1) * rb], gain_attn[...])
     links.greet()
     gather = Gather(links, x, xg, *gather_refs)
     scatter = Scatter(links, *scatter_refs)
-    gather.start_near()
     for b in range(blocks):
         gather.start_far(b)
-    loads[0].wait()
-    loads[1].wait()
+    gather.start_near()
     width = nh * LANES
     series = rb // SEQ
-
-    def places(i):
-        q, second = i // 2, lax.rem(i, 2) == 1
-        k, b = q // blocks, lax.rem(q, blocks)
-        return k, b, lax.rem(i, 2), row_block(links, i, k, b, second)
+    loads[1].wait()
+    for c in range(3):
+        wqkv[c] = dot(wqkv_wide[c].astype(LOW), selector[...]).astype(LOW)
+    loads[2].wait()
+    wout[...] = dot(selector[...], wout_wide[...].astype(LOW), 0, 0).astype(LOW)
+    weights = loader(weight_sems, [(wqkv, wqkv_out), (wout, wout_out)])
 
     def pairs(i):
-        k, b, s, at = places(i)
-        rows = pl.ds(at, rb)
+        rows = links.block(*step_place(links, i))
         return [
             (qkv.at[rows], qkv_out.at[rows]),
             (mixed.at[rows], mixed_out.at[rows]),
-            (xg.at[k, s, links.rows(b)], xg_out.at[k, s, links.rows(b)]),
+            (xg.at[rows], xg_out.at[rows]),
         ]
 
     store = Store(store_sems, pairs)
 
     def compute(i, k, b, second):
-        s = second.astype(jnp.int32)
-        at = row_block(links, i, k, b, second)
-        rows = pl.ds(at, rb)
-        xs = xg[k, s, links.rows(b)]
+        rows = links.block(*step_place(links, i))
+        at = rows.start
         first = at // SEQ
+        xs = xg[rows]
         c, sn = row_angles(cp, sp, starts, first, series)
         for part in range(3):
             proj = dot(xs, wqkv[part])
@@ -360,19 +422,22 @@
         return [part]
 
     run_blocks(links, lambda i, k, b, second: gather.arrive(k, b, second), compute, [scatter])
-    loads[2].wait()
-
-    def last(b, carry):
-        rows = pl.ds(pl.multiple_of(b * rb, rb), rb)
+
+    loads[3].wait()
+    for b in range(blocks):
+        rows = slice(b * rb, (b + 1) * rb)
+        gy[rows] = (cot[rows] * valid_rows(starts, b * series, rb)).astype(LOW)
+    cast_rows(gate_any, gate_out, gate_wide, gate_low, cast_sems.at[0], cast_sems.at[1])
+    cast_rows(down_any, down_out, down_wide, down_low, cast_sems.at[2], cast_sems.at[3])
+    for b in range(blocks):
+        rows = slice(b * rb, (b + 1) * rb)
         value = begin[rows] + scatter.total(b)
         after[rows] = value
-        inverse = lax.rsqrt(jnp.mean(value * value, -1, keepdims=True) + EPSILON)
-        normed[rows] = (value * inverse * gain[...]).astype(LOW)
-        return carry
-
-    lax.fori_loop(0, blocks, last, 0)
+        normed[rows] = norm_low(value, gain_mlp[...])
     gather.finish()
     scatter.finish()
+    for copy in weights:
+        copy.wait()
 
     def stored(i, carry):
         store.wait(i)
@@ -389,21 +454,61 @@
     return grad, jnp.sum(grad_normed * normal, 0, keepdims=True)
 
 
-def mlp_kernel(chips, blocks, rb, x, gy, after, grad_in, gain, wgate_any, wup_any, wdown_any, *refs):
-    hidden_out, gpre_out, xg_out, yg_out, own_out, far_out, grad_after, low_after, gain_grad, refs = *refs[:9], refs[9:]
-    xg, yg, wgate, wup, wdown, hidden, gpre, begin, before, load, store_sems, down_sems, refs = *refs[:12], refs[12:]
+def column_tiles(body, width, tile, stage, sems, copies):
+    def start_all(t, wait):
+        cols = pl.ds(pl.multiple_of(t * tile, tile), tile)
+        slot = lax.rem(t, 2)
+        for j, (a, b) in enumerate(copies(slot, cols)):
+            copy = pltpu.make_async_copy(a, b, sems.at[slot, j])
+            if wait:
+                copy.wait()
+            else:
+                copy.start()
+
+    count = width // tile
+
+    def one(t, carry):
+        @pl.when(t >= 2)
+        def _():
+            start_all(t - 2, True)
+
+        body(lax.rem(t, 2), pl.ds(pl.multiple_of(t * tile, tile), tile))
+        start_all(t, False)
+        return carry
+
+    lax.fori_loop(0, count, one, 0)
+    for t in range(max(count - 2, 0), count):
+        start_all(t, True)
+
+
+def mlp_kernel(chips, inner, blocks, rb, x, gy, after, cot, gain, gate_any, down_any, starts, *refs):
+    gpre_out, xg_out, own_out, far_out, refs = *refs[:4], refs[4:]
+    grad_down, refs = refs[:inner], refs[inner:]
+    grad_after, low_after, gain_grad, refs = *refs[:3], refs[3:]
+    xg, yg, wgate, wup, wdown, hidden, gpre, begin, before, stage, load, store_sems, refs = *refs[:12], refs[12:]
+    down_sems, stage_sems, refs = *refs[:2], refs[2:]
     xg_refs, yg_refs, back_refs = refs[:5], refs[5:10], refs[10:18]
     give, keep, got, down_send, down_recv = refs[18:]
+    d, ff = wgate.shape
     links = Links(chips, blocks, rb)
-    loads = loader(load, [(wgate_any, wgate), (wup_any, wup), (wdown_any, wdown), (after, begin), (grad_in, before)])
+    loads = loader(
+        load,
+        [
+            (gate_any.at[pl.ds(0, d)], wgate),
+            (gate_any.at[pl.ds(d, d)], wup),
+            (down_any, wdown),
+            (after, begin),
+            (cot, before),
+        ],
+    )
     links.greet()
     gather = Gather(links, x, xg, *xg_refs)
     second_gather = Gather(links, gy, yg, *yg_refs)
     back = Scatter(links, *back_refs)
+    for b in range(blocks):
+        gather.start_far(b)
     gather.start_near()
     second_gather.start_near()
-    for b in range(blocks):
-        gather.start_far(b)
 
     def down_to_core(k, b):
         rows = links.rows(b)
@@ -412,16 +517,12 @@
         )
 
     def pairs(i):
-        q, second = i // 2, lax.rem(i, 2) == 1
-        k, b, s = q // blocks, lax.rem(q, blocks), lax.rem(i, 2)
-        rows = pl.ds(row_block(links, i, k, b, second), rb)
+        rows = links.block(*step_place(links, i))
         slot = lax.rem(i, 2)
         return [
-            (hidden.at[slot], hidden_out.at[rows]),
             (gpre.at[slot, 0], gpre_out.at[0, rows]),
             (gpre.at[slot, 1], gpre_out.at[1, rows]),
-            (xg.at[k, s, links.rows(b)], xg_out.at[k, s, links.rows(b)]),
-            (yg.at[k, s, links.rows(b)], yg_out.at[k, s, links.rows(b)]),
+            (xg.at[rows], xg_out.at[rows]),
         ]
 
     store = Store(store_sems, pairs)
@@ -443,26 +544,26 @@
             loads[2].wait()
 
     def compute(i, k, b, second):
-        s = second.astype(jnp.int32)
+        block = links.block(*step_place(links, i))
         slot = lax.rem(i, 2)
 
         @pl.when(i >= 2)
         def _():
             store.wait(i - 2)
 
-        xs = xg[k, s, links.rows(b)]
+        xs = xg[block]
         gate = dot(xs, wgate[...])
         sig = jax.nn.sigmoid(gate)
         act = gate * sig
         slope = sig * (1.0 + gate * (1.0 - sig))
         up = dot(xs, wup[...])
-        hidden[slot] = (act * up).astype(LOW)
+        hidden[block] = (act * up).astype(LOW)
         second_gather.arrive(k, b, second)
-        gh = dot(yg[k, s, links.rows(b)], wdown[...], 1, 1)
+        gh = dot(yg[block], wdown[...], 1, 1)
         gpre[slot, 0] = (gh * up * slope).astype(LOW)
         gpre[slot, 1] = (gh * act).astype(LOW)
         grad = dot(gpre[slot, 0], wgate[...], 1, 1) + dot(gpre[slot, 1], wup[...], 1, 1)
-        down = dot(hidden[slot], wdown[...]).astype(LOW)
+        down = dot(hidden[block], wdown[...]).astype(LOW)
         rows = links.rows(b)
 
         @pl.when(jnp.logical_not(second))
@@ -490,19 +591,34 @@
         outs.append(pltpu.make_async_copy(keep.at[k], far_out.at[k - 1], down_sems.at[k]))
     for copy in outs:
         copy.start()
+
+    side = lax.rem(lax.axis_index("dp"), inner)
+    share = ff // inner
+
+    def down_grad(slot, cols):
+        stage[slot] = dot(hidden[...], yg[:, cols], 0, 0).astype(LOW)
+
+    def shares(slot, cols):
+        return [
+            (stage.at[slot, pl.ds(lax.rem(side + j, inner) * share, share)], grad_down[j].at[:, cols])
+            for j in range(inner)
+        ]
+
+    column_tiles(down_grad, d, stage.shape[2], stage, stage_sems, shares)
     loads[3].wait()
     loads[4].wait()
     gain_grad[...] = jnp.zeros_like(gain_grad)
-
-    def last(b, carry):
-        rows = pl.ds(pl.multiple_of(b * rb, rb), rb)
-        grad, gains = norm_backward_block(begin[rows], gain[...], back.total(b), before[rows])
-        grad_after[rows] = grad
-        low_after[rows] = grad.astype(LOW)
+    for b in range(blocks):
+        rows = slice(b * rb, (b + 1) * rb)
+        grad_out = before[rows] * valid_rows(starts, b * (rb // SEQ), rb)
+        grad, gains = norm_backward_block(begin[rows], gain[...], back.total(b), grad_out)
+        begin[rows] = grad
+        yg[rows] = grad.astype(LOW)
+        for j, (a, to) in enumerate([(begin, grad_after), (yg, low_after)]):
+            at = pl.ds(b * rb, rb)
+            outs.append(pltpu.make_async_copy(a.at[at], to.at[at], down_sems.at[chips + 2 * b + j]))
+            outs[-1].start()
         gain_grad[0:1] += gains
-        return carry
-
-    lax.fori_loop(0, blocks, last, 0)
     gather.finish()
     second_gather.finish()
     back.finish()
@@ -513,42 +629,43 @@
     store.wait(steps - 1)
 
 
-def attn_bwd_kernel(nh, chips, blocks, rb, x, start, grad_in, gain, qkv_any, wqkv_any, wout_any, starts, cp, sp, *refs):
-    gproj_out, xg_out, grad_rows, gain_grad, refs = *refs[:4], refs[4:]
-    xg, wqkv, wout, qkv, gproj, gmix, begin, before, load, store_sems, refs = *refs[:10], refs[10:]
+def attn_bwd_kernel(
+    nh, chips, blocks, rb, x, rows_any, before_any, picked, gain, qkv_any, mixed_any, normed_any, wqkv_any, wout_any,
+    selector, starts, cp, sp, *refs
+):
+    late_out, grad_rows, gain_grad, series_grad, refs = *refs[:4], refs[4:]
+    xg, wqkv, wout, qkv, mixed, normed, gproj, gmix, begin, before, stage, load, stage_sems, refs = *refs[:13], refs[13:]
     gather_refs, scatter_refs = refs[:5], refs[5:]
     links = Links(chips, blocks, rb)
     loads = loader(
-        load, [(wout_any, wout), (qkv_any, qkv), (wqkv_any, wqkv), (start, begin), (grad_in, before)]
+        load,
+        [
+            (wout_any, wout),
+            (qkv_any, qkv),
+            (wqkv_any, wqkv),
+            (rows_any, begin),
+            (before_any, before),
+            (mixed_any, mixed),
+            (normed_any, normed),
+        ],
     )
     links.greet()
     gather = Gather(links, x, xg, *gather_refs)
     scatter = Scatter(links, *scatter_refs)
-    gather.start_near()
     for b in range(blocks):
         gather.start_far(b)
+    gather.start_near()
     for copy in loads[:3]:
         copy.wait()
     width = nh * LANES
     series = rb // SEQ
-
-    def pairs(i):
-        q, second = i // 2, lax.rem(i, 2) == 1
-        k, b, s = q // blocks, lax.rem(q, blocks), lax.rem(i, 2)
-        rows = pl.ds(row_block(links, i, k, b, second), rb)
-        return [
-            (gproj.at[rows], gproj_out.at[rows]),
-            (xg.at[k, s, links.rows(b)], xg_out.at[k, s, links.rows(b)]),
-        ]
-
-    store = Store(store_sems, pairs)
+    real, d = selector.shape[0], xg.shape[1]
 
     def compute(i, k, b, second):
-        s = second.astype(jnp.int32)
-        at = row_block(links, i, k, b, second)
-        rows = pl.ds(at, rb)
+        rows = links.block(*step_place(links, i))
+        at = rows.start
         first = at // SEQ
-        gmix[...] = dot(xg[k, s, links.rows(b)], wout[...], 1, 1).astype(LOW)
+        gmix[...] = dot(xg[rows], wout[...], 1, 1).astype(LOW)
         c, sn = row_angles(cp, sp, starts, first, series)
         qc, qs = c * HS ** (-0.5), sn * HS ** (-0.5)
         kc, ks = c * LN2, sn * LN2
@@ -577,38 +694,41 @@
         value = dot(gproj[rows, :width], wqkv[0], 1, 1)
         value += dot(gproj[rows, width : 2 * width], wqkv[1], 1, 1)
         value += dot(gproj[rows, 2 * width :], wqkv[2], 1, 1)
-        store.start(i)
         return [value]
 
     run_blocks(links, lambda i, k, b, second: gather.arrive(k, b, second), compute, [scatter])
-    loads[3].wait()
-    loads[4].wait()
+    for copy in loads[3:]:
+        copy.wait()
+
+    def projections(slot, cols):
+        for c in range(4):
+            if c < 3:
+                grad = dot(gproj[:, c * width : (c + 1) * width], normed[:, cols], 0, 0)
+            else:
+                grad = dot(mixed[...], xg[:, cols], 0, 0)
+            stage[slot, c * real : (c + 1) * real] = dot(selector[...], grad.astype(LOW)).astype(LOW)
+
+    column_tiles(
+        projections, d, stage.shape[2], stage, stage_sems,
+        lambda slot, cols: [(stage.at[slot], late_out.at[:, cols])],
+    )
+    with_class_rows(begin, picked)
     gain_grad[...] = jnp.zeros_like(gain_grad)
-
-    def last(b, carry):
-        rows = pl.ds(pl.multiple_of(b * rb, rb), rb)
+    for b in range(blocks):
+        rows = slice(b * rb, (b + 1) * rb)
         grad, gains = norm_backward_block(begin[rows], gain[...], scatter.total(b), before[rows])
         grad_rows[rows] = grad
         gain_grad[0:1] += gains
-        return carry
-
-    lax.fori_loop(0, blocks, last, 0)
+        for i in range(series):
+            series_grad[b * series + i : b * series + i + 1] = jnp.sum(
+                grad[i * SEQ : (i + 1) * SEQ], 0, keepdims=True
+            )
     gather.finish()
     scatter.finish()
 
-    def stored(i, carry):
-        store.wait(i)
-        return carry
-
-    lax.fori_loop(0, 2 * chips * blocks, stored, 0)
-
 
 def resident(shape):
     return pl.BlockSpec(shape, lambda i, *_: (0,) * len(shape), pipeline_mode=pl.Buffered(1))
-
-
-def by_rows(rows, width):
-    return pl.BlockSpec((rows, width), lambda i, *_: (i, 0))
 
 
 def params(collective_id=None):
@@ -626,78 +746,99 @@
     return pltpu.SemaphoreType.DMA(shape)
 
 
-def attn_forward(chips, x, start, gain, wqkv, wout, starts, tables):
-    r, d = x.shape
+def attn_forward(chips, rows, cot, picked, gain_attn, gain_mlp, w_qkv, w_out, w_gate_up, w_down, selector, starts, tables):
+    r, d = rows.shape
     m = 2 * chips * r
-    width = wout.shape[0]
+    real, width = selector.shape
+    ff = w_down.shape[0]
     nh = width // LANES
     rb = min(BLOCK, r)
     blocks = r // rb
     steps = 2 * chips * blocks
+    tile = 128
     return pl.pallas_call(
         functools.partial(attn_fwd_kernel, nh, chips, blocks, rb),
         out_shape=[
             jax.ShapeDtypeStruct((m, 3 * width), LOW),
             jax.ShapeDtypeStruct((m, width), LOW),
-            jax.ShapeDtypeStruct((chips, 2, r, d), LOW),
+            jax.ShapeDtypeStruct((m, d), LOW),
+            jax.ShapeDtypeStruct((3, d, width), LOW),
+            jax.ShapeDtypeStruct((width, d), LOW),
+            jax.ShapeDtypeStruct((2 * d, ff), LOW),
+            jax.ShapeDtypeStruct((ff, d), LOW),
             jax.ShapeDtypeStruct((r, d), F32),
             jax.ShapeDtypeStruct((r, d), LOW),
+            jax.ShapeDtypeStruct((r, d), LOW),
         ],
-        in_specs=[ANY, ANY, WHOLE, ANY, ANY, SCALARS, WHOLE, WHOLE],
-        out_specs=[ANY, ANY, ANY, WHOLE, WHOLE],
+        in_specs=[ANY, ANY, WHOLE, WHOLE, WHOLE, ANY, ANY, ANY, ANY, WHOLE, SCALARS, WHOLE, WHOLE],
+        out_specs=[ANY] * 7 + [WHOLE] * 3,
         scratch_shapes=[
-            pltpu.VMEM((chips, 2, r, d), LOW),
+            pltpu.VMEM((r, d), LOW),
+            pltpu.VMEM((m, d), LOW),
             pltpu.VMEM((3, d, width), LOW),
             pltpu.VMEM((width, d), LOW),
+            pltpu.VMEM((3, d, real), F32),
+            pltpu.VMEM((real, d), F32),
             pltpu.VMEM((m, 3 * width), LOW),
             pltpu.VMEM((m, width), LOW),
             pltpu.VMEM((r, d), F32),
-            sems(3),
+            pltpu.VMEM((r, d), F32),
+            sems(4),
             sems(steps, 3),
+            pltpu.VMEM((2, tile, ff), F32),
+            pltpu.VMEM((2, tile, ff), LOW),
+            pltpu.VMEM((2, tile, d), F32),
+            pltpu.VMEM((2, tile, d), LOW),
+            sems(4, 2),
+            sems(2),
             *Gather.scratch(chips, blocks),
             *Scatter.scratch(chips, blocks, r, d),
         ],
         compiler_params=params(1),
         name="attn_fwd",
-    )(x, start, gain, wqkv, wout, starts, *tables)
-
-
-def mlp_both(chips, x, gy, after, grad_in, gain, wgate, wup, wdown):
+    )(
+        rows, cot, picked, gain_attn, gain_mlp, w_qkv, w_out, w_gate_up.reshape(2 * d, ff), w_down, selector,
+        starts, *tables,
+    )
+
+
+def mlp_both(chips, inner, x, gy, after, cot, gain, gate_low, down_low, starts):
     r, d = x.shape
     m = 2 * chips * r
-    ff = wgate.shape[1]
+    ff = down_low.shape[0]
     rb = min(BLOCK, r)
     blocks = r // rb
     steps = 2 * chips * blocks
-    group = jax.ShapeDtypeStruct((chips, 2, r, d), LOW)
+    tile = 256
     return pl.pallas_call(
-        functools.partial(mlp_kernel, chips, blocks, rb),
+        functools.partial(mlp_kernel, chips, inner, blocks, rb),
         out_shape=[
-            jax.ShapeDtypeStruct((m, ff), LOW),
             jax.ShapeDtypeStruct((2, m, ff), LOW),
-            group,
-            group,
+            jax.ShapeDtypeStruct((m, d), LOW),
             jax.ShapeDtypeStruct((r, d), LOW),
             jax.ShapeDtypeStruct((chips - 1, r, d), LOW),
+            *[jax.ShapeDtypeStruct((ff // inner, d), LOW)] * inner,
             jax.ShapeDtypeStruct((r, d), F32),
             jax.ShapeDtypeStruct((r, d), LOW),
             jax.ShapeDtypeStruct((8, d), F32),
         ],
-        in_specs=[ANY, ANY, ANY, ANY, WHOLE, ANY, ANY, ANY],
-        out_specs=[ANY] * 6 + [WHOLE] * 3,
+        in_specs=[ANY, ANY, ANY, ANY, WHOLE, ANY, ANY, SCALARS],
+        out_specs=[ANY] * (6 + inner) + [WHOLE],
         scratch_shapes=[
-            pltpu.VMEM((chips, 2, r, d), LOW),
-            pltpu.VMEM((chips, 2, r, d), LOW),
+            pltpu.VMEM((m, d), LOW),
+            pltpu.VMEM((m, d), LOW),
             pltpu.VMEM((d, ff), LOW),
             pltpu.VMEM((d, ff), LOW),
             pltpu.VMEM((ff, d), LOW),
-            pltpu.VMEM((2, rb, ff), LOW),
+            pltpu.VMEM((m, ff), LOW),
             pltpu.VMEM((2, 2, rb, ff), LOW),
             pltpu.VMEM((r, d), F32),
             pltpu.VMEM((r, d), F32),
+            pltpu.VMEM((2, ff, tile), LOW),
             sems(5),
-            sems(steps, 5),
-            sems(chips),
+            sems(steps, 3),
+            sems(chips + 2 * blocks),
+            sems(2, inner),
             *Gather.scratch(chips, blocks),
             *Gather.scratch(chips, blocks),
             *Scatter.scratch(chips, blocks, r, d),
@@ -707,119 +848,78 @@
         ],
         compiler_params=params(2),
         name="mlp_both",
-    )(x, gy, after, grad_in, gain, wgate, wup, wdown)
-
-
-def attn_backward(chips, x, start, grad_in, gain, qkv, wqkv, wout, starts, tables):
+    )(x, gy, after, cot, gain, gate_low, down_low, starts)
+
+
+def attn_backward(
+    chips, x, rows, before, picked, gain, qkv, mixed, normed, wqkv, wout, selector, starts, tables
+):
     r, d = x.shape
     m = 2 * chips * r
-    width = wout.shape[0]
+    real, width = selector.shape
     nh = width // LANES
     rb = min(BLOCK, r)
     blocks = r // rb
-    steps = 2 * chips * blocks
+    tile = 256
     return pl.pallas_call(
         functools.partial(attn_bwd_kernel, nh, chips, blocks, rb),
         out_shape=[
-            jax.ShapeDtypeStruct((m, 3 * width), LOW),
-            jax.ShapeDtypeStruct((chips, 2, r, d), LOW),
+            jax.ShapeDtypeStruct((4 * real, d), LOW),
             jax.ShapeDtypeStruct((r, d), F32),
             jax.ShapeDtypeStruct((8, d), F32),
+            jax.ShapeDtypeStruct((r // SEQ, d), F32),
         ],
-        in_specs=[ANY, ANY, ANY, WHOLE, ANY, ANY, ANY, SCALARS, WHOLE, WHOLE],
-        out_specs=[ANY, ANY, WHOLE, WHOLE],
+        in_specs=[ANY, ANY, ANY, WHOLE, WHOLE, ANY, ANY, ANY, ANY, ANY, WHOLE, SCALARS, WHOLE, WHOLE],
+        out_specs=[ANY, WHOLE, WHOLE, WHOLE],
         scratch_shapes=[
-            pltpu.VMEM((chips, 2, r, d), LOW),
+            pltpu.VMEM((m, d), LOW),
             pltpu.VMEM((3, d, width), LOW),
             pltpu.VMEM((width, d), LOW),
             pltpu.VMEM((m, 3 * width), LOW),
+            pltpu.VMEM((m, width), LOW),
+            pltpu.VMEM((m, d), LOW),
             pltpu.VMEM((m, 3 * width), LOW),
             pltpu.VMEM((rb, width), LOW),
             pltpu.VMEM((r, d), F32),
             pltpu.VMEM((r, d), F32),
-            sems(5),
-            sems(steps, 2),
+            pltpu.VMEM((2, 4 * real, tile), LOW),
+            sems(7),
+            sems(2, 1),
             *Gather.scratch(chips, blocks),
             *Scatter.scratch(chips, blocks, r, d),
         ],
         compiler_params=params(3),
         name="attn_bwd",
-    )(x, start, grad_in, gain, qkv, wqkv, wout, starts, *tables)
-
-
-def weight_grad(a, b, plane=None):
-    ra, wide = a[0].shape
-    rb, n = b[0].shape[-2:]
-    r = min(ra, rb)
+    )(x, rows, before, picked, gain, qkv, mixed, normed, wqkv, wout, selector, starts, *tables)
+
+
+def weight_grad(a, b, plane, inner):
+    m, wide = a.shape
+    n = b.shape[-1]
     nb = 256 if n % 256 == 0 else 128
-    if plane is None:
-        b_spec = pl.BlockSpec((rb, nb), lambda i: (0, i))
-    else:
-        b_spec = pl.BlockSpec((None, rb, nb), lambda i: (plane, 0, i))
-
-    def kernel(*refs):
-        xs, ys, out = refs[: len(a)], refs[len(a) : -1], refs[-1]
-        total = None
-        for at in range(0, len(a) * ra, r):
-            x = xs[at // ra][at % ra : at % ra + r]
-            y = ys[at // rb][at % rb : at % rb + r]
-            part = dot(x, y, 0, 0)
-            total = part if total is None else total + part
-        out[...] = total.astype(LOW)
+    share = wide // inner
+
+    def kernel(x, y, *refs):
+        outs, total = refs[:-1], refs[-1]
+        side = lax.rem(lax.axis_index("dp"), inner)
+        total[...] = dot(x[...], y[...], 0, 0).astype(LOW)
+        for j, out in enumerate(outs):
+            at = pl.multiple_of(lax.rem(side + j, inner) * share, share)
+            out[...] = total[pl.ds(at, share)]
 
     return pl.pallas_call(
         kernel,
         grid=(n // nb,),
-        out_shape=jax.ShapeDtypeStruct((wide, n), LOW),
-        in_specs=[resident((ra, wide))] * len(a) + [b_spec] * len(b),
-        out_specs=pl.BlockSpec((wide, nb), lambda i: (0, i)),
+        out_shape=[jax.ShapeDtypeStruct((share, n), LOW)] * inner,
+        in_specs=[resident((m, wide)), pl.BlockSpec((None, m, nb), lambda i: (plane, 0, i))],
+        out_specs=[pl.BlockSpec((share, nb), lambda i: (0, i))] * inner,
+        scratch_shapes=[pltpu.VMEM((wide, nb), LOW)],
         compiler_params=params(),
         cost_estimate=pl.CostEstimate(
-            flops=2 * len(a) * ra * wide * n,
-            bytes_accessed=2 * (len(a) * ra * (wide + n) + wide * n),
-            transcendentals=0,
+            flops=2 * m * wide * n, bytes_accessed=2 * (m * (wide + n) + wide * n), transcendentals=0
         ),
         name="weight_grad",
-    )(*a, *b)
-
-
-def attn_weight_grad(gproj, mixed, normed, ga, selector):
-    m, wide = gproj[0].shape
-    width = wide // 3
-    r, d = normed[0].shape
-    real = selector.shape[0]
-    chunks = len(normed)
-    kb = 256 if d % 256 == 0 else d
-
-    def kernel(*refs):
-        gp, mx = refs[: len(gproj)], refs[len(gproj) : 2 * len(gproj)]
-        nm, g, sel, out = refs[2 * len(gproj) : -2 - chunks], refs[-2 - chunks : -2], refs[-2], refs[-1]
-        for c in range(4):
-            total = None
-            for i in range(chunks):
-                k, at = i * r // m, i * r % m
-                x = mx[k][at : at + r] if c == 3 else gp[k][at : at + r, c * width : (c + 1) * width]
-                part = dot(x, (g if c == 3 else nm)[i][...], 0, 0)
-                total = part if total is None else total + part
-            out[c * real : (c + 1) * real] = dot(sel[...], total.astype(LOW)).astype(LOW)
-
-    return pl.pallas_call(
-        kernel,
-        grid=(d // kb,),
-        out_shape=jax.ShapeDtypeStruct((4 * real, d), LOW),
-        in_specs=[resident((m, wide))] * len(gproj)
-        + [resident((m, width))] * len(mixed)
-        + [pl.BlockSpec((r, kb), lambda i: (0, i))] * (2 * chunks)
-        + [resident((real, width))],
-        out_specs=pl.BlockSpec((4 * real, kb), lambda i: (0, i)),
-        compiler_params=params(),
-        cost_estimate=pl.CostEstimate(
-            flops=2 * chunks * r * d * 4 * width,
-            bytes_accessed=2 * chunks * r * (4 * width + 2 * d),
-            transcendentals=0,
-        ),
-        name="attn_weight_grad",
-    )(*gproj, *mixed, *normed, *ga, selector)
+    )(a, b)
 
 
 OUTER = 4
@@ -911,7 +1011,8 @@
 
     loads = []
     for p in range(count):
-        one = [(full[p].at[pl.ds(side * halves[p], halves[p])], loc.at[pl.ds(offsets[p], halves[p])])]
+        own = full[p] if p < early else full[p].at[pl.ds(side * halves[p], halves[p])]
+        one = [(own, loc.at[pl.ds(offsets[p], halves[p])])]
         if p < early:
             for j in range(inner - 1):
                 one.append((got[p].at[j], rc.at[j, pl.ds(offsets[p], halves[p])]))
@@ -1042,23 +1143,21 @@
         self.inner = mesh.shape["dp"] // OUTER
         self.group = mesh.shape["mp"]
 
-    def exchange(self, x):
-        side = lax.rem(lax.axis_index("dp"), self.inner)
-        rows = x.shape[0] // self.inner
+    def exchange(self, shares):
         got = []
         for j in range(1, self.inner):
             pairs = []
             for o in range(OUTER):
                 for i in range(self.inner):
                     pairs.append((o * self.inner + i, o * self.inner + (i + j) % self.inner))
-            share = lax.dynamic_slice_in_dim(x, lax.rem(side + j, self.inner) * rows, rows)
-            got.append(lax.ppermute(share, "dp", pairs))
-        return jnp.stack(got)
-
-    def reduce(self, pieces, got, small):
+            got.append(lax.ppermute(shares[j], "dp", pairs)[None])
+        return got[0] if len(got) == 1 else jnp.concatenate(got, 0)
+
+    def reduce(self, own, got, last, small):
         inner = self.inner
-        width = pieces[0].shape[1]
-        halves = tuple(p.shape[0] // inner for p in pieces)
+        width = last.shape[1]
+        pieces = [*own, last]
+        halves = tuple(p.shape[0] for p in own) + (last.shape[0] // inner,)
         share = sum(halves)
         chunks = share // CHUNK
         any_spec = pl.BlockSpec(memory_space=pl.ANY)
@@ -1131,58 +1230,47 @@
     mine_valid = (slots[None, :] >= starts[0][:, None]).astype(F32)
     starts = starts.reshape(-1)
 
-    by_series = lambda v: v.reshape(own_series, SEQ, d)
+    by_class = [(freq_class == f)[:, None] for f in range(NFREQ)]
     picked = freq_table[NFREQ - 1][None]
     for f in range(NFREQ - 1):
-        picked = jnp.where((freq_class == f)[:, None], freq_table[f][None], picked)
-    start_rows = (by_series(rows) + picked[:, None]).reshape(local_rows, d)
-    inverse = lax.rsqrt(jnp.mean(start_rows * start_rows, -1, keepdims=True) + EPSILON)
-    normed_mine = (start_rows * inverse * gain_attn).astype(LOW)
-    grad_output = (by_series(cotangent) * mine_valid[:, :, None]).reshape(local_rows, d)
-
+        picked = jnp.where(by_class[f], freq_table[f][None], picked)
     selector = head_selector(head_count)
-    qkv_low = jnp.einsum("cdf,fg->cdg", w_qkv.astype(LOW), selector, preferred_element_type=F32).astype(LOW)
-    out_low = dot(selector, w_out.astype(LOW), 0, 0).astype(LOW)
-    gate_low = w_gate_up[0].astype(LOW)
-    up_low = w_gate_up[1].astype(LOW)
-    down_low = w_down.astype(LOW)
-
-    qkv, mixed, normed, after_attn, normed_mlp_mine = attn_forward(
-        chips, normed_mine, start_rows, gain_mlp[None], qkv_low, out_low, starts, tables
-    )
-    hidden, grad_pre, normed_mlp, grad_down_in, down_own, down_far, grad_after, grad_after_low, gains_mlp = mlp_both(
-        chips, normed_mlp_mine, grad_output.astype(LOW), after_attn, grad_output, gain_mlp[None],
-        gate_low, up_low, down_low,
-    )
-    flat = lambda v: v.reshape(-1, d)
-    grad_down = weight_grad([hidden], [flat(grad_down_in)])
-    ups = [weight_grad([flat(normed_mlp)], [grad_pre], c) for c in range(2)]
-    pieces = [grad_down] + (ups if ff >= d else [jnp.concatenate(ups, 1)])
-    got = [reducer.exchange(p) for p in pieces]
+
+    qkv, mixed, normed, qkv_low, out_low, gate_low, down_low, after_attn, normed_mlp, grad_low = attn_forward(
+        chips, rows, cotangent, picked, gain_attn[None], gain_mlp[None], w_qkv, w_out, w_gate_up, w_down, selector,
+        starts, tables,
+    )
+    grad_pre, normed_mlp, down_own, down_far, *rest = mlp_both(
+        chips, reducer.inner, normed_mlp, grad_low, after_attn, cotangent, gain_mlp[None], gate_low, down_low, starts
+    )
+    shares, (grad_after, grad_after_low, gains_mlp) = [rest[: reducer.inner]], rest[reducer.inner :]
+    ups = [weight_grad(normed_mlp, grad_pre, c, reducer.inner) for c in range(2)]
+    if ff >= d:
+        shares += ups
+    else:
+        shares.append([jnp.concatenate(both, 1) for both in zip(*ups)])
+    got = [reducer.exchange(v) for v in shares]
     output = after_attn + down_own.astype(F32)
     for k in range(1, chips):
         far = lax.ppermute(down_far[k - 1], "mp", [(i, (i + 2 * k) % group_size) for i in range(group_size)])
         output += far.astype(F32)
 
-    grad_proj, grad_attn_in, grad_rows, gains_attn = attn_backward(
-        chips, grad_after_low, start_rows, grad_after, gain_attn[None], qkv, qkv_low, out_low, starts, tables
-    )
-    pieces.append(
-        attn_weight_grad([grad_proj], [mixed], [flat(normed)], [flat(grad_attn_in)], selector)
-    )
-    series_sums = jnp.sum(by_series(grad_rows), 1)
-    grad_table = [jnp.sum(jnp.where((freq_class == f)[:, None], series_sums, 0.0), 0) for f in range(NFREQ)]
+    last, grad_rows, gains_attn, series_sums = attn_backward(
+        chips, grad_after_low, rows, grad_after, picked, gain_attn[None], qkv, mixed, normed, qkv_low, out_low,
+        selector, starts, tables,
+    )
+    grad_table = [jnp.sum(jnp.where(by_class[f], series_sums, 0.0), 0) for f in range(NFREQ)]
 
     tokens = jnp.full((d,), jnp.sum(mine_valid))
     zero = jnp.zeros((d,), F32)
     small = jnp.stack([gains_attn[0], gains_mlp[0], *grad_table, tokens, zero, zero])
-    sums, small = reducer.reduce(pieces, got, small)
+    own = [v[0] for v in shares]
+    sums, small = reducer.reduce(own, got, last, small)
     root_scale = lax.rsqrt(small[2 + NFREQ, 0])
     small = small * root_scale
     finals, offset = [], 0
-    for piece in pieces:
-        share = piece.shape[0] // reducer.inner
-        finals.append(sums[:, offset : offset + share].reshape(piece.shape))
+    for share in [v.shape[0] for v in own] + [last.shape[0] // reducer.inner]:
+        finals.append(sums[:, offset : offset + share].reshape(-1, d))
         offset += share
     down_out = finals[0].astype(F32) * root_scale
     if len(finals) == 3:

time: 601 us -> 535 us (0.89); the launches traced: 600 us -> 527 us
  Pallas kernels: 515 us -> 471 us
  other arithmetic: 39.2 us -> 23.4 us
  matrix products: 10.5 us -> 1.9 us
    pallas_call x5 -> x3, Pallas kernels: 164 us -> 122 us  [the longest x1 97.1 us: mlp_both(): pl.pallas_call(functools.partial(mlp_kernel, chips, inner, blocks, rb), o...]
    pallas_call x1, Pallas kernels: 89 us -> 80.7 us  [attn_backward(): pl.pallas_call(functools.partial(attn_bwd_kernel, nh, chips, blocks, rb),...]
    another operation x1 -> x0, other arithmetic: 8.19 us -> none
    dynamic_slice x3 -> x0, local copies, waits for them, and re-layouts: 8.13 us -> none  [exchange(): lax.dynamic_slice_in_dim(x, lax.rem(side + j, self.inner) * rows, rows)]
    unnamed x23 -> x6, local copies, waits for them, and re-layouts: 1.84 us -> 9.04 us
    dot_general x1 -> x0, matrix products: 6.7 us -> none  [body(): jnp.einsum('cdf,fg->cdg', w_qkv.astype(LOW), selector, preferred_element_...]
    convert_element_type x2 -> x0, local copies, waits for them, and re-layouts: 6.3 us -> none  [the longest x1 6.22 us: body(): up_low = w_gate_up[1].astype(LOW)]
  transfers between devices with their start and end apart: 4 -> 4, of which waited for: 0 -> 1; matrix products, arithmetic and copies ran while one was open for 2% -> 2% of each run, Pallas kernels for 24% -> 18%
where the time goes in v3:
time: 535 us; the launch traced here: 527 us
  Pallas kernels  471 us (88%)
  other arithmetic  23.4 us (4%)
  local copies, waits for them, and re-layouts  23.3 us (4%)
    pallas_call x1, Pallas kernels, reduce(): pl.pallas_call(functools.partial(sum_kernel, inner, self.group, len(got),...  196 us
    pallas_call x1, Pallas kernels, mlp_both(): pl.pallas_call(functools.partial(mlp_kernel, chips, inner, blocks, rb), o...  97.1 us
    pallas_call x1, Pallas kernels, attn_backward(): pl.pallas_call(functools.partial(attn_bwd_kernel, nh, chips, blocks, rb),...  80.7 us
    pallas_call x1, Pallas kernels, attn_forward(): pl.pallas_call(functools.partial(attn_fwd_kernel, nh, chips, blocks, rb),...  72.1 us
    pallas_call x2, Pallas kernels, weight_grad(): pl.pallas_call(kernel, grid=(n // nb,), out_shape=[jax.ShapeDtypeStruct((...  25 us
  transfers between devices with their start and end apart: 4, of which 1 were waited for; matrix products, arithmetic and copies ran while one was open for 2% of the time, Pallas kernels for 18%

profile of v3, /device:TPU:0, one launch (start us, length us, event | category | flops | bytes accessed | tf_op | source)
XLA Modules:
  0.0 527.3 jit_solution(2187495626915504313)
XLA Ops:
  0.7 0.7 broadcast_subtract_fusion
  2.6 0.7 broadcast_compare_fusion
  3.3 0.9 slice_reduce_fusion.4
  4.1 1.3 broadcast_in_dim.96.gain_attn.gain
  5.4 1.3 broadcast_in_dim.97.gain_mlp.gain
  6.7 7.2 %copy.24.wqkv_any = f32[3,1280,320]{2,1,0:T(8,128)} copy(f32[3,1280,320]{1,2,0:T(8,128)} %param.20) | data formatting | bytes 9830400 | tf_op args[6]
  14.0 0.7 select_select_fusion.picked
  14.7 72.1 %attn_fwd.1 = (bf16[2048,1536]{1,0:T(8,128)(2,1)}, bf16[2048,512]{1,0:T(8,128)(2,1)}, bf16[2048,1280]{1,0:T(8,128)(2,1)}, bf16[3,1280,512]{2,1,0:T(8,128)(2,1)},...) custom-call(f32[512,1280]{1,0:T(8,128)} %rows_any.3, ...), custom_call_target="tpu_custom_call" | custom-call | tf_op jit(solution)/shard_map/attn_fwd/pallas_call | solution.py:759
  86.8 97.1 %mlp_both.1 = (bf16[2,2048,1280]{2,1,0:T(8,128)(2,1)}, bf16[2048,1280]{1,0:T(8,128)(2,1)}, bf16[512,1280]{1,0:T(8,128)(2,1)}, bf16[1,512,1280]{2,1,0:T(8,128)(2,...) custom-call(bf16[512,1280]{1,0:T(8,128)(2,1)} %get-tuple-element.39., ...), custom_call_target="tpu_custom_call" | custom-call | tf_op jit(solution)/shard_map/mlp_both/pallas_call | solution.py:813
  183.9 12.4 %weight_grad.3 = (bf16[640,1280]{1,0:T(8,128)(2,1)}, bf16[640,1280]{1,0:T(8,128)(2,1)}) custom-call(bf16[2048,1280]{1,0:T(8,128)(2,1)} %get-tuple-element.54.x, bf16[2,2048,1280]{2,1,0:T(8,128)(2,1)} %get-tuple-element.55.y), custom_call_target="tpu_custom_call" | custom-call | flops 6710886400 | bytes 13762560 | tf_op jit(solution)/shard_map/weight_grad/pallas_call | solution.py:910
  196.3 1.4 collective-permute-start.3
  197.6 1.5 collective-permute-start
  199.1 12.6 %weight_grad.2 = (bf16[640,1280]{1,0:T(8,128)(2,1)}, bf16[640,1280]{1,0:T(8,128)(2,1)}) custom-call(bf16[2048,1280]{1,0:T(8,128)(2,1)} %get-tuple-element.54.x, bf16[2,2048,1280]{2,1,0:T(8,128)(2,1)} %get-tuple-element.55.y), custom_call_target="tpu_custom_call" | custom-call | flops 6710886400 | bytes 13762560 | tf_op jit(solution)/shard_map/weight_grad/pallas_call | solution.py:910
  212.3 1.5 collective-permute-start.1
  213.7 80.7 %attn_bwd.1 = (bf16[1280,1280]{1,0:T(8,128)(2,1)}, f32[512,1280]{1,0:T(8,128)}, f32[8,1280]{1,0:T(8,128)}, f32[8,1280]{1,0:T(8,128)}) custom-call(bf16[512,1280]{1,0:T(8,128)(2,1)} %get-tuple-element.45.x, f32[512,1280]{1,0:T(8,128)} %rows_any.3, f32[512,1280]{1,0:T(8,128)} %get-tuple-element.46.before_any, f32[8,1280]{1,0:T(8,128)} %select_select_fusion.picked, ...), custom_call_target="tpu_custom_call" | custom-call | tf_op jit(solution)/shard_map/attn_bwd/pallas_call | solution.py:864
  294.5 0.9 select_reduce_fusion
  295.4 0.8 slice.57
  296.2 0.8 slice.58
  297.0 0.7 convert_reduce_fusion
  297.6 0.6 stack_broadcast_in_dim.3
  298.3 0.7 stack.34.refs_7_
  299.0 4.0 convert_add_fusion
  303.5 196.5 %sum_over_dp.1 = (bf16[2,2560,1280]{2,1,0:T(8,128)(2,1)}, f32[8,1280]{1,0:T(8,128)}) custom-call(bf16[640,1280]{1,0:T(8,128)(2,1)} %get-tuple-element.53.refs_0_, bf16[640,1280]{1,0:T(8,128)(2,1)} %get-tuple-element.56.refs_1_, bf16[640,1280]{1,0:T(8,128)(2,1)} %get-tuple-element.57.refs_2_, bf16[1280,1280]{1,0:T(8,128)(2,1)} %get-tuple-element.58.refs_3_, ...), custom_call_target="tpu_custom_call" | custom-call | bytes 600000000 | tf_op jit(solution)/shard_map/sum_over_dp/pallas_call | solution.py:1166
  500.0 1.2 slice.62
  501.9 0.8 broadcast_multiply_fusion
  503.9 5.2 convert_multiply_fusion.1
  509.1 4.2 fusion.12
  513.3 1.3 convert_multiply_fusion.2
  515.3 0.6 fusion.1
  516.5 6.0 %convert_multiply_fusion = f32[2,1280,1280]{2,1,0:T(8,128)} fusion(bf16[1,1280,1280]{2,1,0:T(8,128)(2,1)S(1)} %bitcast.22, bf16[1,1280,1280]{2,1,0:T(8,128)(2,1)S(1)} %bitcast.21, f32[]{:T(128)} %bitcast.8), kind=kLoop, calls=%fused_computation.1 | loop fusion | flops 9830400 | bytes 19660804 | tf_op jit(solution)/shard_map/mul | solution.py:1279
  522.5 2.6 pad_maximum_fusion
  525.4 1.5 copy.26
  (23 shorter events, 5.2 us)
Async XLA Ops:
  196.3 106.7 %collective-permute-start.3 = (bf16[640,1280]{1,0:T(8,128)(2,1)}, bf16[640,1280]{1,0:T(8,128)(2,1)}, u32[]{:S(2)}, u32[]{:S(2)}) collective-permute-start(bf16[640,1280]{1,0:T(8,128)(2,1)} %get-tuple-element.61), channel_id=1, source_target_pairs={{0,4},{4,0},{8,12},{12,8},{16,20},{20,16},{24,28},{28,24},{1,5},{5... | collective-permute-start | bytes 4915208 | tf_op jit(solution)/shard_map/ppermute | solution.py:1153
  197.6 101.3 %collective-permute-start = (bf16[512,1280]{1,0:T(8,128)(2,1)}, bf16[512,1280]{1,0:T(8,128)(2,1)}, u32[]{:S(2)}, u32[]{:S(2)}) collective-permute-start(bf16[512,1280]{1,0:T(8,128)(2,1)} %bitcast.2), channel_id=1, source_target_pairs={{0,2},{1,3},{2,0},{3,1},{4,6},{5,7},{6,4},{7,5},{8,10},{9,11},{10,... | collective-permute-start | bytes 3932168 | tf_op jit(solution)/shard_map/ppermute | solution.py:1255
  211.7 91.2 %collective-permute-start.2 = (bf16[640,1280]{1,0:T(8,128)(2,1)}, bf16[640,1280]{1,0:T(8,128)(2,1)}, u32[]{:S(2)}, u32[]{:S(2)}) collective-permute-start(bf16[640,1280]{1,0:T(8,128)(2,1)} %get-tuple-element.60), channel_id=1, source_target_pairs={{0,4},{4,0},{8,12},{12,8},{16,20},{20,16},{24,28},{28,24},{1,5},{5... | collective-permute-start | bytes 4915208 | tf_op jit(solution)/shard_map/ppermute | solution.py:1153
  212.3 91.3 %collective-permute-start.1 = (bf16[640,1280]{1,0:T(8,128)(2,1)}, bf16[640,1280]{1,0:T(8,128)(2,1)}, u32[]{:S(2)}, u32[]{:S(2)}) collective-permute-start(bf16[640,1280]{1,0:T(8,128)(2,1)} %get-tuple-element.59), channel_id=1, source_target_pairs={{0,4},{4,0},{8,12},{12,8},{16,20},{20,16},{24,28},{28,24},{1,5},{5... | collective-permute-start | bytes 4915208 | tf_op jit(solution)/shard_map/ppermute | solution.py:1153
  213.7 85.2 %copy-start.1 = (bf16[512,1280]{1,0:T(8,128)(2,1)S(1)}, bf16[512,1280]{1,0:T(8,128)(2,1)}, u32[]{:S(2)}) copy-start(bf16[512,1280]{1,0:T(8,128)(2,1)} %get-tuple-element.43) | copy-start | bytes 3932164
  522.5 2.9 copy-start
